TPU v7x, 256 devices: a whole 4x4x8 slice. The times are simulated.
256 devices in a mesh: ctx: 32 (over z, x_hi, core), head: 8 (over y, x_lo).
Axes of the slice: x: 4 (x_hi: 2, x_lo: 2; x = x_hi * 2 + x_lo), y: 4, z: 8, core: 2. Of those that a mesh axis runs over, the one named last changes fastest.
Arguments:
- query_rows: bfloat16 [6144, 8192], P('ctx', 'head'), may hold values from -6 to 6
- key_rows: bfloat16 [6144, 1024], P('ctx', 'head'), may hold values from -6 to 6
- value_rows: bfloat16 [6144, 1024], P('ctx', 'head'), may hold values from -6 to 6
- attn_output: bfloat16 [6144, 8192], P('ctx', 'head'), may hold values from -6 to 6
- log_norms: float32 [64, 6144], P('head', 'ctx'), may hold values from 3 to 5
- grad_output: bfloat16 [6144, 8192], P(('ctx', 'head')), may hold values from -2.390625 to 2.390625
- span_order: int32 [64], replicated, may hold values from 0 to 63, each once
Outputs:
- grad_query: bfloat16 [6144, 8192], P(('ctx', 'head'))
- grad_key: bfloat16 [6144, 1024], P('ctx', 'head')
- grad_value: bfloat16 [6144, 1024], P('ctx', 'head')
Inputs may be any that keep to these rules, and one draw needn't show every extreme that they name: span_order is a permutation: each of the 64 spans of 96 positions is held by exactly one slot.
All inputs are finite; a program needn't handle non-finite values.
Results may differ from a plain program's by a relative error of at most 0.0051.
Values may be sent and summed in bfloat16 or wider, within the bound.
No kernel may reach another device: no remote copies, remote signals or barrier semaphores. Data moves between devices by JAX's collectives and lax.ppermute only.
A program may use at most 192 MiB of HBM per device.

v0:
```python
import jax
import jax.numpy as jnp
from jax import lax
from jax.sharding import PartitionSpec as P

QH = 64
KVH = 8
HD = 128


def passed_along(block, axis, distance):
    devices = range(lax.axis_size(axis))
    route = [((i - distance) % len(devices), i) for i in devices]
    return lax.ppermute(block, axis, route)


def table_positions(span_order, first_row, row_count, half_span):
    row_ids = first_row + jnp.arange(row_count, dtype=jnp.int32)
    slot_ids = row_ids // half_span
    slot_match = slot_ids[:, None] == jnp.arange(span_order.shape[0], dtype=jnp.int32)[None, :]
    span_ids = jnp.sum(jnp.where(slot_match, span_order[None, :], 0), axis=1)
    return span_ids * half_span + row_ids % half_span


def attend_block(
    query_heads, grad_heads, lse_rows, row_delta, query_pos, key_block, value_block, key_pos
):
    inv_root = query_heads.shape[-1] ** (-0.5)
    scores = (
        jnp.einsum("tngd,snd->tngs", query_heads, key_block, preferred_element_type=jnp.float32)
        * inv_root
    )
    causal = query_pos[:, None, None, None] >= key_pos[None, None, None, :]
    prob_full = jnp.where(causal, jnp.exp(scores - lse_rows[..., None]), 0.0)
    prob_low = prob_full.astype(jnp.bfloat16)
    dprobs = jnp.einsum(
        "tngd,snd->tngs", grad_heads, value_block, preferred_element_type=jnp.float32
    )
    dscores = (prob_full * (dprobs - row_delta[..., None])).astype(jnp.bfloat16)
    grad_q = (
        jnp.einsum("tngs,snd->tngd", dscores, key_block, preferred_element_type=jnp.float32)
        * inv_root
    )
    grad_k = (
        jnp.einsum("tngs,tngd->snd", dscores, query_heads, preferred_element_type=jnp.float32)
        * inv_root
    )
    grad_v = jnp.einsum("tngs,tngd->snd", prob_low, grad_heads, preferred_element_type=jnp.float32)
    return (grad_q, grad_k, grad_v)


def per_device(query_rows, key_rows, value_rows, attn_output, log_norms, grad_output, span_order):
    grad_rows = lax.all_to_all(grad_output, "head", split_axis=1, concat_axis=0, tiled=True)
    row_count = query_rows.shape[0]
    half_span = row_count // 2
    head_dim = HD
    kv_heads = key_rows.shape[1] // head_dim
    groups = QH // KVH
    query_heads = query_rows.reshape(row_count, kv_heads, groups, head_dim)
    grad_heads = grad_rows.reshape(row_count, kv_heads, groups, head_dim)
    out_heads = attn_output.reshape(row_count, kv_heads, groups, head_dim)
    row_delta = jnp.sum(grad_heads.astype(jnp.float32) * out_heads.astype(jnp.float32), axis=-1)
    lse_rows = log_norms.reshape(kv_heads, groups, row_count).transpose(2, 0, 1)
    cycle_size = lax.axis_size("ctx")
    device = lax.axis_index("ctx")
    query_pos = table_positions(span_order, device * row_count, row_count, half_span)

    def attend(key_block, value_block, key_pos):
        return attend_block(
            query_heads, grad_heads, lse_rows, row_delta, query_pos, key_block, value_block, key_pos
        )

    def block_terms(key_block, value_block, key_pos):
        return attend(key_block, value_block, key_pos)

    key_heads = key_rows.reshape(row_count, kv_heads, head_dim)
    value_heads = value_rows.reshape(row_count, kv_heads, head_dim)
    dq_init = jnp.zeros((row_count, kv_heads, groups, head_dim), jnp.float32)
    acc_init = jnp.zeros((row_count, kv_heads, head_dim), jnp.float32)

    def cycle_turn(turn_index, carry_state):
        key_block, value_block, dk_acc, dv_acc, dq_acc = carry_state
        source = (device - turn_index) % cycle_size
        key_pos = table_positions(span_order, source * row_count, row_count, half_span)
        grad_q, grad_k, grad_v = block_terms(key_block, value_block, key_pos)
        key_block, value_block = passed_along((key_block, value_block), "ctx", 1)
        dk_acc, dv_acc = passed_along((dk_acc + grad_k, dv_acc + grad_v), "ctx", 1)
        return (key_block, value_block, dk_acc, dv_acc, dq_acc + grad_q)

    key_block, value_block, dk_acc, dv_acc, dq_acc = lax.fori_loop(
        0, cycle_size - 1, cycle_turn, (key_heads, value_heads, acc_init, acc_init, dq_init)
    )
    source = (device + 1) % cycle_size
    key_pos = table_positions(span_order, source * row_count, row_count, half_span)
    grad_q, grad_k, grad_v = block_terms(key_block, value_block, key_pos)
    dq_acc = dq_acc + grad_q
    dk_mine, dv_mine = (
        passed_along((dk_acc + grad_k).astype(jnp.bfloat16), "ctx", 1).astype(jnp.float32),
        passed_along((dv_acc + grad_v).astype(jnp.bfloat16), "ctx", 1).astype(jnp.float32),
    )
    grad_local = dq_acc.reshape(row_count, kv_heads * groups * head_dim).astype(jnp.bfloat16)
    grad_query = lax.all_to_all(grad_local, "head", split_axis=0, concat_axis=1, tiled=True)
    grad_key = dk_mine.reshape(row_count, kv_heads * head_dim).astype(jnp.bfloat16)
    grad_value = dv_mine.reshape(row_count, kv_heads * head_dim).astype(jnp.bfloat16)
    return (grad_query, grad_key, grad_value)


def solution(mesh):
    return jax.shard_map(
        per_device,
        mesh=mesh,
        in_specs=(
            P("ctx", "head"),
            P("ctx", "head"),
            P("ctx", "head"),
            P("ctx", "head"),
            P("head", "ctx"),
            P(("ctx", "head"), None),
            P(),
        ),
        out_specs=(P(("ctx", "head"), None), P("ctx", "head"), P("ctx", "head")),
        check_vma=False,
    )
```

profile of v0, /device:TPU:2, one launch (start us, length us, event | category | flops | bytes accessed | tf_op | source)
XLA Modules:
  0.0 606.1 jit_solution(14967247438156929629)
XLA Ops:
  5.3 5.9 all-to-all-start
  13.0 5.8 all-to-all-done
  21.2 562.6 %while.25 = (s32[]{:T(128)}, bf16[192,1,128]{2,0,1:T(8,128)(2,1)}, bf16[192,1,128]{2,0,1:T(8,128)(2,1)}, f32[192,1,128]{2,0,1:T(8,128)}, f32[192,1,128]{2,0,1:T(...) while((s32[]{:T(128)}, bf16[192,1,128]{2,0,1:T(8,128)(2,1)}, ...), condition=%wide.region_4.5_spmd.clone, body=%wide.region_2.4_spmd.clone.sunk | while | flops 380292288 | bytes 11642844 | solution.py:90
  24.1 2.2 collective-permute-start
  29.1 1.9 fusion.83
  32.9 2.9 collective-permute-start.3
  38.9 1.9 collective-permute-done.3
  47.1 1.9 fusion.83
  50.9 3.1 collective-permute-start.3
  65.5 1.9 fusion.83
  69.3 2.9 collective-permute-start.3
  83.6 1.9 fusion.83
  87.4 3.1 collective-permute-start.3
  105.8 2.9 collective-permute-start.3
  123.8 3.1 collective-permute-start.3
  142.2 4.1 collective-permute-start.3
  153.0 2.0 collective-permute-start
  161.5 4.3 collective-permute-start.3
  172.3 2.2 collective-permute-start
  181.1 2.1 collective-permute-start.3
  185.1 2.1 collective-permute-done.2
  194.6 1.9 fusion.83
  198.4 3.0 collective-permute-start.3
  212.9 1.9 fusion.83
  216.7 2.1 collective-permute-start.3
  220.7 2.1 collective-permute-done.2
  234.0 3.0 collective-permute-start.3
  248.4 1.9 fusion.83
  252.2 2.1 collective-permute-start.3
  256.2 2.1 collective-permute-done.2
  269.6 3.0 collective-permute-start.3
  287.8 2.1 collective-permute-start.3
  291.8 2.1 collective-permute-done.2
  305.1 2.1 collective-permute-start.3
  309.1 2.1 collective-permute-done.2
  318.7 1.9 fusion.83
  322.5 2.1 collective-permute-start.3
  326.5 2.0 collective-permute-done.2
  339.8 2.3 collective-permute-start.3
  357.4 2.9 collective-permute-start.3
  375.5 3.1 collective-permute-start.3
  390.0 1.9 fusion.83
  393.8 2.9 collective-permute-start.3
  408.1 1.9 fusion.83
  411.9 3.1 collective-permute-start.3
  426.5 1.9 fusion.83
  430.3 4.1 collective-permute-start.3
  441.1 2.0 collective-permute-start
  449.6 4.3 collective-permute-start.3
  460.4 2.2 collective-permute-start
  465.4 1.9 fusion.83
  469.2 2.1 collective-permute-start.3
  473.2 2.1 collective-permute-done.2
  486.5 3.0 collective-permute-start.3
  504.7 2.1 collective-permute-start.3
  508.7 2.1 collective-permute-done.2
  522.1 3.0 collective-permute-start.3
  540.3 2.1 collective-permute-start.3
  544.3 2.1 collective-permute-done.2
  557.6 3.0 collective-permute-start.3
  575.8 2.1 collective-permute-start.3
  579.8 2.1 collective-permute-done.2
  589.1 5.2 all-to-all-start.1
  597.0 5.8 collective-permute-done.4
  (609 shorter events, 436.4 us)
Async XLA Ops:
  5.3 13.4 %all-to-all-start = ((bf16[24,8,1024]{2,0,1:T(8,128)(2,1)}), bf16[24,8,1024]{2,0,1:T(8,128)(2,1)S(1)}, u32[]{:S(2)}, u32[]{:S(2)}) async-start(bf16[24,8,1024]{2,0,1:T(8,128)(2,1)} %bitcast.210), calls=%async_computation | async-start | bytes 786432 | tf_op jit(solution)/shard_map/all_to_all | solution.py:53
  22.7 14.9 %collective-permute-start.1 = (bf16[192,1,128]{2,0,1:T(8,128)(2,1)}, bf16[192,1,128]{2,0,1:T(8,128)(2,1)}, u32[]{:S(2)}, u32[]{:S(2)}) collective-permute-start(bf16[192,1,128]{2,0,1:T(8,128)(2,1)} %copy.99), channel_id=1, source_target_pairs={{248,0},{0,8},{8,16},{16,24},{24,32},{32,40},{40,48},{48,56},{56,6... | collective-permute-start | bytes 147464 | tf_op jit(solution)/shard_map/while/body/eval_jaxpr/ppermute | solution.py:14
  24.1 13.5 %collective-permute-start = (bf16[192,1,128]{2,0,1:T(8,128)(2,1)}, bf16[192,1,128]{2,0,1:T(8,128)(2,1)}, u32[]{:S(2)}, u32[]{:S(2)}) collective-permute-start(bf16[192,1,128]{2,0,1:T(8,128)(2,1)} %copy.98), channel_id=1, source_target_pairs={{248,0},{0,8},{8,16},{16,24},{24,32},{32,40},{40,48},{48,56},{56,6... | collective-permute-start | bytes 147464 | tf_op jit(solution)/shard_map/while/body/eval_jaxpr/ppermute | solution.py:14
  42.2 13.7 %collective-permute-start.1 = (bf16[192,1,128]{2,0,1:T(8,128)(2,1)}, bf16[192,1,128]{2,0,1:T(8,128)(2,1)}, u32[]{:S(2)}, u32[]{:S(2)}) collective-permute-start(bf16[192,1,128]{2,0,1:T(8,128)(2,1)} %copy.99), channel_id=1, source_target_pairs={{248,0},{0,8},{8,16},{16,24},{24,32},{32,40},{40,48},{48,56},{56,6... | collective-permute-start | bytes 147464 | tf_op jit(solution)/shard_map/while/body/eval_jaxpr/ppermute | solution.py:14
  43.7 12.3 %collective-permute-start = (bf16[192,1,128]{2,0,1:T(8,128)(2,1)}, bf16[192,1,128]{2,0,1:T(8,128)(2,1)}, u32[]{:S(2)}, u32[]{:S(2)}) collective-permute-start(bf16[192,1,128]{2,0,1:T(8,128)(2,1)} %copy.98), channel_id=1, source_target_pairs={{248,0},{0,8},{8,16},{16,24},{24,32},{32,40},{40,48},{48,56},{56,6... | collective-permute-start | bytes 147464 | tf_op jit(solution)/shard_map/while/body/eval_jaxpr/ppermute | solution.py:14
  60.3 13.7 %collective-permute-start.1 = (bf16[192,1,128]{2,0,1:T(8,128)(2,1)}, bf16[192,1,128]{2,0,1:T(8,128)(2,1)}, u32[]{:S(2)}, u32[]{:S(2)}) collective-permute-start(bf16[192,1,128]{2,0,1:T(8,128)(2,1)} %copy.99), channel_id=1, source_target_pairs={{248,0},{0,8},{8,16},{16,24},{24,32},{32,40},{40,48},{48,56},{56,6... | collective-permute-start | bytes 147464 | tf_op jit(solution)/shard_map/while/body/eval_jaxpr/ppermute | solution.py:14
  61.8 12.3 %collective-permute-start = (bf16[192,1,128]{2,0,1:T(8,128)(2,1)}, bf16[192,1,128]{2,0,1:T(8,128)(2,1)}, u32[]{:S(2)}, u32[]{:S(2)}) collective-permute-start(bf16[192,1,128]{2,0,1:T(8,128)(2,1)} %copy.98), channel_id=1, source_target_pairs={{248,0},{0,8},{8,16},{16,24},{24,32},{32,40},{40,48},{48,56},{56,6... | collective-permute-start | bytes 147464 | tf_op jit(solution)/shard_map/while/body/eval_jaxpr/ppermute | solution.py:14
  78.7 13.7 %collective-permute-start.1 = (bf16[192,1,128]{2,0,1:T(8,128)(2,1)}, bf16[192,1,128]{2,0,1:T(8,128)(2,1)}, u32[]{:S(2)}, u32[]{:S(2)}) collective-permute-start(bf16[192,1,128]{2,0,1:T(8,128)(2,1)} %copy.99), channel_id=1, source_target_pairs={{248,0},{0,8},{8,16},{16,24},{24,32},{32,40},{40,48},{48,56},{56,6... | collective-permute-start | bytes 147464 | tf_op jit(solution)/shard_map/while/body/eval_jaxpr/ppermute | solution.py:14
  80.1 12.3 %collective-permute-start = (bf16[192,1,128]{2,0,1:T(8,128)(2,1)}, bf16[192,1,128]{2,0,1:T(8,128)(2,1)}, u32[]{:S(2)}, u32[]{:S(2)}) collective-permute-start(bf16[192,1,128]{2,0,1:T(8,128)(2,1)} %copy.98), channel_id=1, source_target_pairs={{248,0},{0,8},{8,16},{16,24},{24,32},{32,40},{40,48},{48,56},{56,6... | collective-permute-start | bytes 147464 | tf_op jit(solution)/shard_map/while/body/eval_jaxpr/ppermute | solution.py:14
  96.8 13.7 %collective-permute-start.1 = (bf16[192,1,128]{2,0,1:T(8,128)(2,1)}, bf16[192,1,128]{2,0,1:T(8,128)(2,1)}, u32[]{:S(2)}, u32[]{:S(2)}) collective-permute-start(bf16[192,1,128]{2,0,1:T(8,128)(2,1)} %copy.99), channel_id=1, source_target_pairs={{248,0},{0,8},{8,16},{16,24},{24,32},{32,40},{40,48},{48,56},{56,6... | collective-permute-start | bytes 147464 | tf_op jit(solution)/shard_map/while/body/eval_jaxpr/ppermute | solution.py:14
  98.2 12.3 %collective-permute-start = (bf16[192,1,128]{2,0,1:T(8,128)(2,1)}, bf16[192,1,128]{2,0,1:T(8,128)(2,1)}, u32[]{:S(2)}, u32[]{:S(2)}) collective-permute-start(bf16[192,1,128]{2,0,1:T(8,128)(2,1)} %copy.98), channel_id=1, source_target_pairs={{248,0},{0,8},{8,16},{16,24},{24,32},{32,40},{40,48},{48,56},{56,6... | collective-permute-start | bytes 147464 | tf_op jit(solution)/shard_map/while/body/eval_jaxpr/ppermute | solution.py:14
  115.1 13.7 %collective-permute-start.1 = (bf16[192,1,128]{2,0,1:T(8,128)(2,1)}, bf16[192,1,128]{2,0,1:T(8,128)(2,1)}, u32[]{:S(2)}, u32[]{:S(2)}) collective-permute-start(bf16[192,1,128]{2,0,1:T(8,128)(2,1)} %copy.99), channel_id=1, source_target_pairs={{248,0},{0,8},{8,16},{16,24},{24,32},{32,40},{40,48},{48,56},{56,6... | collective-permute-start | bytes 147464 | tf_op jit(solution)/shard_map/while/body/eval_jaxpr/ppermute | solution.py:14
  116.6 12.3 %collective-permute-start = (bf16[192,1,128]{2,0,1:T(8,128)(2,1)}, bf16[192,1,128]{2,0,1:T(8,128)(2,1)}, u32[]{:S(2)}, u32[]{:S(2)}) collective-permute-start(bf16[192,1,128]{2,0,1:T(8,128)(2,1)} %copy.98), channel_id=1, source_target_pairs={{248,0},{0,8},{8,16},{16,24},{24,32},{32,40},{40,48},{48,56},{56,6... | collective-permute-start | bytes 147464 | tf_op jit(solution)/shard_map/while/body/eval_jaxpr/ppermute | solution.py:14
  133.2 15.0 %collective-permute-start.1 = (bf16[192,1,128]{2,0,1:T(8,128)(2,1)}, bf16[192,1,128]{2,0,1:T(8,128)(2,1)}, u32[]{:S(2)}, u32[]{:S(2)}) collective-permute-start(bf16[192,1,128]{2,0,1:T(8,128)(2,1)} %copy.99), channel_id=1, source_target_pairs={{248,0},{0,8},{8,16},{16,24},{24,32},{32,40},{40,48},{48,56},{56,6... | collective-permute-start | bytes 147464 | tf_op jit(solution)/shard_map/while/body/eval_jaxpr/ppermute | solution.py:14
  134.7 13.5 %collective-permute-start = (bf16[192,1,128]{2,0,1:T(8,128)(2,1)}, bf16[192,1,128]{2,0,1:T(8,128)(2,1)}, u32[]{:S(2)}, u32[]{:S(2)}) collective-permute-start(bf16[192,1,128]{2,0,1:T(8,128)(2,1)} %copy.98), channel_id=1, source_target_pairs={{248,0},{0,8},{8,16},{16,24},{24,32},{32,40},{40,48},{48,56},{56,6... | collective-permute-start | bytes 147464 | tf_op jit(solution)/shard_map/while/body/eval_jaxpr/ppermute | solution.py:14
  151.6 16.2 %collective-permute-start.1 = (bf16[192,1,128]{2,0,1:T(8,128)(2,1)}, bf16[192,1,128]{2,0,1:T(8,128)(2,1)}, u32[]{:S(2)}, u32[]{:S(2)}) collective-permute-start(bf16[192,1,128]{2,0,1:T(8,128)(2,1)} %copy.99), channel_id=1, source_target_pairs={{248,0},{0,8},{8,16},{16,24},{24,32},{32,40},{40,48},{48,56},{56,6... | collective-permute-start | bytes 147464 | tf_op jit(solution)/shard_map/while/body/eval_jaxpr/ppermute | solution.py:14
  153.0 14.7 %collective-permute-start = (bf16[192,1,128]{2,0,1:T(8,128)(2,1)}, bf16[192,1,128]{2,0,1:T(8,128)(2,1)}, u32[]{:S(2)}, u32[]{:S(2)}) collective-permute-start(bf16[192,1,128]{2,0,1:T(8,128)(2,1)} %copy.98), channel_id=1, source_target_pairs={{248,0},{0,8},{8,16},{16,24},{24,32},{32,40},{40,48},{48,56},{56,6... | collective-permute-start | bytes 147464 | tf_op jit(solution)/shard_map/while/body/eval_jaxpr/ppermute | solution.py:14
  170.9 14.2 %collective-permute-start.1 = (bf16[192,1,128]{2,0,1:T(8,128)(2,1)}, bf16[192,1,128]{2,0,1:T(8,128)(2,1)}, u32[]{:S(2)}, u32[]{:S(2)}) collective-permute-start(bf16[192,1,128]{2,0,1:T(8,128)(2,1)} %copy.99), channel_id=1, source_target_pairs={{248,0},{0,8},{8,16},{16,24},{24,32},{32,40},{40,48},{48,56},{56,6... | collective-permute-start | bytes 147464 | tf_op jit(solution)/shard_map/while/body/eval_jaxpr/ppermute | solution.py:14
  172.3 12.8 %collective-permute-start = (bf16[192,1,128]{2,0,1:T(8,128)(2,1)}, bf16[192,1,128]{2,0,1:T(8,128)(2,1)}, u32[]{:S(2)}, u32[]{:S(2)}) collective-permute-start(bf16[192,1,128]{2,0,1:T(8,128)(2,1)} %copy.98), channel_id=1, source_target_pairs={{248,0},{0,8},{8,16},{16,24},{24,32},{32,40},{40,48},{48,56},{56,6... | collective-permute-start | bytes 147464 | tf_op jit(solution)/shard_map/while/body/eval_jaxpr/ppermute | solution.py:14
  190.5 12.8 %collective-permute-start.1 = (bf16[192,1,128]{2,0,1:T(8,128)(2,1)}, bf16[192,1,128]{2,0,1:T(8,128)(2,1)}, u32[]{:S(2)}, u32[]{:S(2)}) collective-permute-start(bf16[192,1,128]{2,0,1:T(8,128)(2,1)} %copy.99), channel_id=1, source_target_pairs={{248,0},{0,8},{8,16},{16,24},{24,32},{32,40},{40,48},{48,56},{56,6... | collective-permute-start | bytes 147464 | tf_op jit(solution)/shard_map/while/body/eval_jaxpr/ppermute | solution.py:14
  191.9 11.4 %collective-permute-start = (bf16[192,1,128]{2,0,1:T(8,128)(2,1)}, bf16[192,1,128]{2,0,1:T(8,128)(2,1)}, u32[]{:S(2)}, u32[]{:S(2)}) collective-permute-start(bf16[192,1,128]{2,0,1:T(8,128)(2,1)} %copy.98), channel_id=1, source_target_pairs={{248,0},{0,8},{8,16},{16,24},{24,32},{32,40},{40,48},{48,56},{56,6... | collective-permute-start | bytes 147464 | tf_op jit(solution)/shard_map/while/body/eval_jaxpr/ppermute | solution.py:14
  207.8 12.8 %collective-permute-start.1 = (bf16[192,1,128]{2,0,1:T(8,128)(2,1)}, bf16[192,1,128]{2,0,1:T(8,128)(2,1)}, u32[]{:S(2)}, u32[]{:S(2)}) collective-permute-start(bf16[192,1,128]{2,0,1:T(8,128)(2,1)} %copy.99), channel_id=1, source_target_pairs={{248,0},{0,8},{8,16},{16,24},{24,32},{32,40},{40,48},{48,56},{56,6... | collective-permute-start | bytes 147464 | tf_op jit(solution)/shard_map/while/body/eval_jaxpr/ppermute | solution.py:14
  209.3 11.4 %collective-permute-start = (bf16[192,1,128]{2,0,1:T(8,128)(2,1)}, bf16[192,1,128]{2,0,1:T(8,128)(2,1)}, u32[]{:S(2)}, u32[]{:S(2)}) collective-permute-start(bf16[192,1,128]{2,0,1:T(8,128)(2,1)} %copy.98), channel_id=1, source_target_pairs={{248,0},{0,8},{8,16},{16,24},{24,32},{32,40},{40,48},{48,56},{56,6... | collective-permute-start | bytes 147464 | tf_op jit(solution)/shard_map/while/body/eval_jaxpr/ppermute | solution.py:14
  226.0 12.8 %collective-permute-start.1 = (bf16[192,1,128]{2,0,1:T(8,128)(2,1)}, bf16[192,1,128]{2,0,1:T(8,128)(2,1)}, u32[]{:S(2)}, u32[]{:S(2)}) collective-permute-start(bf16[192,1,128]{2,0,1:T(8,128)(2,1)} %copy.99), channel_id=1, source_target_pairs={{248,0},{0,8},{8,16},{16,24},{24,32},{32,40},{40,48},{48,56},{56,6... | collective-permute-start | bytes 147464 | tf_op jit(solution)/shard_map/while/body/eval_jaxpr/ppermute | solution.py:14
  227.5 11.4 %collective-permute-start = (bf16[192,1,128]{2,0,1:T(8,128)(2,1)}, bf16[192,1,128]{2,0,1:T(8,128)(2,1)}, u32[]{:S(2)}, u32[]{:S(2)}) collective-permute-start(bf16[192,1,128]{2,0,1:T(8,128)(2,1)} %copy.98), channel_id=1, source_target_pairs={{248,0},{0,8},{8,16},{16,24},{24,32},{32,40},{40,48},{48,56},{56,6... | collective-permute-start | bytes 147464 | tf_op jit(solution)/shard_map/while/body/eval_jaxpr/ppermute | solution.py:14
  243.4 12.8 %collective-permute-start.1 = (bf16[192,1,128]{2,0,1:T(8,128)(2,1)}, bf16[192,1,128]{2,0,1:T(8,128)(2,1)}, u32[]{:S(2)}, u32[]{:S(2)}) collective-permute-start(bf16[192,1,128]{2,0,1:T(8,128)(2,1)} %copy.99), channel_id=1, source_target_pairs={{248,0},{0,8},{8,16},{16,24},{24,32},{32,40},{40,48},{48,56},{56,6... | collective-permute-start | bytes 147464 | tf_op jit(solution)/shard_map/while/body/eval_jaxpr/ppermute | solution.py:14
  244.8 11.4 %collective-permute-start = (bf16[192,1,128]{2,0,1:T(8,128)(2,1)}, bf16[192,1,128]{2,0,1:T(8,128)(2,1)}, u32[]{:S(2)}, u32[]{:S(2)}) collective-permute-start(bf16[192,1,128]{2,0,1:T(8,128)(2,1)} %copy.98), channel_id=1, source_target_pairs={{248,0},{0,8},{8,16},{16,24},{24,32},{32,40},{40,48},{48,56},{56,6... | collective-permute-start | bytes 147464 | tf_op jit(solution)/shard_map/while/body/eval_jaxpr/ppermute | solution.py:14
  261.6 12.8 %collective-permute-start.1 = (bf16[192,1,128]{2,0,1:T(8,128)(2,1)}, bf16[192,1,128]{2,0,1:T(8,128)(2,1)}, u32[]{:S(2)}, u32[]{:S(2)}) collective-permute-start(bf16[192,1,128]{2,0,1:T(8,128)(2,1)} %copy.99), channel_id=1, source_target_pairs={{248,0},{0,8},{8,16},{16,24},{24,32},{32,40},{40,48},{48,56},{56,6... | collective-permute-start | bytes 147464 | tf_op jit(solution)/shard_map/while/body/eval_jaxpr/ppermute | solution.py:14
  263.0 11.4 %collective-permute-start = (bf16[192,1,128]{2,0,1:T(8,128)(2,1)}, bf16[192,1,128]{2,0,1:T(8,128)(2,1)}, u32[]{:S(2)}, u32[]{:S(2)}) collective-permute-start(bf16[192,1,128]{2,0,1:T(8,128)(2,1)} %copy.98), channel_id=1, source_target_pairs={{248,0},{0,8},{8,16},{16,24},{24,32},{32,40},{40,48},{48,56},{56,6... | collective-permute-start | bytes 147464 | tf_op jit(solution)/shard_map/while/body/eval_jaxpr/ppermute | solution.py:14
  278.9 12.8 %collective-permute-start.1 = (bf16[192,1,128]{2,0,1:T(8,128)(2,1)}, bf16[192,1,128]{2,0,1:T(8,128)(2,1)}, u32[]{:S(2)}, u32[]{:S(2)}) collective-permute-start(bf16[192,1,128]{2,0,1:T(8,128)(2,1)} %copy.99), channel_id=1, source_target_pairs={{248,0},{0,8},{8,16},{16,24},{24,32},{32,40},{40,48},{48,56},{56,6... | collective-permute-start | bytes 147464 | tf_op jit(solution)/shard_map/while/body/eval_jaxpr/ppermute | solution.py:14
  280.4 11.4 %collective-permute-start = (bf16[192,1,128]{2,0,1:T(8,128)(2,1)}, bf16[192,1,128]{2,0,1:T(8,128)(2,1)}, u32[]{:S(2)}, u32[]{:S(2)}) collective-permute-start(bf16[192,1,128]{2,0,1:T(8,128)(2,1)} %copy.98), channel_id=1, source_target_pairs={{248,0},{0,8},{8,16},{16,24},{24,32},{32,40},{40,48},{48,56},{56,6... | collective-permute-start | bytes 147464 | tf_op jit(solution)/shard_map/while/body/eval_jaxpr/ppermute | solution.py:14
  297.2 12.0 %collective-permute-start.1 = (bf16[192,1,128]{2,0,1:T(8,128)(2,1)}, bf16[192,1,128]{2,0,1:T(8,128)(2,1)}, u32[]{:S(2)}, u32[]{:S(2)}) collective-permute-start(bf16[192,1,128]{2,0,1:T(8,128)(2,1)} %copy.99), channel_id=1, source_target_pairs={{248,0},{0,8},{8,16},{16,24},{24,32},{32,40},{40,48},{48,56},{56,6... | collective-permute-start | bytes 147464 | tf_op jit(solution)/shard_map/while/body/eval_jaxpr/ppermute | solution.py:14
  298.6 10.5 %collective-permute-start = (bf16[192,1,128]{2,0,1:T(8,128)(2,1)}, bf16[192,1,128]{2,0,1:T(8,128)(2,1)}, u32[]{:S(2)}, u32[]{:S(2)}) collective-permute-start(bf16[192,1,128]{2,0,1:T(8,128)(2,1)} %copy.98), channel_id=1, source_target_pairs={{248,0},{0,8},{8,16},{16,24},{24,32},{32,40},{40,48},{48,56},{56,6... | collective-permute-start | bytes 147464 | tf_op jit(solution)/shard_map/while/body/eval_jaxpr/ppermute | solution.py:14
  314.5 12.0 %collective-permute-start.1 = (bf16[192,1,128]{2,0,1:T(8,128)(2,1)}, bf16[192,1,128]{2,0,1:T(8,128)(2,1)}, u32[]{:S(2)}, u32[]{:S(2)}) collective-permute-start(bf16[192,1,128]{2,0,1:T(8,128)(2,1)} %copy.99), channel_id=1, source_target_pairs={{248,0},{0,8},{8,16},{16,24},{24,32},{32,40},{40,48},{48,56},{56,6... | collective-permute-start | bytes 147464 | tf_op jit(solution)/shard_map/while/body/eval_jaxpr/ppermute | solution.py:14
  315.9 10.5 %collective-permute-start = (bf16[192,1,128]{2,0,1:T(8,128)(2,1)}, bf16[192,1,128]{2,0,1:T(8,128)(2,1)}, u32[]{:S(2)}, u32[]{:S(2)}) collective-permute-start(bf16[192,1,128]{2,0,1:T(8,128)(2,1)} %copy.98), channel_id=1, source_target_pairs={{248,0},{0,8},{8,16},{16,24},{24,32},{32,40},{40,48},{48,56},{56,6... | collective-permute-start | bytes 147464 | tf_op jit(solution)/shard_map/while/body/eval_jaxpr/ppermute | solution.py:14
  331.8 12.2 %collective-permute-start.1 = (bf16[192,1,128]{2,0,1:T(8,128)(2,1)}, bf16[192,1,128]{2,0,1:T(8,128)(2,1)}, u32[]{:S(2)}, u32[]{:S(2)}) collective-permute-start(bf16[192,1,128]{2,0,1:T(8,128)(2,1)} %copy.99), channel_id=1, source_target_pairs={{248,0},{0,8},{8,16},{16,24},{24,32},{32,40},{40,48},{48,56},{56,6... | collective-permute-start | bytes 147464 | tf_op jit(solution)/shard_map/while/body/eval_jaxpr/ppermute | solution.py:14
  333.3 10.8 %collective-permute-start = (bf16[192,1,128]{2,0,1:T(8,128)(2,1)}, bf16[192,1,128]{2,0,1:T(8,128)(2,1)}, u32[]{:S(2)}, u32[]{:S(2)}) collective-permute-start(bf16[192,1,128]{2,0,1:T(8,128)(2,1)} %copy.98), channel_id=1, source_target_pairs={{248,0},{0,8},{8,16},{16,24},{24,32},{32,40},{40,48},{48,56},{56,6... | collective-permute-start | bytes 147464 | tf_op jit(solution)/shard_map/while/body/eval_jaxpr/ppermute | solution.py:14
  349.2 12.9 %collective-permute-start.1 = (bf16[192,1,128]{2,0,1:T(8,128)(2,1)}, bf16[192,1,128]{2,0,1:T(8,128)(2,1)}, u32[]{:S(2)}, u32[]{:S(2)}) collective-permute-start(bf16[192,1,128]{2,0,1:T(8,128)(2,1)} %copy.99), channel_id=1, source_target_pairs={{248,0},{0,8},{8,16},{16,24},{24,32},{32,40},{40,48},{48,56},{56,6... | collective-permute-start | bytes 147464 | tf_op jit(solution)/shard_map/while/body/eval_jaxpr/ppermute | solution.py:14
  350.6 11.5 %collective-permute-start = (bf16[192,1,128]{2,0,1:T(8,128)(2,1)}, bf16[192,1,128]{2,0,1:T(8,128)(2,1)}, u32[]{:S(2)}, u32[]{:S(2)}) collective-permute-start(bf16[192,1,128]{2,0,1:T(8,128)(2,1)} %copy.98), channel_id=1, source_target_pairs={{248,0},{0,8},{8,16},{16,24},{24,32},{32,40},{40,48},{48,56},{56,6... | collective-permute-start | bytes 147464 | tf_op jit(solution)/shard_map/while/body/eval_jaxpr/ppermute | solution.py:14
  366.7 13.7 %collective-permute-start.1 = (bf16[192,1,128]{2,0,1:T(8,128)(2,1)}, bf16[192,1,128]{2,0,1:T(8,128)(2,1)}, u32[]{:S(2)}, u32[]{:S(2)}) collective-permute-start(bf16[192,1,128]{2,0,1:T(8,128)(2,1)} %copy.99), channel_id=1, source_target_pairs={{248,0},{0,8},{8,16},{16,24},{24,32},{32,40},{40,48},{48,56},{56,6... | collective-permute-start | bytes 147464 | tf_op jit(solution)/shard_map/while/body/eval_jaxpr/ppermute | solution.py:14
  368.2 12.3 %collective-permute-start = (bf16[192,1,128]{2,0,1:T(8,128)(2,1)}, bf16[192,1,128]{2,0,1:T(8,128)(2,1)}, u32[]{:S(2)}, u32[]{:S(2)}) collective-permute-start(bf16[192,1,128]{2,0,1:T(8,128)(2,1)} %copy.98), channel_id=1, source_target_pairs={{248,0},{0,8},{8,16},{16,24},{24,32},{32,40},{40,48},{48,56},{56,6... | collective-permute-start | bytes 147464 | tf_op jit(solution)/shard_map/while/body/eval_jaxpr/ppermute | solution.py:14
  384.8 13.7 %collective-permute-start.1 = (bf16[192,1,128]{2,0,1:T(8,128)(2,1)}, bf16[192,1,128]{2,0,1:T(8,128)(2,1)}, u32[]{:S(2)}, u32[]{:S(2)}) collective-permute-start(bf16[192,1,128]{2,0,1:T(8,128)(2,1)} %copy.99), channel_id=1, source_target_pairs={{248,0},{0,8},{8,16},{16,24},{24,32},{32,40},{40,48},{48,56},{56,6... | collective-permute-start | bytes 147464 | tf_op jit(solution)/shard_map/while/body/eval_jaxpr/ppermute | solution.py:14
  386.3 12.3 %collective-permute-start = (bf16[192,1,128]{2,0,1:T(8,128)(2,1)}, bf16[192,1,128]{2,0,1:T(8,128)(2,1)}, u32[]{:S(2)}, u32[]{:S(2)}) collective-permute-start(bf16[192,1,128]{2,0,1:T(8,128)(2,1)} %copy.98), channel_id=1, source_target_pairs={{248,0},{0,8},{8,16},{16,24},{24,32},{32,40},{40,48},{48,56},{56,6... | collective-permute-start | bytes 147464 | tf_op jit(solution)/shard_map/while/body/eval_jaxpr/ppermute | solution.py:14
  403.2 13.7 %collective-permute-start.1 = (bf16[192,1,128]{2,0,1:T(8,128)(2,1)}, bf16[192,1,128]{2,0,1:T(8,128)(2,1)}, u32[]{:S(2)}, u32[]{:S(2)}) collective-permute-start(bf16[192,1,128]{2,0,1:T(8,128)(2,1)} %copy.99), channel_id=1, source_target_pairs={{248,0},{0,8},{8,16},{16,24},{24,32},{32,40},{40,48},{48,56},{56,6... | collective-permute-start | bytes 147464 | tf_op jit(solution)/shard_map/while/body/eval_jaxpr/ppermute | solution.py:14
  404.6 12.3 %collective-permute-start = (bf16[192,1,128]{2,0,1:T(8,128)(2,1)}, bf16[192,1,128]{2,0,1:T(8,128)(2,1)}, u32[]{:S(2)}, u32[]{:S(2)}) collective-permute-start(bf16[192,1,128]{2,0,1:T(8,128)(2,1)} %copy.98), channel_id=1, source_target_pairs={{248,0},{0,8},{8,16},{16,24},{24,32},{32,40},{40,48},{48,56},{56,6... | collective-permute-start | bytes 147464 | tf_op jit(solution)/shard_map/while/body/eval_jaxpr/ppermute | solution.py:14
  421.3 15.0 %collective-permute-start.1 = (bf16[192,1,128]{2,0,1:T(8,128)(2,1)}, bf16[192,1,128]{2,0,1:T(8,128)(2,1)}, u32[]{:S(2)}, u32[]{:S(2)}) collective-permute-start(bf16[192,1,128]{2,0,1:T(8,128)(2,1)} %copy.99), channel_id=1, source_target_pairs={{248,0},{0,8},{8,16},{16,24},{24,32},{32,40},{40,48},{48,56},{56,6... | collective-permute-start | bytes 147464 | tf_op jit(solution)/shard_map/while/body/eval_jaxpr/ppermute | solution.py:14
  422.7 13.5 %collective-permute-start = (bf16[192,1,128]{2,0,1:T(8,128)(2,1)}, bf16[192,1,128]{2,0,1:T(8,128)(2,1)}, u32[]{:S(2)}, u32[]{:S(2)}) collective-permute-start(bf16[192,1,128]{2,0,1:T(8,128)(2,1)} %copy.98), channel_id=1, source_target_pairs={{248,0},{0,8},{8,16},{16,24},{24,32},{32,40},{40,48},{48,56},{56,6... | collective-permute-start | bytes 147464 | tf_op jit(solution)/shard_map/while/body/eval_jaxpr/ppermute | solution.py:14
  439.7 16.2 %collective-permute-start.1 = (bf16[192,1,128]{2,0,1:T(8,128)(2,1)}, bf16[192,1,128]{2,0,1:T(8,128)(2,1)}, u32[]{:S(2)}, u32[]{:S(2)}) collective-permute-start(bf16[192,1,128]{2,0,1:T(8,128)(2,1)} %copy.99), channel_id=1, source_target_pairs={{248,0},{0,8},{8,16},{16,24},{24,32},{32,40},{40,48},{48,56},{56,6... | collective-permute-start | bytes 147464 | tf_op jit(solution)/shard_map/while/body/eval_jaxpr/ppermute | solution.py:14
  441.1 14.7 %collective-permute-start = (bf16[192,1,128]{2,0,1:T(8,128)(2,1)}, bf16[192,1,128]{2,0,1:T(8,128)(2,1)}, u32[]{:S(2)}, u32[]{:S(2)}) collective-permute-start(bf16[192,1,128]{2,0,1:T(8,128)(2,1)} %copy.98), channel_id=1, source_target_pairs={{248,0},{0,8},{8,16},{16,24},{24,32},{32,40},{40,48},{48,56},{56,6... | collective-permute-start | bytes 147464 | tf_op jit(solution)/shard_map/while/body/eval_jaxpr/ppermute | solution.py:14
  459.0 14.2 %collective-permute-start.1 = (bf16[192,1,128]{2,0,1:T(8,128)(2,1)}, bf16[192,1,128]{2,0,1:T(8,128)(2,1)}, u32[]{:S(2)}, u32[]{:S(2)}) collective-permute-start(bf16[192,1,128]{2,0,1:T(8,128)(2,1)} %copy.99), channel_id=1, source_target_pairs={{248,0},{0,8},{8,16},{16,24},{24,32},{32,40},{40,48},{48,56},{56,6... | collective-permute-start | bytes 147464 | tf_op jit(solution)/shard_map/while/body/eval_jaxpr/ppermute | solution.py:14
  460.4 12.8 %collective-permute-start = (bf16[192,1,128]{2,0,1:T(8,128)(2,1)}, bf16[192,1,128]{2,0,1:T(8,128)(2,1)}, u32[]{:S(2)}, u32[]{:S(2)}) collective-permute-start(bf16[192,1,128]{2,0,1:T(8,128)(2,1)} %copy.98), channel_id=1, source_target_pairs={{248,0},{0,8},{8,16},{16,24},{24,32},{32,40},{40,48},{48,56},{56,6... | collective-permute-start | bytes 147464 | tf_op jit(solution)/shard_map/while/body/eval_jaxpr/ppermute | solution.py:14
  478.5 12.8 %collective-permute-start.1 = (bf16[192,1,128]{2,0,1:T(8,128)(2,1)}, bf16[192,1,128]{2,0,1:T(8,128)(2,1)}, u32[]{:S(2)}, u32[]{:S(2)}) collective-permute-start(bf16[192,1,128]{2,0,1:T(8,128)(2,1)} %copy.99), channel_id=1, source_target_pairs={{248,0},{0,8},{8,16},{16,24},{24,32},{32,40},{40,48},{48,56},{56,6... | collective-permute-start | bytes 147464 | tf_op jit(solution)/shard_map/while/body/eval_jaxpr/ppermute | solution.py:14
  480.0 11.4 %collective-permute-start = (bf16[192,1,128]{2,0,1:T(8,128)(2,1)}, bf16[192,1,128]{2,0,1:T(8,128)(2,1)}, u32[]{:S(2)}, u32[]{:S(2)}) collective-permute-start(bf16[192,1,128]{2,0,1:T(8,128)(2,1)} %copy.98), channel_id=1, source_target_pairs={{248,0},{0,8},{8,16},{16,24},{24,32},{32,40},{40,48},{48,56},{56,6... | collective-permute-start | bytes 147464 | tf_op jit(solution)/shard_map/while/body/eval_jaxpr/ppermute | solution.py:14
  495.9 12.8 %collective-permute-start.1 = (bf16[192,1,128]{2,0,1:T(8,128)(2,1)}, bf16[192,1,128]{2,0,1:T(8,128)(2,1)}, u32[]{:S(2)}, u32[]{:S(2)}) collective-permute-start(bf16[192,1,128]{2,0,1:T(8,128)(2,1)} %copy.99), channel_id=1, source_target_pairs={{248,0},{0,8},{8,16},{16,24},{24,32},{32,40},{40,48},{48,56},{56,6... | collective-permute-start | bytes 147464 | tf_op jit(solution)/shard_map/while/body/eval_jaxpr/ppermute | solution.py:14
  497.3 11.4 %collective-permute-start = (bf16[192,1,128]{2,0,1:T(8,128)(2,1)}, bf16[192,1,128]{2,0,1:T(8,128)(2,1)}, u32[]{:S(2)}, u32[]{:S(2)}) collective-permute-start(bf16[192,1,128]{2,0,1:T(8,128)(2,1)} %copy.98), channel_id=1, source_target_pairs={{248,0},{0,8},{8,16},{16,24},{24,32},{32,40},{40,48},{48,56},{56,6... | collective-permute-start | bytes 147464 | tf_op jit(solution)/shard_map/while/body/eval_jaxpr/ppermute | solution.py:14
  514.1 12.8 %collective-permute-start.1 = (bf16[192,1,128]{2,0,1:T(8,128)(2,1)}, bf16[192,1,128]{2,0,1:T(8,128)(2,1)}, u32[]{:S(2)}, u32[]{:S(2)}) collective-permute-start(bf16[192,1,128]{2,0,1:T(8,128)(2,1)} %copy.99), channel_id=1, source_target_pairs={{248,0},{0,8},{8,16},{16,24},{24,32},{32,40},{40,48},{48,56},{56,6... | collective-permute-start | bytes 147464 | tf_op jit(solution)/shard_map/while/body/eval_jaxpr/ppermute | solution.py:14
  515.5 11.4 %collective-permute-start = (bf16[192,1,128]{2,0,1:T(8,128)(2,1)}, bf16[192,1,128]{2,0,1:T(8,128)(2,1)}, u32[]{:S(2)}, u32[]{:S(2)}) collective-permute-start(bf16[192,1,128]{2,0,1:T(8,128)(2,1)} %copy.98), channel_id=1, source_target_pairs={{248,0},{0,8},{8,16},{16,24},{24,32},{32,40},{40,48},{48,56},{56,6... | collective-permute-start | bytes 147464 | tf_op jit(solution)/shard_map/while/body/eval_jaxpr/ppermute | solution.py:14
  531.4 12.8 %collective-permute-start.1 = (bf16[192,1,128]{2,0,1:T(8,128)(2,1)}, bf16[192,1,128]{2,0,1:T(8,128)(2,1)}, u32[]{:S(2)}, u32[]{:S(2)}) collective-permute-start(bf16[192,1,128]{2,0,1:T(8,128)(2,1)} %copy.99), channel_id=1, source_target_pairs={{248,0},{0,8},{8,16},{16,24},{24,32},{32,40},{40,48},{48,56},{56,6... | collective-permute-start | bytes 147464 | tf_op jit(solution)/shard_map/while/body/eval_jaxpr/ppermute | solution.py:14
  532.9 11.4 %collective-permute-start = (bf16[192,1,128]{2,0,1:T(8,128)(2,1)}, bf16[192,1,128]{2,0,1:T(8,128)(2,1)}, u32[]{:S(2)}, u32[]{:S(2)}) collective-permute-start(bf16[192,1,128]{2,0,1:T(8,128)(2,1)} %copy.98), channel_id=1, source_target_pairs={{248,0},{0,8},{8,16},{16,24},{24,32},{32,40},{40,48},{48,56},{56,6... | collective-permute-start | bytes 147464 | tf_op jit(solution)/shard_map/while/body/eval_jaxpr/ppermute | solution.py:14
  549.7 12.8 %collective-permute-start.1 = (bf16[192,1,128]{2,0,1:T(8,128)(2,1)}, bf16[192,1,128]{2,0,1:T(8,128)(2,1)}, u32[]{:S(2)}, u32[]{:S(2)}) collective-permute-start(bf16[192,1,128]{2,0,1:T(8,128)(2,1)} %copy.99), channel_id=1, source_target_pairs={{248,0},{0,8},{8,16},{16,24},{24,32},{32,40},{40,48},{48,56},{56,6... | collective-permute-start | bytes 147464 | tf_op jit(solution)/shard_map/while/body/eval_jaxpr/ppermute | solution.py:14
  551.1 11.4 %collective-permute-start = (bf16[192,1,128]{2,0,1:T(8,128)(2,1)}, bf16[192,1,128]{2,0,1:T(8,128)(2,1)}, u32[]{:S(2)}, u32[]{:S(2)}) collective-permute-start(bf16[192,1,128]{2,0,1:T(8,128)(2,1)} %copy.98), channel_id=1, source_target_pairs={{248,0},{0,8},{8,16},{16,24},{24,32},{32,40},{40,48},{48,56},{56,6... | collective-permute-start | bytes 147464 | tf_op jit(solution)/shard_map/while/body/eval_jaxpr/ppermute | solution.py:14
  567.0 12.8 %collective-permute-start.1 = (bf16[192,1,128]{2,0,1:T(8,128)(2,1)}, bf16[192,1,128]{2,0,1:T(8,128)(2,1)}, u32[]{:S(2)}, u32[]{:S(2)}) collective-permute-start(bf16[192,1,128]{2,0,1:T(8,128)(2,1)} %copy.99), channel_id=1, source_target_pairs={{248,0},{0,8},{8,16},{16,24},{24,32},{32,40},{40,48},{48,56},{56,6... | collective-permute-start | bytes 147464 | tf_op jit(solution)/shard_map/while/body/eval_jaxpr/ppermute | solution.py:14
  568.4 11.4 %collective-permute-start = (bf16[192,1,128]{2,0,1:T(8,128)(2,1)}, bf16[192,1,128]{2,0,1:T(8,128)(2,1)}, u32[]{:S(2)}, u32[]{:S(2)}) collective-permute-start(bf16[192,1,128]{2,0,1:T(8,128)(2,1)} %copy.98), channel_id=1, source_target_pairs={{248,0},{0,8},{8,16},{16,24},{24,32},{32,40},{40,48},{48,56},{56,6... | collective-permute-start | bytes 147464 | tf_op jit(solution)/shard_map/while/body/eval_jaxpr/ppermute | solution.py:14
  589.1 15.0 %all-to-all-start.1 = ((bf16[8,24,1024]{2,1,0:T(8,128)(2,1)}), bf16[8,24,1024]{2,1,0:T(8,128)(2,1)S(1)}, u32[]{:S(2)}, u32[]{:S(2)}) async-start(bf16[8,24,1024]{2,1,0:T(8,128)(2,1)} %convert_element_type.81), calls=%async_computation.1 | async-start | bytes 786432 | tf_op jit(solution)/shard_map/all_to_all | solution.py:102
  (71 other events, 543.6 us)
where the time goes:
time: 617 us; the launch traced here: 606 us
  matrix products  239 us (39%)
  starting transfers between devices  125 us (20%)
  local copies, waits for them, and re-layouts  119 us (19%)
  waiting for transfers between devices  113 us (18%)
  other arithmetic  8.12 us (1%)
    ppermute x126, starting transfers between devices, passed_along(): return lax.ppermute(block, axis, route)  114 us
    ppermute x126, waiting for transfers between devices, passed_along(): return lax.ppermute(block, axis, route)  107 us
    while x62, local copies, waits for them, and re-layouts  87.8 us
    dot_general x32, matrix products, attend_block(): jnp.einsum('tngs,tngd->snd', dscores, query_heads, preferred_element_type...  60.1 us
    dot_general x32, matrix products, attend_block(): jnp.einsum('tngs,tngd->snd', prob_low, grad_heads, preferred_element_type...  59.9 us
    dot_general x32, matrix products, attend_block(): jnp.einsum('tngd,snd->tngs', query_heads, key_block, preferred_element_ty...  41.5 us
    dot_general x32, matrix products, attend_block(): jnp.einsum('tngs,snd->tngd', dscores, key_block, preferred_element_type=j...  39 us
    dot_general x32, matrix products, attend_block(): jnp.einsum('tngd,snd->tngs', grad_heads, value_block, preferred_element_t...  38 us
  transfers between devices with their start and end apart: 128, of which 63 were waited for; matrix products, arithmetic and copies ran while one was open for 51% of the time, Pallas kernels for 0%

commit v1 on v0

v1 whole, which is shorter than its diff:
```python
import functools

import jax
import jax.numpy as jnp
import numpy as np
from jax import lax
from jax.experimental import pallas as pl
from jax.experimental.pallas import tpu as pltpu
from jax.sharding import PartitionSpec as P
HD=128; G=8; SP=96
LOG2E=1.4426950408889634
SC=HD**-0.5
NT=(((1,),(1,)),((),()))
def kernel(nkb, KB, spans, kv_ref, qo_ref, qm_ref, do_ref, dm_ref, lse_ref, del_ref,
           dkv_ref, dq_ref, qs, ds_, kt, dqt, dka, dva):
    for s in range(4):
        src_q, src_d = (qo_ref, do_ref) if s<2 else (qm_ref, dm_ref)
        r0=(s%2)*SP
        for h in range(G):
            qs[pl.ds(s*768+h*SP,SP),:]=src_q[r0:r0+SP, h*HD:(h+1)*HD]
            ds_[pl.ds(s*768+h*SP,SP),:]=src_d[r0:r0+SP, h*HD:(h+1)*HD]
    dqt[...]=jnp.zeros_like(dqt)
    nsp=KB//SP
    def kb_body(kb,_):
        k=kv_ref[kb,:, :HD]
        kt[...]=k.astype(jnp.float32).T.astype(jnp.bfloat16)
        dka[...]=jnp.zeros_like(dka)
        dva[...]=jnp.zeros_like(dva)
        kspan=[spans[4+kb*nsp+j] for j in range(nsp)]
        kmin=functools.reduce(jnp.minimum,kspan)
        kmax=functools.reduce(jnp.maximum,kspan)
        def s_body(s,_):
            rs=spans[s]
            def work(masked):
                row=pl.multiple_of(s*768,768)
                q=qs[pl.ds(row,768),:]
                do=ds_[pl.ds(row,768),:]
                kk=kv_ref[kb,:, :HD]; vv=kv_ref[kb,:, HD:]
                st=lax.dot_general(kk,q,NT,preferred_element_type=jnp.float32)
                p=jnp.exp2(st*(SC*LOG2E)-lse_ref[s])
                if masked:
                    ki=lax.broadcasted_iota(jnp.int32,(KB,1),0)
                    kpos=ki%SP
                    base=jnp.full((KB,1),kspan[0]*SP,jnp.int32)
                    for j in range(1,nsp):
                        base=jnp.where(ki>=j*SP,kspan[j]*SP,base)
                    kpos=kpos+base
                    qpos=lax.broadcasted_iota(jnp.int32,(1,768),1)%SP+rs*SP
                    p=jnp.where(qpos>=kpos,p,0.0)
                dp=lax.dot_general(vv,do,NT,preferred_element_type=jnp.float32)
                dsb=(p*(dp-del_ref[s])).astype(jnp.bfloat16)
                pb=p.astype(jnp.bfloat16)
                dva[...]+=jnp.dot(pb,do,preferred_element_type=jnp.float32)
                dka[...]+=jnp.dot(dsb,q,preferred_element_type=jnp.float32)
                dqt[s]+=jnp.dot(kt[...],dsb,preferred_element_type=jnp.float32)
            @pl.when(kmax<rs)
            def _(): work(False)
            @pl.when((kmax>=rs)&(kmin<=rs))
            def _(): work(True)
            return 0
        lax.fori_loop(0,4,s_body,0)
        dkv_ref[kb,:, :HD]=dka[...]*SC
        dkv_ref[kb,:, HD:]=dva[...]
        return 0
    lax.fori_loop(0,nkb,kb_body,0)
    for s in range(4):
        t=dqt[s].T*SC
        for h in range(G):
            dq_ref[s*SP:(s+1)*SP, h*HD:(h+1)*HD]=t[h*SP:(h+1)*SP,:]

def attn(spans, kv, qo, qm, do, dm, lse, dl, KB):
    nkb=kv.shape[0]
    vm=pl.BlockSpec(memory_space=pltpu.VMEM)
    return pl.pallas_call(
        functools.partial(kernel,nkb,KB),
        out_shape=(jax.ShapeDtypeStruct((nkb,KB,256),jnp.float32), jax.ShapeDtypeStruct((384,1024),jnp.float32)),
        in_specs=[pl.BlockSpec(memory_space=pltpu.SMEM)]+[vm]*7,
        out_specs=(vm,vm),
        scratch_shapes=[pltpu.VMEM((3072,128),jnp.bfloat16)]*2+[pltpu.VMEM((128,KB),jnp.bfloat16),pltpu.VMEM((4,128,768),jnp.float32),
            pltpu.VMEM((KB,128),jnp.float32),pltpu.VMEM((KB,128),jnp.float32)],
        compiler_params=pltpu.CompilerParams(vmem_limit_bytes=56*2**20),
    )(spans,kv,qo,qm,do,dm,lse,dl)


N = 32
CORE = [(i, i ^ 1) for i in range(N)]
XSW = [(i, i ^ 2) for i in range(N)]


def zmap(f):
    return [(i, f(i // 4) * 4 + i % 4) for i in range(N)]


EVEN = zmap(lambda z: z ^ 1)
ODD = zmap(lambda z: (z + 1) % 8 if z % 2 else (z - 1) % 8)


def arrival(first, second):
    f = [dict((s // 4, d // 4) for s, d in m)for m in (first, second)]
    a0 = [[z] for z in range(8)]
    a1 = [a0[f[0][z]] for z in range(8)]
    a2 = [a0[f[1][z]] + a1[f[1][z]] for z in range(8)]
    a3 = [a2[f[0][z]] for z in range(8)]
    a4 = [a3[f[1][z]] for z in range(8)]
    return np.array([a0[z] + a1[z] + a2[z] + a3[z] + a4[z] for z in range(8)], np.int32)


ORDER_A = arrival(EVEN, ODD)
ORDER_B = arrival(ODD, EVEN)


def pp(x, route):
    return lax.ppermute(x, "ctx", route)


def gather(a0, first, second):
    a1 = pp(a0, first)
    a2 = pp(jnp.concatenate([a0, a1]), second)
    a3 = pp(a2, first)
    a4 = pp(a3, second)
    return jnp.concatenate([a0, a1, a2, a3, a4])


def scatter(d, first, second):
    low = lambda x: x.astype(jnp.bfloat16)
    t3 = d[4:6] + pp(low(d[6:8]), second)
    t2 = d[2:4] + pp(low(t3), first)
    t01 = d[0:2] + pp(low(t2), second)
    return t01[0] + pp(low(t01[1]), first)


def per_device(query_rows, key_rows, value_rows, attn_output, log_norms, grad_output, span_order):
    ctx = lax.axis_index("ctx")
    z, x_hi, core = ctx // 4, (ctx // 2) % 2, ctx % 2
    q_mate = pp(query_rows, CORE)
    kv = jnp.concatenate([key_rows, value_rows], axis=1)
    kvx = pp(kv, XSW)
    both = jnp.stack([kv, kvx])
    blocks_a = gather(both[None, :, :SP].reshape(1, 2 * SP, 256), EVEN, ODD)
    blocks_b = gather(both[None, :, SP:].reshape(1, 2 * SP, 256), ODD, EVEN)
    grad_rows = lax.all_to_all(grad_output, "head", split_axis=1, concat_axis=0, tiled=True)
    prod = grad_rows.astype(jnp.float32) * attn_output.astype(jnp.float32)
    delta = jnp.sum(prod.reshape(192, G, HD), axis=-1)
    stats = jnp.stack([
        (log_norms * LOG2E).reshape(G, 2, SP).transpose(1, 0, 2).reshape(2, 1, 768),
        delta.reshape(2, SP, G).transpose(0, 2, 1).reshape(2, 1, 768),
    ], axis=1)
    grad_mate = pp(grad_rows, CORE)
    stats = jnp.concatenate([stats, pp(stats, CORE)])
    kv_all = jnp.concatenate([blocks_a, blocks_b])
    za = jnp.asarray(ORDER_A)[z]
    zb = jnp.asarray(ORDER_B)[z]
    xs = jnp.stack([x_hi, 1 - x_hi])
    slot = lambda zz, j: (((zz[:, None] * 2 + xs[None, :]) * 2 + core) * 2 + j).reshape(-1)
    slots = jnp.concatenate([
        jnp.stack([2 * ctx, 2 * ctx + 1, 2 * (ctx ^ 1), 2 * (ctx ^ 1) + 1]),
        slot(za, 0), slot(zb, 1)])
    spans = span_order[slots]
    dkv, dq = attn(spans, kv_all, query_rows, q_mate, grad_rows, grad_mate, stats[:, 0], stats[:, 1], 192)
    ta = scatter(dkv[:8], EVEN, ODD)
    tb = scatter(dkv[8:], ODD, EVEN)
    t = jnp.stack([ta.reshape(2, SP, 256), tb.reshape(2, SP, 256)], axis=1)
    fin = t[0] + pp(t[1].astype(jnp.bfloat16), XSW)
    fin = fin.reshape(192, 256).astype(jnp.bfloat16)
    dq_own = (dq[:192] + pp(dq[192:].astype(jnp.bfloat16), CORE)).astype(jnp.bfloat16)
    grad_query = lax.all_to_all(dq_own, "head", split_axis=0, concat_axis=1, tiled=True)
    return (grad_query, fin[:, :HD], fin[:, HD:])


def solution(mesh):
    return jax.shard_map(
        per_device,
        mesh=mesh,
        in_specs=(
            P("ctx", "head"),
            P("ctx", "head"),
            P("ctx", "head"),
            P("ctx", "head"),
            P("head", "ctx"),
            P(("ctx", "head"), None),
            P(),
        ),
        out_specs=(P(("ctx", "head"), None), P("ctx", "head"), P("ctx", "head")),
        check_vma=False,
    )
```

time: 617 us -> 137 us (0.22); the launches traced: 606 us -> 136 us
  matrix products: 239 us -> 0 us
  local copies, waits for them, and re-layouts: 119 us -> 11.8 us
  starting transfers between devices: 125 us -> 42.7 us
  waiting for transfers between devices: 113 us -> 35.9 us
  Pallas kernels: 0 us -> 36.7 us
    dot_general x160 -> x0, matrix products: 239 us -> none  [the longest x32 60.1 us: attend_block(): jnp.einsum('tngs,tngd->snd', dscores, query_heads, preferred_element_type...]
    while x62 -> x0, local copies, waits for them, and re-layouts: 87.8 us -> none
    ppermute x126 -> x22, starting transfers between devices: 114 us -> 30.9 us  [pp(): return lax.ppermute(x, 'ctx', route)]
    ppermute x126 -> x22, waiting for transfers between devices: 107 us -> 35.9 us  [pp(): return lax.ppermute(x, 'ctx', route)]
    pallas_call x0 -> x1, Pallas kernels: none -> 36.7 us  [attn(): pl.pallas_call(functools.partial(kernel, nkb, KB), out_shape=(jax.ShapeDt...]
    another operation x31 -> x2, local copies, waits for them, and re-layouts: 20.2 us -> 0.17 us  [per_device(): jnp.stack([(log_norms * LOG2E).reshape(G, 2, SP).transpose(1, 0, 2).resha...]
  transfers between devices with their start and end apart: 128 -> 24, of which waited for: 63 -> 14; matrix products, arithmetic and copies ran while one was open for 51% -> 10% of each run, Pallas kernels for 0% -> 0%
where the time goes in v1:
time: 137 us; the launch traced here: 136 us
  starting transfers between devices  42.7 us (31%)
  Pallas kernels  36.7 us (27%)
  waiting for transfers between devices  35.9 us (26%)
  local copies, waits for them, and re-layouts  11.8 us (9%)
  other arithmetic  7.97 us (6%)
    pallas_call x1, Pallas kernels, attn(): pl.pallas_call(functools.partial(kernel, nkb, KB), out_shape=(jax.ShapeDt...  36.7 us
    ppermute x22, waiting for transfers between devices, pp(): return lax.ppermute(x, 'ctx', route)  35.9 us
    ppermute x22, starting transfers between devices, pp(): return lax.ppermute(x, 'ctx', route)  30.9 us
    all_to_all x1, starting transfers between devices, per_device(): lax.all_to_all(grad_output, 'head', split_axis=1, concat_axis=0, tiled=True)  6.06 us
    all_to_all x1, starting transfers between devices, per_device(): lax.all_to_all(dq_own, 'head', split_axis=0, concat_axis=1, tiled=True)  5.7 us
    unnamed x31, local copies, waits for them, and re-layouts  4.22 us
  transfers between devices with their start and end apart: 24, of which 14 were waited for; matrix products, arithmetic and copies ran while one was open for 10% of the time, Pallas kernels for 0%

profile of v1, /device:TPU:2, one launch (start us, length us, event | category | flops | bytes accessed | tf_op | source)
XLA Modules:
  0.0 136.1 jit_solution(9498594909880527708)
XLA Ops:
  0.7 0.9 constant_dynamic-update-slice_fusion.1
  1.5 0.8 constant_dynamic-update-slice_fusion
  2.3 2.2 %collective-permute-start = (bf16[192,256]{1,0:T(8,128)(2,1)S(1)}, bf16[192,256]{1,0:T(8,128)(2,1)S(1)}, u32[]{:S(2)}, u32[]{:S(2)}) collective-permute-start(bf16[192,256]{1,0:T(8,128)(2,1)S(1)} %constant_dynamic-update-slice_fusion), channel_id=1, source_target_pairs={{0,16},{8,24},{16,0},{24,8},{32,48},{40,56},{48,32},{56,40},{64,80... | collective-permute-start | bytes 294920 | tf_op jit(solution)/shard_map/ppermute | solution.py:113
  4.6 1.8 %copy.34 = bf16[3,8,8,1024]{3,2,0,1:T(8,128)(2,1)} copy(bf16[3,8,8,1024]{3,2,1,0:T(8,128)(2,1)} %bitcast.84) | data formatting | bytes 786432 | tf_op jit(solution)/shard_map/all_to_all | solution.py:141
  6.3 6.1 %all-to-all-start = ((bf16[24,8,1024]{2,0,1:T(8,128)(2,1)}), bf16[24,8,1024]{2,0,1:T(8,128)(2,1)S(1)}, u32[]{:S(2)}, u32[]{:S(2)}) async-start(bf16[24,8,1024]{2,0,1:T(8,128)(2,1)} %bitcast.65), calls=%async_computation | async-start | bytes 786432 | tf_op jit(solution)/shard_map/all_to_all | solution.py:141
  12.5 0.7 multiply_bitcast_fusion.1
  13.2 0.1 multiply_add_fusion
  13.3 0.1 concatenate.54
  13.4 0.1 concatenate.53
  13.5 0.1 concatenate.55
  13.6 0.1 reshape.313
  13.7 0.1 stack_reshape.12
  13.8 1.3 gather_fusion
  15.1 2.0 %collective-permute-start.1 = (bf16[1,192,256]{2,1,0:T(8,128)(2,1)S(1)}, bf16[1,192,256]{2,1,0:T(8,128)(2,1)S(1)}, u32[]{:S(2)}, u32[]{:S(2)}) collective-permute-start(bf16[1,192,256]{2,1,0:T(8,128)(2,1)S(1)} %bitcast.81), channel_id=1, source_target_pairs={{0,32},{8,40},{16,48},{24,56},{32,0},{40,8},{48,16},{56,24},{64,96... | collective-permute-start | bytes 294920 | tf_op jit(solution)/shard_map/ppermute | solution.py:113
  17.1 4.9 %collective-permute-start.5 = (bf16[1,192,256]{2,1,0:T(8,128)(2,1)S(1)}, bf16[1,192,256]{2,1,0:T(8,128)(2,1)S(1)}, u32[]{:S(2)}, u32[]{:S(2)}) collective-permute-start(bf16[1,192,256]{2,1,0:T(8,128)(2,1)S(1)} %bitcast.78), channel_id=1, source_target_pairs={{0,224},{8,232},{16,240},{24,248},{32,64},{40,72},{48,80},{56,88},... | collective-permute-start | bytes 294920 | tf_op jit(solution)/shard_map/ppermute | solution.py:113
  22.1 0.7 pad_maximum_fusion.1
  22.8 4.1 %collective-permute-start.2 = (bf16[2,192,256]{2,1,0:T(8,128)(2,1)}, bf16[2,192,256]{2,1,0:T(8,128)(2,1)}, u32[]{:S(2)}, u32[]{:S(2)}) collective-permute-start(bf16[2,192,256]{2,1,0:T(8,128)(2,1)} %pad_maximum_fusion.1), channel_id=1, source_target_pairs={{0,224},{8,232},{16,240},{24,248},{32,64},{40,72},{48,80},{56,88},... | collective-permute-start | bytes 589832 | tf_op jit(solution)/shard_map/ppermute | solution.py:113
  26.9 0.7 pad_maximum_fusion.2
  27.6 0.2 multiply_bitcast_fusion
  27.8 0.1 copy.31
  27.9 0.3 reduce_sum.9
  28.3 0.1 stack_reshape.13
  28.4 0.1 collective-permute-start.11
  28.5 0.6 collective-permute-start.10
  29.1 0.6 collective-permute-done.11
  29.7 2.2 %collective-permute-done.2 = bf16[2,192,256]{2,1,0:T(8,128)(2,1)} collective-permute-done((bf16[2,192,256]{2,1,0:T(8,128)(2,1)}, bf16[2,192,256]{2,1,0:T(8,128)(2,1)}, u32[]{:S(2)}, u32[]{:S(2)}) %collective-permute-start.2) | collective-permute-done | bytes 196640 | tf_op jit(solution)/shard_map/ppermute | solution.py:113
  32.0 2.3 %collective-permute-done.6 = bf16[2,192,256]{2,1,0:T(8,128)(2,1)} collective-permute-done((bf16[2,192,256]{2,1,0:T(8,128)(2,1)}, bf16[2,192,256]{2,1,0:T(8,128)(2,1)}, u32[]{:S(2)}, u32[]{:S(2)}) %collective-permute-start.6) | collective-permute-done | bytes 196640 | tf_op jit(solution)/shard_map/ppermute | solution.py:113
  34.2 1.1 collective-permute-start.7
  35.3 0.6 slice_bitcast_fusion.2
  35.9 2.3 %collective-permute-done.3 = bf16[2,192,256]{2,1,0:T(8,128)(2,1)S(1)} collective-permute-done((bf16[2,192,256]{2,1,0:T(8,128)(2,1)}, bf16[2,192,256]{2,1,0:T(8,128)(2,1)S(1)}, u32[]{:S(2)}, u32[]{:S(2)}) %collective-permute-start.3) | collective-permute-done | bytes 196640 | tf_op jit(solution)/shard_map/ppermute | solution.py:113
  38.2 2.6 %collective-permute-start.4 = (bf16[2,192,256]{2,1,0:T(8,128)(2,1)S(1)}, bf16[2,192,256]{2,1,0:T(8,128)(2,1)S(1)}, u32[]{:S(2)}, u32[]{:S(2)}) collective-permute-start(bf16[2,192,256]{2,1,0:T(8,128)(2,1)S(1)} %collective-permute-done.3), channel_id=1, source_target_pairs={{0,224},{8,232},{16,240},{24,248},{32,64},{40,72},{48,80},{56,88},... | collective-permute-start | bytes 589832 | tf_op jit(solution)/shard_map/ppermute | solution.py:113
  40.8 0.9 constant_dynamic-update-slice_fusion.9
  41.7 0.5 collective-permute-done.7
  42.3 3.3 %collective-permute-done.4 = bf16[2,192,256]{2,1,0:T(8,128)(2,1)S(1)} collective-permute-done((bf16[2,192,256]{2,1,0:T(8,128)(2,1)S(1)}, bf16[2,192,256]{2,1,0:T(8,128)(2,1)S(1)}, u32[]{:S(2)}, u32[]{:S(2)}) %collective-permute-start.4) | collective-permute-done | bytes 196640 | tf_op jit(solution)/shard_map/ppermute | solution.py:113
  45.6 0.9 constant_dynamic-update-slice_fusion.4
  46.5 1.4 collective-permute-done.8
  48.0 1.1 copy-done.3
  49.1 0.1 copy-done.8
  49.2 36.7 %shard_map.112 = (f32[16,192,256]{2,1,0:T(8,128)}, f32[384,1024]{1,0:T(8,128)}) custom-call(s32[36]{0:T(128)} %gather_fusion, bf16[16,192,256]{2,1,0:T(8,128)(2,1)} %copy-done.3, bf16[192,1024]{1,0:T(8,128)(2,1)} %qo_ref.1, bf16[192,1024]{1,0:T(8,128)(2,1)} %collective-permute-done.9.qm_ref, bf16[192,1024]{1,0:T(8,128)(2,1)} %bitcast.70, ...), custom_call_target="tpu_custom_call" | custom-call | tf_op jit(solution)/shard_map/pallas_call | solution.py:74
  85.9 2.2 %convert.17 = bf16[16,192,256]{2,1,0:T(8,128)(2,1)S(1)} convert(f32[16,192,256]{2,1,0:T(8,128)} %get-tuple-element.6) | non-fusion elementwise | flops 786432 | bytes 4718592 | tf_op jit(solution)/shard_map/convert.4
  88.2 0.1 collective-permute-start.17
  88.3 5.7 %collective-permute-done.17 = bf16[2,192,256]{2,1,0:T(8,128)(2,1)S(1)} collective-permute-done((bf16[2,192,256]{2,1,0:T(8,128)(2,1)S(1)}, bf16[2,192,256]{2,1,0:T(8,128)(2,1)S(1)}, u32[]{:S(2)}, u32[]{:S(2)}) %collective-permute-start.17) | collective-permute-done | bytes 196640 | tf_op jit(solution)/shard_map/ppermute | solution.py:113
  94.0 0.1 collective-permute-start.18
  94.1 3.2 %collective-permute-start.13 = (bf16[2,192,256]{2,1,0:T(8,128)(2,1)S(1)}, bf16[2,192,256]{2,1,0:T(8,128)(2,1)S(1)}, u32[]{:S(2)}, u32[]{:S(2)}) collective-permute-start(bf16[2,192,256]{2,1,0:T(8,128)(2,1)S(1)} %get-tuple-element.10), channel_id=1, source_target_pairs={{0,224},{8,232},{16,240},{24,248},{32,64},{40,72},{48,80},{56,88},... | collective-permute-start | bytes 589832 | tf_op jit(solution)/shard_map/ppermute | solution.py:113
  97.3 3.6 %collective-permute-done.18 = bf16[2,192,256]{2,1,0:T(8,128)(2,1)S(1)} collective-permute-done((bf16[2,192,256]{2,1,0:T(8,128)(2,1)S(1)}, bf16[2,192,256]{2,1,0:T(8,128)(2,1)S(1)}, u32[]{:S(2)}, u32[]{:S(2)}) %collective-permute-start.18) | collective-permute-done | bytes 196640 | tf_op jit(solution)/shard_map/ppermute | solution.py:113
  101.0 1.3 collective-permute-start.19
  102.3 0.1 collective-permute-start.12
  102.4 0.6 collective-permute-done.13
  103.1 3.8 %collective-permute-done.19 = bf16[2,192,256]{2,1,0:T(8,128)(2,1)S(1)} collective-permute-done((bf16[2,192,256]{2,1,0:T(8,128)(2,1)S(1)}, bf16[2,192,256]{2,1,0:T(8,128)(2,1)S(1)}, u32[]{:S(2)}, u32[]{:S(2)}) %collective-permute-start.19) | collective-permute-done | bytes 196640 | tf_op jit(solution)/shard_map/ppermute | solution.py:113
  106.8 0.9 convert_add_fusion
  107.7 1.5 %collective-permute-start.14 = (bf16[2,192,256]{2,1,0:T(8,128)(2,1)}, bf16[2,192,256]{2,1,0:T(8,128)(2,1)}, u32[]{:S(2)}, u32[]{:S(2)}) collective-permute-start(bf16[2,192,256]{2,1,0:T(8,128)(2,1)} %get-tuple-element.8), channel_id=1, source_target_pairs={{0,32},{8,40},{16,48},{24,56},{32,0},{40,8},{48,16},{56,24},{64,96... | collective-permute-start | bytes 589832 | tf_op jit(solution)/shard_map/ppermute | solution.py:113
  109.2 0.8 add_convert_fusion
  110.1 5.7 %all-to-all-start.1 = ((bf16[8,24,1024]{2,1,0:T(8,128)(2,1)}), bf16[8,24,1024]{2,1,0:T(8,128)(2,1)S(1)}, u32[]{:S(2)}, u32[]{:S(2)}) async-start(bf16[8,24,1024]{2,1,0:T(8,128)(2,1)} %bitcast.77), calls=%async_computation.1 | async-start | bytes 786432 | tf_op jit(solution)/shard_map/all_to_all | solution.py:166
  115.8 1.0 add_convert_fusion.3
  116.8 0.1 collective-permute-start.15
  116.9 0.9 fusion.9
  117.9 3.3 %collective-permute-start.20 = (bf16[192,256]{1,0:T(8,128)(2,1)S(1)}, bf16[192,256]{1,0:T(8,128)(2,1)S(1)}, u32[]{:S(2)}, u32[]{:S(2)}) collective-permute-start(bf16[192,256]{1,0:T(8,128)(2,1)S(1)} %fusion.9), channel_id=1, source_target_pairs={{0,224},{8,232},{16,240},{24,248},{32,64},{40,72},{48,80},{56,88},... | collective-permute-start | bytes 294920 | tf_op jit(solution)/shard_map/ppermute | solution.py:113
  121.2 2.6 %collective-permute-done.15 = bf16[2,192,256]{2,1,0:T(8,128)(2,1)S(1)} collective-permute-done((bf16[2,192,256]{2,1,0:T(8,128)(2,1)S(1)}, bf16[2,192,256]{2,1,0:T(8,128)(2,1)S(1)}, u32[]{:S(2)}, u32[]{:S(2)}) %collective-permute-start.15) | collective-permute-done | bytes 196640 | tf_op jit(solution)/shard_map/ppermute | solution.py:113
  123.9 2.7 %collective-permute-start.16 = (bf16[192,256]{1,0:T(8,128)(2,1)S(1)}, bf16[192,256]{1,0:T(8,128)(2,1)S(1)}, u32[]{:S(2)}, u32[]{:S(2)}) collective-permute-start(bf16[192,256]{1,0:T(8,128)(2,1)S(1)} %fusion.8), channel_id=1, source_target_pairs={{0,32},{8,40},{16,48},{24,56},{32,0},{40,8},{48,16},{56,24},{64,96... | collective-permute-start | bytes 294920 | tf_op jit(solution)/shard_map/ppermute | solution.py:113
  126.6 2.6 %collective-permute-done.16 = bf16[192,256]{1,0:T(8,128)(2,1)S(1)} collective-permute-done((bf16[192,256]{1,0:T(8,128)(2,1)S(1)}, bf16[192,256]{1,0:T(8,128)(2,1)S(1)}, u32[]{:S(2)}, u32[]{:S(2)}) %collective-permute-start.16) | collective-permute-done | bytes 98336 | tf_op jit(solution)/shard_map/ppermute | solution.py:113
  129.2 0.9 collective-permute-start.21
  130.1 0.8 copy.30
  130.9 4.5 %collective-permute-done.21 = bf16[2,96,256]{2,1,0:T(8,128)(2,1)S(1)} collective-permute-done((bf16[2,96,256]{2,1,0:T(8,128)(2,1)S(1)}, bf16[2,96,256]{2,1,0:T(8,128)(2,1)S(1)}, u32[]{:S(2)}, u32[]{:S(2)}) %collective-permute-start.21) | collective-permute-done | bytes 98336 | tf_op jit(solution)/shard_map/ppermute | solution.py:113
  135.5 0.6 fusion.13
  (60 shorter events, 0.7 us)
Async XLA Ops:
  0.6 13.2 %copy-start = (s32[64]{0:T(128)S(1)}, s32[64]{0:T(128)}, u32[]{:S(2)}) copy-start(s32[64]{0:T(128)} %param.15) | copy-start | bytes 772
  0.6 11.7 %copy-start.7 = (bf16[192,1024]{1,0:T(8,128)(2,1)S(1)}, bf16[192,1024]{1,0:T(8,128)(2,1)}, u32[]{:S(2)}) copy-start(bf16[192,1024]{1,0:T(8,128)(2,1)} %qo_ref.1) | copy-start | bytes 1179652
  0.7 12.9 %copy-start.9 = (f32[8,192]{1,0:T(8,128)S(1)}, f32[8,192]{1,0:T(8,128)}, u32[]{:S(2)}) copy-start(f32[8,192]{1,0:T(8,128)} %param.13) | copy-start | bytes 18436
  2.3 12.8 %collective-permute-start = (bf16[192,256]{1,0:T(8,128)(2,1)S(1)}, bf16[192,256]{1,0:T(8,128)(2,1)S(1)}, u32[]{:S(2)}, u32[]{:S(2)}) collective-permute-start(bf16[192,256]{1,0:T(8,128)(2,1)S(1)} %constant_dynamic-update-slice_fusion), channel_id=1, source_target_pairs={{0,16},{8,24},{16,0},{24,8},{32,48},{40,56},{48,32},{56,40},{64,80... | collective-permute-start | bytes 294920 | tf_op jit(solution)/shard_map/ppermute | solution.py:113
  6.3 21.3 %copy-start.6 = (bf16[192,1024]{1,0:T(8,128)(2,1)S(1)}, bf16[192,1024]{1,0:T(8,128)(2,1)}, u32[]{:S(2)}) copy-start(bf16[192,1024]{1,0:T(8,128)(2,1)} %param.12) | copy-start | bytes 1179652
  6.3 21.3 %all-to-all-start = ((bf16[24,8,1024]{2,0,1:T(8,128)(2,1)}), bf16[24,8,1024]{2,0,1:T(8,128)(2,1)S(1)}, u32[]{:S(2)}, u32[]{:S(2)}) async-start(bf16[24,8,1024]{2,0,1:T(8,128)(2,1)} %bitcast.65), calls=%async_computation | async-start | bytes 786432 | tf_op jit(solution)/shard_map/all_to_all | solution.py:141
  12.4 35.5 %collective-permute-start.9 = (bf16[192,1024]{1,0:T(8,128)(2,1)S(1)}, bf16[192,1024]{1,0:T(8,128)(2,1)}, u32[]{:S(2)}, u32[]{:S(2)}) collective-permute-start(bf16[192,1024]{1,0:T(8,128)(2,1)S(1)} %copy-done.7), channel_id=1, source_target_pairs={{0,8},{8,0},{16,24},{24,16},{32,40},{40,32},{48,56},{56,48},{64,72... | collective-permute-start | bytes 1179656 | tf_op jit(solution)/shard_map/ppermute | solution.py:113
  15.1 7.0 %collective-permute-start.1 = (bf16[1,192,256]{2,1,0:T(8,128)(2,1)S(1)}, bf16[1,192,256]{2,1,0:T(8,128)(2,1)S(1)}, u32[]{:S(2)}, u32[]{:S(2)}) collective-permute-start(bf16[1,192,256]{2,1,0:T(8,128)(2,1)S(1)} %bitcast.81), channel_id=1, source_target_pairs={{0,32},{8,40},{16,48},{24,56},{32,0},{40,8},{48,16},{56,24},{64,96... | collective-permute-start | bytes 294920 | tf_op jit(solution)/shard_map/ppermute | solution.py:113
  17.1 9.8 %collective-permute-start.5 = (bf16[1,192,256]{2,1,0:T(8,128)(2,1)S(1)}, bf16[1,192,256]{2,1,0:T(8,128)(2,1)S(1)}, u32[]{:S(2)}, u32[]{:S(2)}) collective-permute-start(bf16[1,192,256]{2,1,0:T(8,128)(2,1)S(1)} %bitcast.78), channel_id=1, source_target_pairs={{0,224},{8,232},{16,240},{24,248},{32,64},{40,72},{48,80},{56,88},... | collective-permute-start | bytes 294920 | tf_op jit(solution)/shard_map/ppermute | solution.py:113
  22.8 9.2 %collective-permute-start.2 = (bf16[2,192,256]{2,1,0:T(8,128)(2,1)}, bf16[2,192,256]{2,1,0:T(8,128)(2,1)}, u32[]{:S(2)}, u32[]{:S(2)}) collective-permute-start(bf16[2,192,256]{2,1,0:T(8,128)(2,1)} %pad_maximum_fusion.1), channel_id=1, source_target_pairs={{0,224},{8,232},{16,240},{24,248},{32,64},{40,72},{48,80},{56,88},... | collective-permute-start | bytes 589832 | tf_op jit(solution)/shard_map/ppermute | solution.py:113
  27.6 6.6 %collective-permute-start.6 = (bf16[2,192,256]{2,1,0:T(8,128)(2,1)}, bf16[2,192,256]{2,1,0:T(8,128)(2,1)}, u32[]{:S(2)}, u32[]{:S(2)}) collective-permute-start(bf16[2,192,256]{2,1,0:T(8,128)(2,1)} %pad_maximum_fusion.2), channel_id=1, source_target_pairs={{0,32},{8,40},{16,48},{24,56},{32,0},{40,8},{48,16},{56,24},{64,96... | collective-permute-start | bytes 589832 | tf_op jit(solution)/shard_map/ppermute | solution.py:113
  27.6 0.9 copy-start.2
  28.4 1.3 collective-permute-start.11
  28.5 19.4 %collective-permute-start.10 = (bf16[192,1024]{1,0:T(8,128)(2,1)S(1)}, bf16[192,1024]{1,0:T(8,128)(2,1)S(1)}, u32[]{:S(2)}, u32[]{:S(2)}) collective-permute-start(bf16[192,1024]{1,0:T(8,128)(2,1)S(1)} %bitcast.69), channel_id=1, source_target_pairs={{0,8},{8,0},{16,24},{24,16},{32,40},{40,32},{48,56},{56,48},{64,72... | collective-permute-start | bytes 1179656 | tf_op jit(solution)/shard_map/ppermute | solution.py:113
  32.0 6.3 %collective-permute-start.3 = (bf16[2,192,256]{2,1,0:T(8,128)(2,1)}, bf16[2,192,256]{2,1,0:T(8,128)(2,1)S(1)}, u32[]{:S(2)}, u32[]{:S(2)}) collective-permute-start(bf16[2,192,256]{2,1,0:T(8,128)(2,1)} %collective-permute-done.2), channel_id=1, source_target_pairs={{0,32},{8,40},{16,48},{24,56},{32,0},{40,8},{48,16},{56,24},{64,96... | collective-permute-start | bytes 589832 | tf_op jit(solution)/shard_map/ppermute | solution.py:113
  34.2 8.0 %collective-permute-start.7 = (bf16[2,192,256]{2,1,0:T(8,128)(2,1)}, bf16[2,192,256]{2,1,0:T(8,128)(2,1)S(1)}, u32[]{:S(2)}, u32[]{:S(2)}) collective-permute-start(bf16[2,192,256]{2,1,0:T(8,128)(2,1)} %collective-permute-done.6), channel_id=1, source_target_pairs={{0,224},{8,232},{16,240},{24,248},{32,64},{40,72},{48,80},{56,88},... | collective-permute-start | bytes 589832 | tf_op jit(solution)/shard_map/ppermute | solution.py:113
  38.2 7.3 %collective-permute-start.4 = (bf16[2,192,256]{2,1,0:T(8,128)(2,1)S(1)}, bf16[2,192,256]{2,1,0:T(8,128)(2,1)S(1)}, u32[]{:S(2)}, u32[]{:S(2)}) collective-permute-start(bf16[2,192,256]{2,1,0:T(8,128)(2,1)S(1)} %collective-permute-done.3), channel_id=1, source_target_pairs={{0,224},{8,232},{16,240},{24,248},{32,64},{40,72},{48,80},{56,88},... | collective-permute-start | bytes 589832 | tf_op jit(solution)/shard_map/ppermute | solution.py:113
  42.2 5.7 %collective-permute-start.8 = (bf16[2,192,256]{2,1,0:T(8,128)(2,1)S(1)}, bf16[2,192,256]{2,1,0:T(8,128)(2,1)S(1)}, u32[]{:S(2)}, u32[]{:S(2)}) collective-permute-start(bf16[2,192,256]{2,1,0:T(8,128)(2,1)S(1)} %collective-permute-done.7), channel_id=1, source_target_pairs={{0,32},{8,40},{16,48},{24,56},{32,0},{40,8},{48,16},{56,24},{64,96... | collective-permute-start | bytes 589832 | tf_op jit(solution)/shard_map/ppermute | solution.py:113
  47.9 1.1 copy-start.3
  47.9 1.2 copy-start.8
  85.9 8.0 %copy-start.1 = (f32[16,192,256]{2,1,0:T(8,128)S(1)}, f32[16,192,256]{2,1,0:T(8,128)}, u32[]{:S(2)}) copy-start(f32[16,192,256]{2,1,0:T(8,128)} %get-tuple-element.6) | copy-start | bytes 9437188
  88.1 14.2 %copy-start.5 = (f32[384,1024]{1,0:T(8,128)S(1)}, f32[384,1024]{1,0:T(8,128)}, u32[]{:S(2)}) copy-start(f32[384,1024]{1,0:T(8,128)} %get-tuple-element.5) | copy-start | bytes 4718596
  88.2 5.8 %collective-permute-start.17 = (bf16[2,192,256]{2,1,0:T(8,128)(2,1)S(1)}, bf16[2,192,256]{2,1,0:T(8,128)(2,1)S(1)}, u32[]{:S(2)}, u32[]{:S(2)}) collective-permute-start(bf16[2,192,256]{2,1,0:T(8,128)(2,1)S(1)} %get-tuple-element.9), channel_id=1, source_target_pairs={{0,32},{8,40},{16,48},{24,56},{32,0},{40,8},{48,16},{56,24},{64,96... | collective-permute-start | bytes 589832 | tf_op jit(solution)/shard_map/ppermute | solution.py:113
  94.0 7.0 %collective-permute-start.18 = (bf16[2,192,256]{2,1,0:T(8,128)(2,1)S(1)}, bf16[2,192,256]{2,1,0:T(8,128)(2,1)S(1)}, u32[]{:S(2)}, u32[]{:S(2)}) collective-permute-start(bf16[2,192,256]{2,1,0:T(8,128)(2,1)S(1)} %add_convert_fusion.2), channel_id=1, source_target_pairs={{0,224},{8,232},{16,240},{24,248},{32,64},{40,72},{48,80},{56,88},... | collective-permute-start | bytes 589832 | tf_op jit(solution)/shard_map/ppermute | solution.py:113
  94.1 9.0 %collective-permute-start.13 = (bf16[2,192,256]{2,1,0:T(8,128)(2,1)S(1)}, bf16[2,192,256]{2,1,0:T(8,128)(2,1)S(1)}, u32[]{:S(2)}, u32[]{:S(2)}) collective-permute-start(bf16[2,192,256]{2,1,0:T(8,128)(2,1)S(1)} %get-tuple-element.10), channel_id=1, source_target_pairs={{0,224},{8,232},{16,240},{24,248},{32,64},{40,72},{48,80},{56,88},... | collective-permute-start | bytes 589832 | tf_op jit(solution)/shard_map/ppermute | solution.py:113
  101.0 5.8 %collective-permute-start.19 = (bf16[2,192,256]{2,1,0:T(8,128)(2,1)S(1)}, bf16[2,192,256]{2,1,0:T(8,128)(2,1)S(1)}, u32[]{:S(2)}, u32[]{:S(2)}) collective-permute-start(bf16[2,192,256]{2,1,0:T(8,128)(2,1)S(1)} %add_convert_fusion.1), channel_id=1, source_target_pairs={{0,32},{8,40},{16,48},{24,56},{32,0},{40,8},{48,16},{56,24},{64,96... | collective-permute-start | bytes 589832 | tf_op jit(solution)/shard_map/ppermute | solution.py:113
  102.3 6.9 %collective-permute-start.12 = (bf16[192,1024]{1,0:T(8,128)(2,1)S(1)}, bf16[192,1024]{1,0:T(8,128)(2,1)S(1)}, u32[]{:S(2)}, u32[]{:S(2)}) collective-permute-start(bf16[192,1024]{1,0:T(8,128)(2,1)S(1)} %slice.161), channel_id=1, source_target_pairs={{0,8},{8,0},{16,24},{24,16},{32,40},{40,32},{48,56},{56,48},{64,72... | collective-permute-start | bytes 1179656 | tf_op jit(solution)/shard_map/ppermute | solution.py:113
  107.7 8.1 %collective-permute-start.14 = (bf16[2,192,256]{2,1,0:T(8,128)(2,1)}, bf16[2,192,256]{2,1,0:T(8,128)(2,1)}, u32[]{:S(2)}, u32[]{:S(2)}) collective-permute-start(bf16[2,192,256]{2,1,0:T(8,128)(2,1)} %get-tuple-element.8), channel_id=1, source_target_pairs={{0,32},{8,40},{16,48},{24,56},{32,0},{40,8},{48,16},{56,24},{64,96... | collective-permute-start | bytes 589832 | tf_op jit(solution)/shard_map/ppermute | solution.py:113
  110.1 20.1 %all-to-all-start.1 = ((bf16[8,24,1024]{2,1,0:T(8,128)(2,1)}), bf16[8,24,1024]{2,1,0:T(8,128)(2,1)S(1)}, u32[]{:S(2)}, u32[]{:S(2)}) async-start(bf16[8,24,1024]{2,1,0:T(8,128)(2,1)} %bitcast.77), calls=%async_computation.1 | async-start | bytes 786432 | tf_op jit(solution)/shard_map/all_to_all | solution.py:166
  115.8 10.8 %copy-start.4 = (f32[2,192,256]{2,1,0:T(8,128)S(1)}, f32[2,192,256]{2,1,0:T(8,128)}, u32[]{:S(2)}) copy-start(f32[2,192,256]{2,1,0:T(8,128)} %get-tuple-element.7) | copy-start | bytes 1179652
  116.8 7.0 %collective-permute-start.15 = (bf16[2,192,256]{2,1,0:T(8,128)(2,1)S(1)}, bf16[2,192,256]{2,1,0:T(8,128)(2,1)S(1)}, u32[]{:S(2)}, u32[]{:S(2)}) collective-permute-start(bf16[2,192,256]{2,1,0:T(8,128)(2,1)S(1)} %add_convert_fusion.3), channel_id=1, source_target_pairs={{0,224},{8,232},{16,240},{24,248},{32,64},{40,72},{48,80},{56,88},... | collective-permute-start | bytes 589832 | tf_op jit(solution)/shard_map/ppermute | solution.py:113
  117.9 8.7 %collective-permute-start.20 = (bf16[192,256]{1,0:T(8,128)(2,1)S(1)}, bf16[192,256]{1,0:T(8,128)(2,1)S(1)}, u32[]{:S(2)}, u32[]{:S(2)}) collective-permute-start(bf16[192,256]{1,0:T(8,128)(2,1)S(1)} %fusion.9), channel_id=1, source_target_pairs={{0,224},{8,232},{16,240},{24,248},{32,64},{40,72},{48,80},{56,88},... | collective-permute-start | bytes 294920 | tf_op jit(solution)/shard_map/ppermute | solution.py:113
  123.9 5.3 %collective-permute-start.16 = (bf16[192,256]{1,0:T(8,128)(2,1)S(1)}, bf16[192,256]{1,0:T(8,128)(2,1)S(1)}, u32[]{:S(2)}, u32[]{:S(2)}) collective-permute-start(bf16[192,256]{1,0:T(8,128)(2,1)S(1)} %fusion.8), channel_id=1, source_target_pairs={{0,32},{8,40},{16,48},{24,56},{32,0},{40,8},{48,16},{56,24},{64,96... | collective-permute-start | bytes 294920 | tf_op jit(solution)/shard_map/ppermute | solution.py:113
  129.2 6.2 %collective-permute-start.21 = (bf16[2,96,256]{2,1,0:T(8,128)(2,1)S(1)}, bf16[2,96,256]{2,1,0:T(8,128)(2,1)S(1)}, u32[]{:S(2)}, u32[]{:S(2)}) collective-permute-start(bf16[2,96,256]{2,1,0:T(8,128)(2,1)S(1)} %fusion.10), channel_id=1, source_target_pairs={{0,16},{8,24},{16,0},{24,8},{32,48},{40,56},{48,32},{56,40},{64,80... | collective-permute-start | bytes 294920 | tf_op jit(solution)/shard_map/ppermute | solution.py:113

commit v2 on v0

v2 whole, which is shorter than its diff:
```python
import jax
import jax.numpy as jnp
import numpy as np
from jax import lax
from jax.experimental import pallas as pl
from jax.experimental.pallas import tpu as pltpu
from jax.sharding import Mesh
from jax.sharding import PartitionSpec as P

HD = 128
G = 8
SP = 96
ROWS = 192
W = G * SP
KB = 2 * SP
NB = 8
LOG2E = 1.4426950408889634
SC = HD**-0.5
NT = (((1,), (1,)), ((), ()))


def unit(k, v, kt, q, do, lse, delta, kpos, qpos):
    st = lax.dot_general(k, q, NT, preferred_element_type=jnp.float32)
    p = jnp.exp2(st * (SC * LOG2E) - lse)
    if kpos is not None:
        p = jnp.where(qpos >= kpos, p, 0.0)
    dp = lax.dot_general(v, do, NT, preferred_element_type=jnp.float32)
    ds = (p * (dp - delta)).astype(jnp.bfloat16)
    pb = p.astype(jnp.bfloat16)
    dv = jnp.dot(pb, do, preferred_element_type=jnp.float32)
    dk = jnp.dot(ds, q, preferred_element_type=jnp.float32)
    dqt = jnp.dot(kt, ds, preferred_element_type=jnp.float32)
    return dk, dv, dqt


NS = 16
COUNTS = (1, 1, 2, 2, 2)


def kernel(info, a0, a1, a2, a3, a4, q0, q1, q2, q3, d_own, d_mate, lse, delta,
           g0, g1, g2, g3, g4, dq_own, dq_mate, qs, dos, kk, vv, kt, dka, dva, dqt):
    x_hi = info[8]
    for rel, q_src in enumerate((q0, q1, q2, q3)):
        d_src = d_own if rel < 2 else d_mate
        x_abs = x_hi if rel % 2 == 0 else 1 - x_hi
        for s in range(2):
            for h in range(G):
                dst = pl.ds((rel * 2 + s) * W + h * SP, SP)
                qs[dst, :] = q_src[s * SP:(s + 1) * SP, h * HD:(h + 1) * HD]
                dos[dst, :] = d_src[x_abs, s * SP:(s + 1) * SP, h * HD:(h + 1) * HD]

    def spans(refs):
        i = 0
        for ref, n in zip(refs, COUNTS):
            for b in range(n):
                for s in range(2):
                    place = pl.ds(pl.multiple_of(info[9 + NS + i] * SP, SP), SP)
                    yield place, ref, b, slice(s * SP, (s + 1) * SP)
                    i += 1

    for place, ref, b, rows in spans((a0, a1, a2, a3, a4)):
        kk[place, :] = ref[b, rows, :HD]
        vv[place, :] = ref[b, rows, HD:]
    for j in range(NS // 4):
        cols = slice(j * 4 * SP, (j + 1) * 4 * SP)
        kt[:, cols] = kk[cols].astype(jnp.float32).T.astype(jnp.bfloat16)
    dka[...] = jnp.zeros_like(dka)
    dva[...] = jnp.zeros_like(dva)

    def row_span(s, carry):
        span = info[s]
        count = info[9 + 2 * NS + s]
        row = pl.multiple_of(s * W, W)
        dqt[s] = jnp.zeros((HD, W), jnp.float32)

        def work(start, n, masked):
            k0, k1 = start * SP, (start + n) * SP
            kpos = qpos = None
            if masked:
                ki = lax.broadcasted_iota(jnp.int32, (n * SP, 1), 0)
                kpos = ki + info[9 + start] * SP
                for j in range(1, n):
                    kpos = jnp.where(ki >= j * SP, ki + (info[9 + start + j] - j) * SP, kpos)
                qpos = lax.broadcasted_iota(jnp.int32, (1, W), 1) % SP + span * SP
            dk, dv, dq = unit(kk[k0:k1], vv[k0:k1], kt[:, k0:k1], qs[pl.ds(row, W), :], dos[pl.ds(row, W), :],
                              lse[s], delta[s], kpos, qpos)
            dka[k0:k1] += dk
            dva[k0:k1] += dv
            dqt[s] += dq

        for b in range(NS // 4):
            start = 4 * b
            full = info[9 + start + 3] < span

            @pl.when(full)
            def _():
                work(start, 4, False)

            @pl.when((count >= start + 3) & jnp.logical_not(full))
            def _():
                work(start, 4, True)

            @pl.when((count >= start + 1) & (count < start + 3))
            def _():
                work(start, 2, True)

        return carry

    lax.fori_loop(0, 8, row_span, 0)
    for place, ref, b, rows in spans((g0, g1, g2, g3, g4)):
        ref[b, rows, :HD] = (dka[place, :] * SC).astype(ref.dtype)
        ref[b, rows, HD:] = dva[place, :].astype(ref.dtype)
    for rel in range(4):
        x_abs = x_hi if rel % 2 == 0 else 1 - x_hi
        for s in range(2):
            t = dqt[rel * 2 + s].T * SC
            for h in range(G):
                o = t[h * SP:(h + 1) * SP, :]
                if rel < 2:
                    dq_own[x_abs, s * SP:(s + 1) * SP, h * HD:(h + 1) * HD] = o
                else:
                    dq_mate[x_abs, s * SP:(s + 1) * SP, h * HD:(h + 1) * HD] = o.astype(jnp.bfloat16)


def attend(info, keys, qs, d_own, d_mate, lse, delta):
    vm = pl.BlockSpec(memory_space=pltpu.VMEM)
    f32 = jnp.float32
    bf16 = jnp.bfloat16
    out_shape = [jax.ShapeDtypeStruct((n, ROWS, 2 * HD), bf16 if i == 4 else f32) for i, n in enumerate(COUNTS)]
    out_shape += [jax.ShapeDtypeStruct((2, ROWS, G * HD), f32), jax.ShapeDtypeStruct((2, ROWS, G * HD), bf16)]
    scratch = [
        pltpu.VMEM((8 * W, HD), bf16),
        pltpu.VMEM((8 * W, HD), bf16),
        pltpu.VMEM((NS * SP, HD), bf16),
        pltpu.VMEM((NS * SP, HD), bf16),
        pltpu.VMEM((HD, NS * SP), bf16),
        pltpu.VMEM((NS * SP, HD), f32),
        pltpu.VMEM((NS * SP, HD), f32),
        pltpu.VMEM((8, HD, W), f32),
    ]
    return pl.pallas_call(
        kernel,
        out_shape=out_shape,
        in_specs=[pl.BlockSpec(memory_space=pltpu.SMEM)] + [vm] * 13,
        out_specs=[vm] * len(out_shape),
        scratch_shapes=scratch,
        compiler_params=pltpu.CompilerParams(vmem_limit_bytes=48 * 2**20),
        cost_estimate=pl.CostEstimate(flops=16 * 10**9, bytes_accessed=10**7, transcendentals=5 * 10**6),
    )(info, *keys, *qs, d_own, d_mate, lse, delta)


SWAP = [(0, 1), (1, 0)]
EVEN = [(z, z ^ 1) for z in range(8)]
ODD = [(z, (z + 1) % 8 if z % 2 else (z - 1) % 8) for z in range(8)]


def arrival():
    f, g = dict(EVEN), dict(ODD)
    a0 = [[z] for z in range(8)]
    a1 = [a0[f[z]] for z in range(8)]
    a2 = [a0[g[z]] + a1[g[z]] for z in range(8)]
    a3 = [a2[f[z]] for z in range(8)]
    a4 = [a3[g[z]] for z in range(8)]
    return np.array([a0[z] + a1[z] + a2[z] + a3[z] + a4[z] for z in range(8)], np.int32)


ORDER = arrival()


def mate(x):
    return lax.ppermute(x, "core", SWAP)


def across(x):
    return lax.ppermute(x, "x", SWAP)


def along(x, route):
    return lax.ppermute(x, "z", route)


def exchange(x, axes):
    return lax.all_to_all(x, axes, split_axis=0, concat_axis=0, tiled=True)


def table(span_order, row_slots, key_slots, x_hi):
    rows, keys = span_order[row_slots], span_order[key_slots]
    rank = jnp.sum(keys[None, :] < keys[:, None], axis=1)
    hot = rank[None, :] == jnp.arange(NS)[:, None]
    ordered = jnp.sum(jnp.where(hot, keys[None, :], 0), axis=1)
    count = jnp.sum(keys[None, :] <= rows[:, None], axis=1)
    return jnp.concatenate([rows, x_hi[None], ordered, rank, count]).astype(jnp.int32)


def per_device(query_rows, key_rows, value_rows, attn_output, log_norms, grad_output, span_order):
    z, x_hi, core = lax.axis_index("z"), lax.axis_index("x"), lax.axis_index("core")
    f32 = jnp.float32
    bf16 = jnp.bfloat16
    twice = jnp.broadcast_to(grad_output.reshape(1, 24, G, 1024).transpose(0, 2, 1, 3), (2, G, 24, 1024))
    grad_rows = exchange(twice.reshape(16, 24, 1024), ("x", "head")).reshape(2, ROWS, 1024)
    a0 = jnp.concatenate([key_rows, value_rows], axis=1)[None]
    a1 = along(a0, EVEN)
    a2 = along(jnp.concatenate([a0, a1]), ODD)
    a3 = along(a2, EVEN)
    a4 = along(a3, ODD)
    q_x = across(query_rows)
    q_m = mate(query_rows)
    q_mx = mate(q_x)
    mine = lax.dynamic_index_in_dim(grad_rows, x_hi, 0, keepdims=False)
    prod = mine.astype(f32) * attn_output.astype(f32)
    delta = jnp.sum(prod.reshape(ROWS, G, HD), axis=-1)

    def share(t):
        t = jnp.concatenate([t, across(t)])
        return jnp.concatenate([t, mate(t)])

    lse = share((log_norms * LOG2E).reshape(G, 2, SP).transpose(1, 0, 2).reshape(2, 1, W))
    delta = share(delta.reshape(2, SP, G).transpose(0, 2, 1).reshape(2, 1, W))
    grad_mate = mate(grad_rows)
    base = lambda zz, xx, cc: ((zz * 2 + xx) * 2 + cc) * 2
    row_slots = jnp.stack([base(z, xx, cc) + s for cc in (core, 1 - core) for xx in (x_hi, 1 - x_hi) for s in (0, 1)])
    key_slots = base(jnp.asarray(ORDER)[z], x_hi, core)
    key_slots = jnp.stack([key_slots, key_slots + 1], axis=1).reshape(-1)
    info = table(span_order, row_slots, key_slots, x_hi)
    g0, g1, g2, g3, g4, dq_own, dq_mate = attend(
        info, (a0, a1, a2, a3, a4), (query_rows, q_x, q_m, q_mx), grad_rows, grad_mate, lse, delta)
    dq = (dq_own + mate(dq_mate)).astype(bf16).reshape(16, 24, 1024)
    dq = exchange(dq, ("x", "head")).reshape(2, G, 24, 1024)
    t3 = (g3 + along(g4, ODD)).astype(bf16)
    t2 = (g2 + along(t3, EVEN)).astype(bf16)
    r = along(t2, ODD)
    t1 = (g1 + r[1:]).astype(bf16)
    fin = (g0 + r[:1] + along(t1, EVEN)).astype(bf16)[0]
    dq = (dq[0].astype(f32) + dq[1].astype(f32)).astype(bf16)
    grad_query = dq.transpose(1, 0, 2).reshape(24, G * 1024)
    return (grad_query, fin[:, :HD], fin[:, HD:])


def solution(mesh):
    fine = Mesh(mesh.devices.reshape(8, 2, 2, 8), ("z", "x", "core", "head"))
    ctx = ("z", "x", "core")
    return jax.shard_map(
        per_device,
        mesh=fine,
        in_specs=(
            P(ctx, "head"),
            P(ctx, "head"),
            P(ctx, "head"),
            P(ctx, "head"),
            P("head", ctx),
            P(ctx + ("head",), None),
            P(),
        ),
        out_specs=(P(ctx + ("head",), None), P(ctx, "head"), P(ctx, "head")),
        check_vma=False,
    )
```

time: 617 us -> 114 us (0.18); the launches traced: 606 us -> 114 us
  matrix products: 239 us -> 0 us
  local copies, waits for them, and re-layouts: 119 us -> 12.7 us
  waiting for transfers between devices: 113 us -> 27.8 us
  starting transfers between devices: 125 us -> 45.1 us
  Pallas kernels: 0 us -> 18.6 us
    dot_general x160 -> x0, matrix products: 239 us -> none  [the longest x32 60.1 us: attend_block(): jnp.einsum('tngs,tngd->snd', dscores, query_heads, preferred_element_type...]
    ppermute x126 -> x17, starting transfers between devices: 114 us -> 24.1 us  [the longest x8 13.8 us: along(): return lax.ppermute(x, 'z', route)]
    ppermute x126 -> x17, waiting for transfers between devices: 107 us -> 17.7 us  [the longest x8 14.2 us: along(): return lax.ppermute(x, 'z', route)]
    while x62 -> x0, local copies, waits for them, and re-layouts: 87.8 us -> none
    another operation x31 -> x2, local copies, waits for them, and re-layouts: 20.2 us -> 0.19 us  [the longest x1 0.1 us: per_device(): jnp.stack([base(z, xx, cc) + s for cc in (core, 1 - core) for xx in (x_hi...]
    pallas_call x0 -> x1, Pallas kernels: none -> 18.6 us  [attend(): pl.pallas_call(kernel, out_shape=out_shape, in_specs=[pl.BlockSpec(memory...]
    all_to_all x2, starting transfers between devices: 11.1 us -> 21 us  [exchange(): return lax.all_to_all(x, axes, split_axis=0, concat_axis=0, tiled=True)]
  transfers between devices with their start and end apart: 128 -> 19, of which waited for: 63 -> 8; matrix products, arithmetic and copies ran while one was open for 51% -> 17% of each run, Pallas kernels for 0% -> 0%
where the time goes in v2:
time: 114 us
  starting transfers between devices  45.1 us (40%)
  waiting for transfers between devices  27.8 us (24%)
  Pallas kernels  18.6 us (16%)
  local copies, waits for them, and re-layouts  12.7 us (11%)
  other arithmetic  9.2 us (8%)
    all_to_all x2, starting transfers between devices, exchange(): return lax.all_to_all(x, axes, split_axis=0, concat_axis=0, tiled=True)  21 us
    pallas_call x1, Pallas kernels, attend(): pl.pallas_call(kernel, out_shape=out_shape, in_specs=[pl.BlockSpec(memory...  18.6 us
    ppermute x8, waiting for transfers between devices, along(): return lax.ppermute(x, 'z', route)  14.2 us
    ppermute x8, starting transfers between devices, along(): return lax.ppermute(x, 'z', route)  13.8 us
    all_to_all x2, waiting for transfers between devices, exchange(): return lax.all_to_all(x, axes, split_axis=0, concat_axis=0, tiled=True)  10.1 us
    ppermute x3, starting transfers between devices, across(): return lax.ppermute(x, 'x', SWAP)  5.14 us
    ppermute x6, starting transfers between devices, mate(): return lax.ppermute(x, 'core', SWAP)  5.11 us
    unnamed x14, local copies, waits for them, and re-layouts  4.02 us
  transfers between devices with their start and end apart: 19, of which 8 were waited for; matrix products, arithmetic and copies ran while one was open for 17% of the time, Pallas kernels for 0%

profile of v2, /device:TPU:2, one launch (start us, length us, event | category | flops | bytes accessed | tf_op | source)
XLA Modules:
  0.0 114.3 jit_solution(2242985081438916043)
XLA Ops:
  0.6 0.0 copy-start
  0.6 2.2 %collective-permute-start.4 = (bf16[192,1024]{1,0:T(8,128)(2,1)}, bf16[192,1024]{1,0:T(8,128)(2,1)S(1)}, u32[]{:S(2)}, u32[]{:S(2)}) collective-permute-start(bf16[192,1024]{1,0:T(8,128)(2,1)} %q0.1), channel_id=1, source_target_pairs={{0,16},{16,0},{1,17},{17,1},{2,18},{18,2},{3,19},{19,3},{4,20},{20... | collective-permute-start | bytes 1179656 | tf_op jit(solution)/shard_map/ppermute | solution.py:175
  2.9 0.0 collective-permute-start.5
  2.9 0.7 broadcast_multiply_fusion
  3.6 0.1 reshape.432
  3.6 0.1 reshape.433
  3.7 1.5 %collective-permute-start.8 = (f32[2,1,768]{2,1,0:T(1,128)S(1)}, f32[2,1,768]{2,1,0:T(1,128)}, u32[]{:S(2)}, u32[]{:S(2)}) collective-permute-start(f32[2,1,768]{2,1,0:T(1,128)S(1)} %reshape.433), channel_id=1, source_target_pairs={{0,16},{16,0},{1,17},{17,1},{2,18},{18,2},{3,19},{19,3},{4,20},{20... | collective-permute-start | bytes 18440 | tf_op jit(solution)/shard_map/ppermute | solution.py:175
  5.2 0.8 maximum_bitcast_fusion.a0
  6.0 2.0 %collective-permute-start = (bf16[1,192,256]{2,1,0:T(8,128)(2,1)S(1)}, bf16[1,192,256]{2,1,0:T(8,128)(2,1)S(1)}, u32[]{:S(2)}, u32[]{:S(2)}) collective-permute-start(bf16[1,192,256]{2,1,0:T(8,128)(2,1)S(1)} %maximum_bitcast_fusion.a0), channel_id=1, source_target_pairs={{0,32},{32,0},{64,96},{96,64},{128,160},{160,128},{192,224},{224,1... | collective-permute-start | bytes 294920 | tf_op jit(solution)/shard_map/ppermute | solution.py:179
  8.0 1.2 %copy.34 = bf16[3,8,8,1024]{3,2,1,0:T(8,128)(2,1)S(1)} copy(bf16[3,8,8,1024]{3,1,2,0:T(8,128)(2,1)} %bitcast.52) | data formatting | bytes 786432
  9.3 0.2 copy.27
  9.5 1.0 broadcast_in_dim.36
  10.5 7.6 %all-to-all-start = ((bf16[16,24,1024]{2,1,0:T(8,128)(2,1)}), bf16[16,24,1024]{2,1,0:T(8,128)(2,1)S(1)}, u32[]{:S(2)}, u32[]{:S(2)}) async-start(bf16[16,24,1024]{2,1,0:T(8,128)(2,1)} %bitcast.15), calls=%async_computation | async-start | bytes 1572864 | tf_op jit(solution)/shard_map/all_to_all | solution.py:183
  18.1 0.7 broadcast_add_fusion
  18.8 0.1 copy.26
  18.9 0.1 reshape.428
  19.0 0.7 gather_fusion.1
  19.7 0.1 stack.40
  19.8 0.2 convert_reduce_fusion
  20.0 0.6 gather_fusion
  20.7 5.0 %collective-permute-start.1 = (bf16[2,192,256]{2,1,0:T(8,128)(2,1)S(1)}, bf16[2,192,256]{2,1,0:T(8,128)(2,1)S(1)}, u32[]{:S(2)}, u32[]{:S(2)}) collective-permute-start(bf16[2,192,256]{2,1,0:T(8,128)(2,1)S(1)} %pad_maximum_fusion), channel_id=1, source_target_pairs={{0,224},{32,64},{64,32},{96,128},{128,96},{160,192},{192,160},{224... | collective-permute-start | bytes 589832 | tf_op jit(solution)/shard_map/ppermute | solution.py:179
  25.7 0.2 convert_reduce_fusion.1
  25.9 5.3 %all-to-all-done = bf16[16,24,1024]{2,1,0:T(8,128)(2,1)S(1)} async-done(((bf16[16,24,1024]{2,1,0:T(8,128)(2,1)}), bf16[16,24,1024]{2,1,0:T(8,128)(2,1)S(1)}, u32[]{:S(2)}, u32[]{:S(2)}) %all-to-all-start) | async-done | bytes 786464 | tf_op jit(solution)/shard_map/all_to_all | solution.py:183
  31.2 0.0 collective-permute-start.7
  31.2 0.1 select_reduce_fusion
  31.3 0.1 concatenate.42.info
  31.4 0.4 collective-permute-start.2
  31.8 0.0 collective-permute-done.4.q1
  31.8 0.3 collective-permute-start.6
  32.1 0.1 fusion
  32.2 0.0 copy-start.1
  32.2 1.0 copy.35
  33.2 2.1 %reduce_sum.39 = f32[192,8]{1,0:T(8,128)} reduce(f32[192,8,128]{2,1,0:T(8,128)} %bitcast.50, f32[]{:T(128)} %constant.39.clone.1), dimensions={2}, to_apply=%region_3.4 | reduce | flops 195072 | bytes 792580 | tf_op jit(solution)/shard_map/reduce_sum | solution.py:211
  35.3 1.6 %copy.32 = f32[2,96,8]{1,0,2:T(2,128)} copy(f32[2,96,8]{2,1,0:T(8,128)} %bitcast.54) | data formatting | bytes 12288 | tf_op jit(solution)/shard_map/reshape | solution.py:218
  36.9 1.3 %copy.30 = f32[2,8,96]{2,1,0:T(8,128)} copy(f32[2,8,96]{2,0,1:T(2,128)} %bitcast.56) | data formatting | bytes 12288 | tf_op jit(solution)/shard_map/transpose | solution.py:218
  38.2 1.4 %reshape.436 = f32[2,1,768]{2,1,0:T(1,128)} reshape(f32[2,8,96]{2,1,0:T(8,128)} %copy.30) | data formatting | bytes 12288 | tf_op jit(solution)/shard_map/reshape | solution.py:218
  39.5 0.0 collective-permute-done.8
  39.5 1.5 %collective-permute-start.10 = (f32[2,1,768]{2,1,0:T(1,128)}, f32[2,1,768]{2,1,0:T(1,128)S(1)}, u32[]{:S(2)}, u32[]{:S(2)}) collective-permute-start(f32[2,1,768]{2,1,0:T(1,128)} %reshape.436), channel_id=1, source_target_pairs={{0,16},{16,0},{1,17},{17,1},{2,18},{18,2},{3,19},{19,3},{4,20},{20... | collective-permute-start | bytes 18440 | tf_op jit(solution)/shard_map/ppermute | solution.py:175
  41.0 0.7 pad_maximum_fusion.3
  41.7 0.1 collective-permute-start.9
  41.8 3.1 %collective-permute-done.10 = f32[2,1,768]{2,1,0:T(1,128)S(1)} collective-permute-done((f32[2,1,768]{2,1,0:T(1,128)}, f32[2,1,768]{2,1,0:T(1,128)S(1)}, u32[]{:S(2)}, u32[]{:S(2)}) %collective-permute-start.10) | collective-permute-done | bytes 6176 | tf_op jit(solution)/shard_map/ppermute | solution.py:175
  44.9 5.6 %collective-permute-start.3 = (bf16[2,192,256]{2,1,0:T(8,128)(2,1)}, bf16[2,192,256]{2,1,0:T(8,128)(2,1)S(1)}, u32[]{:S(2)}, u32[]{:S(2)}) collective-permute-start(bf16[2,192,256]{2,1,0:T(8,128)(2,1)} %collective-permute-done.2.a3), channel_id=1, source_target_pairs={{0,224},{32,64},{64,32},{96,128},{128,96},{160,192},{192,160},{224... | collective-permute-start | bytes 589832 | tf_op jit(solution)/shard_map/ppermute | solution.py:179
  50.4 0.7 pad_maximum_fusion.4
  51.2 0.3 collective-permute-start.11
  51.4 0.7 pad_maximum_fusion.1.lse
  52.2 0.4 collective-permute-done.11
  52.6 0.7 pad_maximum_fusion.2.delta
  53.3 1.5 %collective-permute-done.3.a4 = bf16[2,192,256]{2,1,0:T(8,128)(2,1)S(1)} collective-permute-done((bf16[2,192,256]{2,1,0:T(8,128)(2,1)}, bf16[2,192,256]{2,1,0:T(8,128)(2,1)S(1)}, u32[]{:S(2)}, u32[]{:S(2)}) %collective-permute-start.3) | collective-permute-done | bytes 196640 | tf_op jit(solution)/shard_map/ppermute | solution.py:179
  54.9 0.7 copy-done.2
  55.6 1.0 copy-done.3
  56.6 18.6 %shard_map.103 = (f32[1,192,256]{2,1,0:T(8,128)S(1)}, f32[1,192,256]{2,1,0:T(8,128)S(1)}, f32[2,192,256]{2,1,0:T(8,128)S(1)}, f32[2,192,256]{2,1,0:T(8,128)S(1)}...) custom-call(s32[49]{0:T(128)S(1)} %concatenate.42.info, ...), custom_call_target="tpu_custom_call" | custom-call | flops 16000000000 | bytes 10000000 | tf_op jit(solution)/shard_map/pallas_call | solution.py:141
  75.2 4.5 %collective-permute-start.12 = (bf16[2,192,1024]{2,1,0:T(8,128)(2,1)S(1)}, bf16[2,192,1024]{2,1,0:T(8,128)(2,1)S(1)}, u32[]{:S(2)}, u32[]{:S(2)}) collective-permute-start(bf16[2,192,1024]{2,1,0:T(8,128)(2,1)S(1)} %get-tuple-element.11), channel_id=1, source_target_pairs={{0,8},{8,0},{1,9},{9,1},{2,10},{10,2},{3,11},{11,3},{4,12},{12,4},... | collective-permute-start | bytes 2359304 | tf_op jit(solution)/shard_map/ppermute | solution.py:171
  79.7 2.4 %collective-permute-done.13 = bf16[2,192,256]{2,1,0:T(8,128)(2,1)S(1)} collective-permute-done((bf16[2,192,256]{2,1,0:T(8,128)(2,1)S(1)}, bf16[2,192,256]{2,1,0:T(8,128)(2,1)S(1)}, u32[]{:S(2)}, u32[]{:S(2)}) %collective-permute-start.13) | collective-permute-done | bytes 196640 | tf_op jit(solution)/shard_map/ppermute | solution.py:179
  82.2 0.1 collective-permute-start.14
  82.3 5.7 %collective-permute-done.14 = bf16[2,192,256]{2,1,0:T(8,128)(2,1)S(1)} collective-permute-done((bf16[2,192,256]{2,1,0:T(8,128)(2,1)S(1)}, bf16[2,192,256]{2,1,0:T(8,128)(2,1)S(1)}, u32[]{:S(2)}, u32[]{:S(2)}) %collective-permute-start.14) | collective-permute-done | bytes 196640 | tf_op jit(solution)/shard_map/ppermute | solution.py:179
  88.0 0.6 collective-permute-start.15
  88.6 1.2 %add_convert_fusion = bf16[2,192,1024]{2,1,0:T(8,128)(2,1)} fusion(f32[2,192,1024]{2,1,0:T(8,128)S(1)} %copy-done.4, bf16[2,192,1024]{2,1,0:T(8,128)(2,1)S(1)} %collective-permute-done.12), kind=kLoop, calls=%fused_computation.2 | loop fusion | flops 1179648 | bytes 3145728 | tf_op jit(solution)/shard_map/convert_element_type | solution.py:227
  89.8 13.4 %all-to-all-start.1 = ((bf16[16,24,1024]{2,1,0:T(8,128)(2,1)}), bf16[16,24,1024]{2,1,0:T(8,128)(2,1)S(1)}, u32[]{:S(2)}, u32[]{:S(2)}) async-start(bf16[16,24,1024]{2,1,0:T(8,128)(2,1)} %bitcast.21), calls=%async_computation.1 | async-start | bytes 1572864 | tf_op jit(solution)/shard_map/all_to_all | solution.py:183
  103.2 0.1 collective-permute-start.16
  103.3 4.6 %collective-permute-done.16 = bf16[1,192,256]{2,1,0:T(8,128)(2,1)S(1)} collective-permute-done((bf16[1,192,256]{2,1,0:T(8,128)(2,1)S(1)}, bf16[1,192,256]{2,1,0:T(8,128)(2,1)S(1)}, u32[]{:S(2)}, u32[]{:S(2)}) %collective-permute-start.16) | collective-permute-done | bytes 98336 | tf_op jit(solution)/shard_map/ppermute | solution.py:179
  108.0 0.6 fusion.5
  108.6 4.8 %all-to-all-done.1 = bf16[16,24,1024]{2,1,0:T(8,128)(2,1)S(1)} async-done(((bf16[16,24,1024]{2,1,0:T(8,128)(2,1)}), bf16[16,24,1024]{2,1,0:T(8,128)(2,1)S(1)}, u32[]{:S(2)}, u32[]{:S(2)}) %all-to-all-start.1) | async-done | bytes 786464 | tf_op jit(solution)/shard_map/all_to_all | solution.py:183
  113.4 0.1 fusion.1
  113.5 0.8 copy.33
  (30 shorter events, 0.3 us)
Async XLA Ops:
  0.6 18.4 %copy-start = (s32[64]{0:T(128)S(1)}, s32[64]{0:T(128)}, u32[]{:S(2)}) copy-start(s32[64]{0:T(128)} %param.14) | copy-start | bytes 772
  0.6 31.2 %collective-permute-start.4 = (bf16[192,1024]{1,0:T(8,128)(2,1)}, bf16[192,1024]{1,0:T(8,128)(2,1)S(1)}, u32[]{:S(2)}, u32[]{:S(2)}) collective-permute-start(bf16[192,1024]{1,0:T(8,128)(2,1)} %q0.1), channel_id=1, source_target_pairs={{0,16},{16,0},{1,17},{17,1},{2,18},{18,2},{3,19},{19,3},{4,20},{20... | collective-permute-start | bytes 1179656 | tf_op jit(solution)/shard_map/ppermute | solution.py:175
  2.9 50.5 %collective-permute-start.5 = (bf16[192,1024]{1,0:T(8,128)(2,1)}, bf16[192,1024]{1,0:T(8,128)(2,1)S(1)}, u32[]{:S(2)}, u32[]{:S(2)}) collective-permute-start(bf16[192,1024]{1,0:T(8,128)(2,1)} %q0.1), channel_id=1, source_target_pairs={{0,8},{8,0},{1,9},{9,1},{2,10},{10,2},{3,11},{11,3},{4,12},{12,4},... | collective-permute-start | bytes 1179656 | tf_op jit(solution)/shard_map/ppermute | solution.py:171
  3.7 35.8 %collective-permute-start.8 = (f32[2,1,768]{2,1,0:T(1,128)S(1)}, f32[2,1,768]{2,1,0:T(1,128)}, u32[]{:S(2)}, u32[]{:S(2)}) collective-permute-start(f32[2,1,768]{2,1,0:T(1,128)S(1)} %reshape.433), channel_id=1, source_target_pairs={{0,16},{16,0},{1,17},{17,1},{2,18},{18,2},{3,19},{19,3},{4,20},{20... | collective-permute-start | bytes 18440 | tf_op jit(solution)/shard_map/ppermute | solution.py:175
  6.0 14.6 %collective-permute-start = (bf16[1,192,256]{2,1,0:T(8,128)(2,1)S(1)}, bf16[1,192,256]{2,1,0:T(8,128)(2,1)S(1)}, u32[]{:S(2)}, u32[]{:S(2)}) collective-permute-start(bf16[1,192,256]{2,1,0:T(8,128)(2,1)S(1)} %maximum_bitcast_fusion.a0), channel_id=1, source_target_pairs={{0,32},{32,0},{64,96},{96,64},{128,160},{160,128},{192,224},{224,1... | collective-permute-start | bytes 294920 | tf_op jit(solution)/shard_map/ppermute | solution.py:179
  10.5 21.6 %copy-start.5 = (bf16[192,1024]{1,0:T(8,128)(2,1)S(1)}, bf16[192,1024]{1,0:T(8,128)(2,1)}, u32[]{:S(2)}) copy-start(bf16[192,1024]{1,0:T(8,128)(2,1)} %param.11) | copy-start | bytes 1179652
  10.5 20.7 %all-to-all-start = ((bf16[16,24,1024]{2,1,0:T(8,128)(2,1)}), bf16[16,24,1024]{2,1,0:T(8,128)(2,1)S(1)}, u32[]{:S(2)}, u32[]{:S(2)}) async-start(bf16[16,24,1024]{2,1,0:T(8,128)(2,1)} %bitcast.15), calls=%async_computation | async-start | bytes 1572864 | tf_op jit(solution)/shard_map/all_to_all | solution.py:183
  20.7 10.7 %collective-permute-start.1 = (bf16[2,192,256]{2,1,0:T(8,128)(2,1)S(1)}, bf16[2,192,256]{2,1,0:T(8,128)(2,1)S(1)}, u32[]{:S(2)}, u32[]{:S(2)}) collective-permute-start(bf16[2,192,256]{2,1,0:T(8,128)(2,1)S(1)} %pad_maximum_fusion), channel_id=1, source_target_pairs={{0,224},{32,64},{64,32},{96,128},{128,96},{160,192},{192,160},{224... | collective-permute-start | bytes 589832 | tf_op jit(solution)/shard_map/ppermute | solution.py:179
  31.2 24.4 %collective-permute-start.7 = (bf16[2,192,1024]{2,1,0:T(8,128)(2,1)S(1)}, bf16[2,192,1024]{2,1,0:T(8,128)(2,1)S(1)}, u32[]{:S(2)}, u32[]{:S(2)}) collective-permute-start(bf16[2,192,1024]{2,1,0:T(8,128)(2,1)S(1)} %bitcast.47), channel_id=1, source_target_pairs={{0,8},{8,0},{1,9},{9,1},{2,10},{10,2},{3,11},{11,3},{4,12},{12,4},... | collective-permute-start | bytes 2359304 | tf_op jit(solution)/shard_map/ppermute | solution.py:171
  31.4 10.3 %collective-permute-start.2 = (bf16[2,192,256]{2,1,0:T(8,128)(2,1)S(1)}, bf16[2,192,256]{2,1,0:T(8,128)(2,1)}, u32[]{:S(2)}, u32[]{:S(2)}) collective-permute-start(bf16[2,192,256]{2,1,0:T(8,128)(2,1)S(1)} %collective-permute-done.1.a2), channel_id=1, source_target_pairs={{0,32},{32,0},{64,96},{96,64},{128,160},{160,128},{192,224},{224,1... | collective-permute-start | bytes 589832 | tf_op jit(solution)/shard_map/ppermute | solution.py:179
  31.8 23.1 %collective-permute-start.6 = (bf16[192,1024]{1,0:T(8,128)(2,1)S(1)}, bf16[192,1024]{1,0:T(8,128)(2,1)S(1)}, u32[]{:S(2)}, u32[]{:S(2)}) collective-permute-start(bf16[192,1024]{1,0:T(8,128)(2,1)S(1)} %collective-permute-done.4.q1), channel_id=1, source_target_pairs={{0,8},{8,0},{1,9},{9,1},{2,10},{10,2},{3,11},{11,3},{4,12},{12,4},... | collective-permute-start | bytes 1179656 | tf_op jit(solution)/shard_map/ppermute | solution.py:171
  32.2 23.4 %copy-start.1 = (bf16[192,1024]{1,0:T(8,128)(2,1)S(1)}, bf16[192,1024]{1,0:T(8,128)(2,1)}, u32[]{:S(2)}) copy-start(bf16[192,1024]{1,0:T(8,128)(2,1)} %q0.1) | copy-start | bytes 1179652
  39.5 5.3 %collective-permute-start.10 = (f32[2,1,768]{2,1,0:T(1,128)}, f32[2,1,768]{2,1,0:T(1,128)S(1)}, u32[]{:S(2)}, u32[]{:S(2)}) collective-permute-start(f32[2,1,768]{2,1,0:T(1,128)} %reshape.436), channel_id=1, source_target_pairs={{0,16},{16,0},{1,17},{17,1},{2,18},{18,2},{3,19},{19,3},{4,20},{20... | collective-permute-start | bytes 18440 | tf_op jit(solution)/shard_map/ppermute | solution.py:175
  41.7 9.4 %collective-permute-start.9 = (f32[4,1,768]{2,1,0:T(1,128)S(1)}, f32[4,1,768]{2,1,0:T(1,128)S(1)}, u32[]{:S(2)}, u32[]{:S(2)}) collective-permute-start(f32[4,1,768]{2,1,0:T(1,128)S(1)} %pad_maximum_fusion.3), channel_id=1, source_target_pairs={{0,8},{8,0},{1,9},{9,1},{2,10},{10,2},{3,11},{11,3},{4,12},{12,4},... | collective-permute-start | bytes 36872 | tf_op jit(solution)/shard_map/ppermute | solution.py:171
  44.9 10.0 %collective-permute-start.3 = (bf16[2,192,256]{2,1,0:T(8,128)(2,1)}, bf16[2,192,256]{2,1,0:T(8,128)(2,1)S(1)}, u32[]{:S(2)}, u32[]{:S(2)}) collective-permute-start(bf16[2,192,256]{2,1,0:T(8,128)(2,1)} %collective-permute-done.2.a3), channel_id=1, source_target_pairs={{0,224},{32,64},{64,32},{96,128},{128,96},{160,192},{192,160},{224... | collective-permute-start | bytes 589832 | tf_op jit(solution)/shard_map/ppermute | solution.py:179
  51.2 1.4 %collective-permute-start.11 = (f32[4,1,768]{2,1,0:T(1,128)S(1)}, f32[4,1,768]{2,1,0:T(1,128)S(1)}, u32[]{:S(2)}, u32[]{:S(2)}) collective-permute-start(f32[4,1,768]{2,1,0:T(1,128)S(1)} %pad_maximum_fusion.4), channel_id=1, source_target_pairs={{0,8},{8,0},{1,9},{9,1},{2,10},{10,2},{3,11},{11,3},{4,12},{12,4},... | collective-permute-start | bytes 36872 | tf_op jit(solution)/shard_map/ppermute | solution.py:171
  54.9 0.7 copy-start.2
  55.6 1.0 copy-start.3
  75.2 13.4 %copy-start.4 = (f32[2,192,1024]{2,1,0:T(8,128)S(1)}, f32[2,192,1024]{2,1,0:T(8,128)}, u32[]{:S(2)}) copy-start(f32[2,192,1024]{2,1,0:T(8,128)} %get-tuple-element.10) | copy-start | bytes 4718596
  75.2 6.9 %collective-permute-start.13 = (bf16[2,192,256]{2,1,0:T(8,128)(2,1)S(1)}, bf16[2,192,256]{2,1,0:T(8,128)(2,1)S(1)}, u32[]{:S(2)}, u32[]{:S(2)}) collective-permute-start(bf16[2,192,256]{2,1,0:T(8,128)(2,1)S(1)} %get-tuple-element.15), channel_id=1, source_target_pairs={{0,224},{32,64},{64,32},{96,128},{128,96},{160,192},{192,160},{224... | collective-permute-start | bytes 589832 | tf_op jit(solution)/shard_map/ppermute | solution.py:179
  75.2 13.4 %collective-permute-start.12 = (bf16[2,192,1024]{2,1,0:T(8,128)(2,1)S(1)}, bf16[2,192,1024]{2,1,0:T(8,128)(2,1)S(1)}, u32[]{:S(2)}, u32[]{:S(2)}) collective-permute-start(bf16[2,192,1024]{2,1,0:T(8,128)(2,1)S(1)} %get-tuple-element.11), channel_id=1, source_target_pairs={{0,8},{8,0},{1,9},{9,1},{2,10},{10,2},{3,11},{11,3},{4,12},{12,4},... | collective-permute-start | bytes 2359304 | tf_op jit(solution)/shard_map/ppermute | solution.py:171
  82.2 5.8 %collective-permute-start.14 = (bf16[2,192,256]{2,1,0:T(8,128)(2,1)S(1)}, bf16[2,192,256]{2,1,0:T(8,128)(2,1)S(1)}, u32[]{:S(2)}, u32[]{:S(2)}) collective-permute-start(bf16[2,192,256]{2,1,0:T(8,128)(2,1)S(1)} %add_convert_fusion.3), channel_id=1, source_target_pairs={{0,32},{32,0},{64,96},{96,64},{128,160},{160,128},{192,224},{224,1... | collective-permute-start | bytes 589832 | tf_op jit(solution)/shard_map/ppermute | solution.py:179
  88.0 15.2 %collective-permute-start.15 = (bf16[2,192,256]{2,1,0:T(8,128)(2,1)S(1)}, bf16[2,192,256]{2,1,0:T(8,128)(2,1)S(1)}, u32[]{:S(2)}, u32[]{:S(2)}) collective-permute-start(bf16[2,192,256]{2,1,0:T(8,128)(2,1)S(1)} %add_convert_fusion.2), channel_id=1, source_target_pairs={{0,224},{32,64},{64,32},{96,128},{128,96},{160,192},{192,160},{224... | collective-permute-start | bytes 589832 | tf_op jit(solution)/shard_map/ppermute | solution.py:179
  89.8 23.6 %all-to-all-start.1 = ((bf16[16,24,1024]{2,1,0:T(8,128)(2,1)}), bf16[16,24,1024]{2,1,0:T(8,128)(2,1)S(1)}, u32[]{:S(2)}, u32[]{:S(2)}) async-start(bf16[16,24,1024]{2,1,0:T(8,128)(2,1)} %bitcast.21), calls=%async_computation.1 | async-start | bytes 1572864 | tf_op jit(solution)/shard_map/all_to_all | solution.py:183
  103.2 4.7 %collective-permute-start.16 = (bf16[1,192,256]{2,1,0:T(8,128)(2,1)S(1)}, bf16[1,192,256]{2,1,0:T(8,128)(2,1)S(1)}, u32[]{:S(2)}, u32[]{:S(2)}) collective-permute-start(bf16[1,192,256]{2,1,0:T(8,128)(2,1)S(1)} %add_convert_fusion.5), channel_id=1, source_target_pairs={{0,32},{32,0},{64,96},{96,64},{128,160},{160,128},{192,224},{224,1... | collective-permute-start | bytes 294920 | tf_op jit(solution)/shard_map/ppermute | solution.py:179

commit v3 on v2

--- a/solution.py
+++ b/solution.py
@@ -37,9 +37,12 @@
 COUNTS = (1, 1, 2, 2, 2)
 
 
-def kernel(info, a0, a1, a2, a3, a4, q0, q1, q2, q3, d_own, d_mate, lse, delta,
-           g0, g1, g2, g3, g4, dq_own, dq_mate, qs, dos, kk, vv, kt, dka, dva, dqt):
+def kernel(info, a0, a1, a2, a3, a4, q0, q1, q2, q3, d_own, d_mate,
+           st0, st1, st2, st3, g0, g1, g2, g3, g4, dq_own, dq_mate, qs, dos, kk, vv, kt, dka, dva, dqt, lse, delta):
     x_hi = info[8]
+    for rel, st in enumerate((st0, st1, st2, st3)):
+        lse[2 * rel:2 * rel + 2] = st[0]
+        delta[2 * rel:2 * rel + 2] = st[1]
     for rel, q_src in enumerate((q0, q1, q2, q3)):
         d_src = d_own if rel < 2 else d_mate
         x_abs = x_hi if rel % 2 == 0 else 1 - x_hi
@@ -122,7 +125,7 @@
                     dq_mate[x_abs, s * SP:(s + 1) * SP, h * HD:(h + 1) * HD] = o.astype(jnp.bfloat16)
 
 
-def attend(info, keys, qs, d_own, d_mate, lse, delta):
+def attend(info, keys, qs, d_own, d_mate, stats):
     vm = pl.BlockSpec(memory_space=pltpu.VMEM)
     f32 = jnp.float32
     bf16 = jnp.bfloat16
@@ -137,16 +140,43 @@
         pltpu.VMEM((NS * SP, HD), f32),
         pltpu.VMEM((NS * SP, HD), f32),
         pltpu.VMEM((8, HD, W), f32),
+        pltpu.VMEM((8, 1, W), f32),
+        pltpu.VMEM((8, 1, W), f32),
     ]
     return pl.pallas_call(
         kernel,
         out_shape=out_shape,
-        in_specs=[pl.BlockSpec(memory_space=pltpu.SMEM)] + [vm] * 13,
+        in_specs=[pl.BlockSpec(memory_space=pltpu.SMEM)] + [vm] * 15,
         out_specs=[vm] * len(out_shape),
         scratch_shapes=scratch,
-        compiler_params=pltpu.CompilerParams(vmem_limit_bytes=48 * 2**20),
+        compiler_params=pltpu.CompilerParams(vmem_limit_bytes=24 * 2**20),
         cost_estimate=pl.CostEstimate(flops=16 * 10**9, bytes_accessed=10**7, transcendentals=5 * 10**6),
-    )(info, *keys, *qs, d_own, d_mate, lse, delta)
+    )(info, *keys, *qs, d_own, d_mate, *stats)
+
+
+def prepare(grad, keys, values, out, a0):
+    for x in range(2):
+        for h in range(G):
+            out[x * G + h] = grad[:, h * 1024:(h + 1) * 1024]
+    a0[0, :, :HD] = keys[...]
+    a0[0, :, HD:] = values[...]
+
+
+def row_stats(x_hi, grad, attn, lse, out, prod):
+    bf16 = jnp.bfloat16
+    for s in range(2):
+        rows = slice(s * SP, (s + 1) * SP)
+        for h in range(G):
+            cols = slice(h * HD, (h + 1) * HD)
+            prod[h * SP:(h + 1) * SP] = grad[x_hi[0], rows, cols].astype(jnp.float32) * attn[rows, cols].astype(jnp.float32)
+        full = prod[...]
+        high = full.astype(bf16)
+        low = (full - high.astype(jnp.float32)).astype(bf16)
+        ones = jnp.ones((8, HD), bf16)
+        sums = lax.dot_general(ones, high, NT, preferred_element_type=jnp.float32)
+        sums += lax.dot_general(ones, low, NT, preferred_element_type=jnp.float32)
+        out[1, s] = sums[:1]
+        out[0, s] = lse[s]
 
 
 SWAP = [(0, 1), (1, 0)]
@@ -196,40 +226,51 @@
     z, x_hi, core = lax.axis_index("z"), lax.axis_index("x"), lax.axis_index("core")
     f32 = jnp.float32
     bf16 = jnp.bfloat16
-    twice = jnp.broadcast_to(grad_output.reshape(1, 24, G, 1024).transpose(0, 2, 1, 3), (2, G, 24, 1024))
-    grad_rows = exchange(twice.reshape(16, 24, 1024), ("x", "head")).reshape(2, ROWS, 1024)
-    a0 = jnp.concatenate([key_rows, value_rows], axis=1)[None]
-    a1 = along(a0, EVEN)
-    a2 = along(jnp.concatenate([a0, a1]), ODD)
-    a3 = along(a2, EVEN)
-    a4 = along(a3, ODD)
-    q_x = across(query_rows)
-    q_m = mate(query_rows)
-    q_mx = mate(q_x)
-    mine = lax.dynamic_index_in_dim(grad_rows, x_hi, 0, keepdims=False)
-    prod = mine.astype(f32) * attn_output.astype(f32)
-    delta = jnp.sum(prod.reshape(ROWS, G, HD), axis=-1)
-
-    def share(t):
-        t = jnp.concatenate([t, across(t)])
-        return jnp.concatenate([t, mate(t)])
-
-    lse = share((log_norms * LOG2E).reshape(G, 2, SP).transpose(1, 0, 2).reshape(2, 1, W))
-    delta = share(delta.reshape(2, SP, G).transpose(0, 2, 1).reshape(2, 1, W))
-    grad_mate = mate(grad_rows)
     base = lambda zz, xx, cc: ((zz * 2 + xx) * 2 + cc) * 2
     row_slots = jnp.stack([base(z, xx, cc) + s for cc in (core, 1 - core) for xx in (x_hi, 1 - x_hi) for s in (0, 1)])
     key_slots = base(jnp.asarray(ORDER)[z], x_hi, core)
     key_slots = jnp.stack([key_slots, key_slots + 1], axis=1).reshape(-1)
     info = table(span_order, row_slots, key_slots, x_hi)
+    vm = pl.BlockSpec(memory_space=pltpu.VMEM)
+    twice, a0 = pl.pallas_call(
+        prepare,
+        out_shape=(jax.ShapeDtypeStruct((16, 24, 1024), bf16), jax.ShapeDtypeStruct((1, ROWS, 2 * HD), bf16)),
+        in_specs=[vm] * 3,
+        out_specs=(vm, vm),
+    )(grad_output, key_rows, value_rows)
+    grad_rows = exchange(twice, ("x", "head")).reshape(2, ROWS, 1024)
+    a1 = along(a0, EVEN)
+    a2 = along(jnp.concatenate([a0, a1]), ODD)
+    lse = (log_norms * LOG2E).reshape(G, 2, SP).transpose(1, 0, 2).reshape(2, 1, W)
+    grad_rows, a2, info, lse = lax.optimization_barrier((grad_rows, a2, info, lse))
+    a3 = along(a2, EVEN)
+    q_x = across(query_rows)
+    q_m = mate(query_rows)
+    q_mx = mate(q_x)
+    stats = pl.pallas_call(
+        row_stats,
+        out_shape=jax.ShapeDtypeStruct((2, 2, 1, W), f32),
+        in_specs=[pl.BlockSpec(memory_space=pltpu.SMEM), vm, vm, vm],
+        out_specs=vm,
+        scratch_shapes=[pltpu.VMEM((W, HD), f32)],
+    )(x_hi[None].astype(jnp.int32), grad_rows, attn_output, lse)
+    stats, a3 = lax.optimization_barrier((stats, a3))
+    a4 = along(a3, ODD)
+    grad_mate = mate(grad_rows)
+    stats_x = across(stats)
+    stats_x, a4 = lax.optimization_barrier((stats_x, a4))
+    stats = (stats, stats_x, mate(stats), mate(stats_x))
     g0, g1, g2, g3, g4, dq_own, dq_mate = attend(
-        info, (a0, a1, a2, a3, a4), (query_rows, q_x, q_m, q_mx), grad_rows, grad_mate, lse, delta)
+        info, (a0, a1, a2, a3, a4), (query_rows, q_x, q_m, q_mx), grad_rows, grad_mate, stats)
+    r = along(g4, ODD)
     dq = (dq_own + mate(dq_mate)).astype(bf16).reshape(16, 24, 1024)
+    r, dq = lax.optimization_barrier((r, dq))
     dq = exchange(dq, ("x", "head")).reshape(2, G, 24, 1024)
-    t3 = (g3 + along(g4, ODD)).astype(bf16)
+    t3 = (g3 + r).astype(bf16)
     t2 = (g2 + along(t3, EVEN)).astype(bf16)
     r = along(t2, ODD)
     t1 = (g1 + r[1:]).astype(bf16)
+    t1, dq = lax.optimization_barrier((t1, dq))
     fin = (g0 + r[:1] + along(t1, EVEN)).astype(bf16)[0]
     dq = (dq[0].astype(f32) + dq[1].astype(f32)).astype(bf16)
     grad_query = dq.transpose(1, 0, 2).reshape(24, G * 1024)

time: 114 us -> 103 us (0.904); the launches traced: 114 us -> 102 us
  starting transfers between devices: 45.1 us -> 36.5 us
  other arithmetic: 9.2 us -> 2.7 us
  local copies, waits for them, and re-layouts: 12.7 us -> 6.33 us
  Pallas kernels: 18.6 us -> 24.3 us
  waiting for transfers between devices: 27.8 us -> 31.2 us
    all_to_all x2, starting transfers between devices: 21 us -> 14.1 us  [exchange(): return lax.all_to_all(x, axes, split_axis=0, concat_axis=0, tiled=True)]
    ppermute x8, waiting for transfers between devices: 14.2 us -> 19 us  [along(): return lax.ppermute(x, 'z', route)]
    all_to_all x2, waiting for transfers between devices: 10.1 us -> 5.52 us  [exchange(): return lax.all_to_all(x, axes, split_axis=0, concat_axis=0, tiled=True)]
    pallas_call x0 -> x2, Pallas kernels: none -> 4.2 us  [the longest x1 2.22 us: per_device(): pl.pallas_call(row_stats, out_shape=jax.ShapeDtypeStruct((2, 2, 1, W), f3...]
    ppermute x6, starting transfers between devices: 5.11 us -> 1.3 us  [mate(): return lax.ppermute(x, 'core', SWAP)]
    reshape x3 -> x0, local copies, waits for them, and re-layouts: 3.7 us -> none  [the longest x2 2.93 us: per_device(): delta = share(delta.reshape(2, SP, G).transpose(0, 2, 1).reshape(2, 1, W))]
    ppermute x8, starting transfers between devices: 13.8 us -> 17.1 us  [along(): return lax.ppermute(x, 'z', route)]
    concatenate x4 -> x0, other arithmetic: 2.84 us -> none  [the longest x2 1.43 us: share(): return jnp.concatenate([t, mate(t)])]
  transfers between devices with their start and end apart: 19 -> 18, of which waited for: 8 -> 9; matrix products, arithmetic and copies ran while one was open for 17% -> 6% of each run, Pallas kernels for 0% -> 4%
where the time goes in v3:
time: 103 us; the launch traced here: 102 us
  starting transfers between devices  36.5 us (35%)
  waiting for transfers between devices  31.2 us (30%)
  Pallas kernels  24.3 us (24%)
  local copies, waits for them, and re-layouts  6.33 us (6%)
  other arithmetic  2.7 us (3%)
    pallas_call x1, Pallas kernels, attend(): pl.pallas_call(kernel, out_shape=out_shape, in_specs=[pl.BlockSpec(memory...  20.1 us
    ppermute x8, waiting for transfers between devices, along(): return lax.ppermute(x, 'z', route)  19 us
    ppermute x8, starting transfers between devices, along(): return lax.ppermute(x, 'z', route)  17.1 us
    all_to_all x2, starting transfers between devices, exchange(): return lax.all_to_all(x, axes, split_axis=0, concat_axis=0, tiled=True)  14.1 us
    all_to_all x2, waiting for transfers between devices, exchange(): return lax.all_to_all(x, axes, split_axis=0, concat_axis=0, tiled=True)  5.52 us
    ppermute x2, starting transfers between devices, across(): return lax.ppermute(x, 'x', SWAP)  3.95 us
    ppermute x2, waiting for transfers between devices, across(): return lax.ppermute(x, 'x', SWAP)  3.68 us
    ppermute x6, waiting for transfers between devices, mate(): return lax.ppermute(x, 'core', SWAP)  2.97 us
  transfers between devices with their start and end apart: 18, of which 9 were waited for; matrix products, arithmetic and copies ran while one was open for 6% of the time, Pallas kernels for 4%

profile of v3, /device:TPU:2, one launch (start us, length us, event | category | flops | bytes accessed | tf_op | source)
XLA Modules:
  0.0 101.7 jit_solution(3768439229402260314)
XLA Ops:
  0.6 0.0 copy-start
  0.6 0.0 copy-start.6
  0.7 2.2 %collective-permute-start.5 = (bf16[192,1024]{1,0:T(8,128)(2,1)}, bf16[192,1024]{1,0:T(8,128)(2,1)S(1)}, u32[]{:S(2)}, u32[]{:S(2)}) collective-permute-start(bf16[192,1024]{1,0:T(8,128)(2,1)} %q0.1), channel_id=1, source_target_pairs={{0,16},{16,0},{1,17},{17,1},{2,18},{18,2},{3,19},{19,3},{4,20},{20... | collective-permute-start | bytes 1179656 | tf_op jit(solution)/shard_map/ppermute | solution.py:205
  2.9 2.0 %shard_map.103 = (bf16[16,24,1024]{2,1,0:T(8,128)(2,1)}, bf16[1,192,256]{2,1,0:T(8,128)(2,1)}) custom-call(bf16[24,8192]{1,0:T(8,128)(2,1)} %grad.1, bf16[192,128]{1,0:T(8,128)(2,1)} %keys.1, bf16[192,128]{1,0:T(8,128)(2,1)} %values.1), custom_call_target="tpu_custom_call" | custom-call | tf_op jit(solution)/shard_map/pallas_call | solution.py:235
  4.9 6.6 %all-to-all-start = ((bf16[16,24,1024]{2,1,0:T(8,128)(2,1)}), bf16[16,24,1024]{2,1,0:T(8,128)(2,1)S(1)}, u32[]{:S(2)}, u32[]{:S(2)}) async-start(bf16[16,24,1024]{2,1,0:T(8,128)(2,1)} %get-tuple-element.24), calls=%async_computation | async-start | bytes 1572864 | tf_op jit(solution)/shard_map/all_to_all | solution.py:213
  11.5 0.0 copy-done.3
  11.5 2.0 %collective-permute-start = (bf16[1,192,256]{2,1,0:T(8,128)(2,1)S(1)}, bf16[1,192,256]{2,1,0:T(8,128)(2,1)S(1)}, u32[]{:S(2)}, u32[]{:S(2)}) collective-permute-start(bf16[1,192,256]{2,1,0:T(8,128)(2,1)S(1)} %copy-done.3), channel_id=1, source_target_pairs={{0,32},{32,0},{64,96},{96,64},{128,160},{160,128},{192,224},{224,1... | collective-permute-start | bytes 294920 | tf_op jit(solution)/shard_map/ppermute | solution.py:209
  13.5 0.1 stack.40
  13.6 0.7 broadcast_add_fusion
  14.3 0.1 copy.19
  14.4 0.1 reshape.414
  14.5 0.0 copy-done
  14.5 0.7 gather_fusion.1
  15.2 0.7 gather_fusion
  15.8 0.0 copy-done.6
  15.8 0.1 reshape.415
  15.9 0.7 reshape.416.lse
  16.6 0.2 convert_reduce_fusion
  16.8 0.0 collective-permute-done.a1
  16.8 5.3 %collective-permute-start.1 = (bf16[2,192,256]{2,1,0:T(8,128)(2,1)S(1)}, bf16[2,192,256]{2,1,0:T(8,128)(2,1)S(1)}, u32[]{:S(2)}, u32[]{:S(2)}) collective-permute-start(bf16[2,192,256]{2,1,0:T(8,128)(2,1)S(1)} %pad_maximum_fusion), channel_id=1, source_target_pairs={{0,224},{32,64},{64,32},{96,128},{128,96},{160,192},{192,160},{224... | collective-permute-start | bytes 589832 | tf_op jit(solution)/shard_map/ppermute | solution.py:209
  22.1 0.1 select_reduce_fusion
  22.3 0.2 convert_reduce_fusion.1
  22.4 0.1 concatenate.26.info
  22.5 3.3 %collective-permute-done.1.a2 = bf16[2,192,256]{2,1,0:T(8,128)(2,1)S(1)} collective-permute-done((bf16[2,192,256]{2,1,0:T(8,128)(2,1)S(1)}, bf16[2,192,256]{2,1,0:T(8,128)(2,1)S(1)}, u32[]{:S(2)}, u32[]{:S(2)}) %collective-permute-start.1) | collective-permute-done | bytes 196640 | tf_op jit(solution)/shard_map/ppermute | solution.py:209
  25.8 0.0 all-to-all-done
  25.8 0.0 collective-permute-start.8
  25.8 0.7 collective-permute-start.2
  26.5 0.0 copy-done.5
  26.5 0.2 collective-permute-start.6
  26.8 0.0 collective-permute-done.5.q1
  26.8 0.3 collective-permute-start.7
  27.1 2.2 %shard_map.104.st0 = f32[2,2,1,768]{3,2,1,0:T(1,128)} custom-call(s32[1]{0:T(128)} %bitcast.10.x_hi, bf16[2,192,1024]{2,1,0:T(8,128)(2,1)} %bitcast.30, bf16[192,1024]{1,0:T(8,128)(2,1)} %attn.1, f32[2,1,768]{2,1,0:T(1,128)} %reshape.416.lse), custom_call_target="tpu_custom_call" | custom-call | tf_op jit(solution)/shard_map/pallas_call | solution.py:250
  29.3 4.0 %collective-permute-done.2.a3 = bf16[2,192,256]{2,1,0:T(8,128)(2,1)} collective-permute-done((bf16[2,192,256]{2,1,0:T(8,128)(2,1)S(1)}, bf16[2,192,256]{2,1,0:T(8,128)(2,1)}, u32[]{:S(2)}, u32[]{:S(2)}) %collective-permute-start.2) | collective-permute-done | bytes 196640 | tf_op jit(solution)/shard_map/ppermute | solution.py:209
  33.2 4.7 %collective-permute-start.4 = (bf16[2,192,256]{2,1,0:T(8,128)(2,1)}, bf16[2,192,256]{2,1,0:T(8,128)(2,1)S(1)}, u32[]{:S(2)}, u32[]{:S(2)}) collective-permute-start(bf16[2,192,256]{2,1,0:T(8,128)(2,1)} %collective-permute-done.2.a3), channel_id=1, source_target_pairs={{0,224},{32,64},{64,32},{96,128},{128,96},{160,192},{192,160},{224... | collective-permute-start | bytes 589832 | tf_op jit(solution)/shard_map/ppermute | solution.py:209
  37.9 1.7 %collective-permute-start.3 = (f32[2,2,1,768]{3,2,1,0:T(1,128)}, f32[2,2,1,768]{3,2,1,0:T(1,128)S(1)}, u32[]{:S(2)}, u32[]{:S(2)}) collective-permute-start(f32[2,2,1,768]{3,2,1,0:T(1,128)} %shard_map.104.st0), channel_id=1, source_target_pairs={{0,16},{16,0},{1,17},{17,1},{2,18},{18,2},{3,19},{19,3},{4,20},{20... | collective-permute-start | bytes 36872 | tf_op jit(solution)/shard_map/ppermute | solution.py:205
  39.6 3.7 %collective-permute-done.3.st1 = f32[2,2,1,768]{3,2,1,0:T(1,128)S(1)} collective-permute-done((f32[2,2,1,768]{3,2,1,0:T(1,128)}, f32[2,2,1,768]{3,2,1,0:T(1,128)S(1)}, u32[]{:S(2)}, u32[]{:S(2)}) %collective-permute-start.3) | collective-permute-done | bytes 12320 | tf_op jit(solution)/shard_map/ppermute | solution.py:205
  43.3 0.0 collective-permute-start.9
  43.3 0.0 collective-permute-done.4.a4
  43.3 0.5 collective-permute-start.10
  43.8 0.0 collective-permute-done.6.q2
  43.8 0.0 collective-permute-done.7.q3
  43.8 0.9 collective-permute-done.9.st2
  44.7 0.0 collective-permute-done.10.st3
  44.7 0.0 collective-permute-done.8.d_mate
  44.7 1.1 %copy-done.2 = bf16[16,24,1024]{2,1,0:T(8,128)(2,1)S(1)} copy-done((bf16[16,24,1024]{2,1,0:T(8,128)(2,1)S(1)}, bf16[16,24,1024]{2,1,0:T(8,128)(2,1)}, u32[]{:S(2)}) %copy-start.2) | copy-done | bytes 786456
  45.8 0.7 copy-done.4
  46.6 20.1 %shard_map.105 = (f32[1,192,256]{2,1,0:T(8,128)S(1)}, f32[1,192,256]{2,1,0:T(8,128)S(1)}, f32[2,192,256]{2,1,0:T(8,128)S(1)}, f32[2,192,256]{2,1,0:T(8,128)S(1)}...) custom-call(s32[49]{0:T(128)S(1)} %concatenate.26.info, ...), custom_call_target="tpu_custom_call" | custom-call | flops 16000000000 | bytes 10000000 | tf_op jit(solution)/shard_map/pallas_call | solution.py:146
  66.7 0.3 collective-permute-start.12
  67.0 0.0 collective-permute-start.11
  67.0 2.1 %collective-permute-done.12 = bf16[2,192,1024]{2,1,0:T(8,128)(2,1)S(1)} collective-permute-done((bf16[2,192,1024]{2,1,0:T(8,128)(2,1)S(1)}, bf16[2,192,1024]{2,1,0:T(8,128)(2,1)S(1)}, u32[]{:S(2)}, u32[]{:S(2)}) %collective-permute-start.12) | collective-permute-done | bytes 786464 | tf_op jit(solution)/shard_map/ppermute | solution.py:201
  69.1 1.2 %add_convert_fusion = bf16[2,192,1024]{2,1,0:T(8,128)(2,1)} fusion(f32[2,192,1024]{2,1,0:T(8,128)S(1)} %get-tuple-element.38, bf16[2,192,1024]{2,1,0:T(8,128)(2,1)S(1)} %collective-permute-done.12), kind=kLoop, calls=%fused_computation.2 | loop fusion | flops 1179648 | bytes 3145728 | tf_op jit(solution)/shard_map/convert_element_type | solution.py:266
  70.2 5.1 %collective-permute-done.11 = bf16[2,192,256]{2,1,0:T(8,128)(2,1)S(1)} collective-permute-done((bf16[2,192,256]{2,1,0:T(8,128)(2,1)S(1)}, bf16[2,192,256]{2,1,0:T(8,128)(2,1)S(1)}, u32[]{:S(2)}, u32[]{:S(2)}) %collective-permute-start.11) | collective-permute-done | bytes 196640 | tf_op jit(solution)/shard_map/ppermute | solution.py:209
  75.4 0.3 collective-permute-start.13
  75.7 7.5 %all-to-all-start.1 = ((bf16[16,24,1024]{2,1,0:T(8,128)(2,1)}), bf16[16,24,1024]{2,1,0:T(8,128)(2,1)S(1)}, u32[]{:S(2)}, u32[]{:S(2)}) async-start(bf16[16,24,1024]{2,1,0:T(8,128)(2,1)} %bitcast.14), calls=%async_computation.1 | async-start | bytes 1572864 | tf_op jit(solution)/shard_map/all_to_all | solution.py:213
  83.1 0.0 collective-permute-done.13
  83.2 2.3 %collective-permute-start.14 = (bf16[2,192,256]{2,1,0:T(8,128)(2,1)S(1)}, bf16[2,192,256]{2,1,0:T(8,128)(2,1)S(1)}, u32[]{:S(2)}, u32[]{:S(2)}) collective-permute-start(bf16[2,192,256]{2,1,0:T(8,128)(2,1)S(1)} %add_convert_fusion.2), channel_id=1, source_target_pairs={{0,224},{32,64},{64,32},{96,128},{128,96},{160,192},{192,160},{224... | collective-permute-start | bytes 589832 | tf_op jit(solution)/shard_map/ppermute | solution.py:209
  85.5 4.9 %collective-permute-done.14 = bf16[2,192,256]{2,1,0:T(8,128)(2,1)S(1)} collective-permute-done((bf16[2,192,256]{2,1,0:T(8,128)(2,1)S(1)}, bf16[2,192,256]{2,1,0:T(8,128)(2,1)S(1)}, u32[]{:S(2)}, u32[]{:S(2)}) %collective-permute-start.14) | collective-permute-done | bytes 196640 | tf_op jit(solution)/shard_map/ppermute | solution.py:209
  90.4 5.5 %all-to-all-done.1 = bf16[16,24,1024]{2,1,0:T(8,128)(2,1)S(1)} async-done(((bf16[16,24,1024]{2,1,0:T(8,128)(2,1)}), bf16[16,24,1024]{2,1,0:T(8,128)(2,1)S(1)}, u32[]{:S(2)}, u32[]{:S(2)}) %all-to-all-start.1) | async-done | bytes 786464 | tf_op jit(solution)/shard_map/all_to_all | solution.py:213
  95.9 0.4 copy.21
  96.3 1.8 %collective-permute-start.15 = (bf16[1,192,256]{2,1,0:T(8,128)(2,1)S(1)}, bf16[1,192,256]{2,1,0:T(8,128)(2,1)S(1)}, u32[]{:S(2)}, u32[]{:S(2)}) collective-permute-start(bf16[1,192,256]{2,1,0:T(8,128)(2,1)S(1)} %add_convert_fusion.5), channel_id=1, source_target_pairs={{0,32},{32,0},{64,96},{96,64},{128,160},{160,128},{192,224},{224,1... | collective-permute-start | bytes 294920 | tf_op jit(solution)/shard_map/ppermute | solution.py:209
  98.2 0.1 add_convert_fusion.1
  98.3 1.0 copy.23
  99.3 1.8 %collective-permute-done.15 = bf16[1,192,256]{2,1,0:T(8,128)(2,1)S(1)} collective-permute-done((bf16[1,192,256]{2,1,0:T(8,128)(2,1)S(1)}, bf16[1,192,256]{2,1,0:T(8,128)(2,1)S(1)}, u32[]{:S(2)}, u32[]{:S(2)}) %collective-permute-start.15) | collective-permute-done | bytes 98336 | tf_op jit(solution)/shard_map/ppermute | solution.py:209
  101.1 0.6 fusion.3
  (18 shorter events, 0.2 us)
Async XLA Ops:
  0.6 13.9 %copy-start = (s32[64]{0:T(128)S(1)}, s32[64]{0:T(128)}, u32[]{:S(2)}) copy-start(s32[64]{0:T(128)} %param.14) | copy-start | bytes 772
  0.6 15.2 %copy-start.6 = (f32[8,192]{1,0:T(8,128)S(1)}, f32[8,192]{1,0:T(8,128)}, u32[]{:S(2)}) copy-start(f32[8,192]{1,0:T(8,128)} %param.12) | copy-start | bytes 18436
  0.7 26.1 %collective-permute-start.5 = (bf16[192,1024]{1,0:T(8,128)(2,1)}, bf16[192,1024]{1,0:T(8,128)(2,1)S(1)}, u32[]{:S(2)}, u32[]{:S(2)}) collective-permute-start(bf16[192,1024]{1,0:T(8,128)(2,1)} %q0.1), channel_id=1, source_target_pairs={{0,16},{16,0},{1,17},{17,1},{2,18},{18,2},{3,19},{19,3},{4,20},{20... | collective-permute-start | bytes 1179656 | tf_op jit(solution)/shard_map/ppermute | solution.py:205
  4.8 6.6 %copy-start.3 = (bf16[1,192,256]{2,1,0:T(8,128)(2,1)S(1)}, bf16[1,192,256]{2,1,0:T(8,128)(2,1)}, u32[]{:S(2)}) copy-start(bf16[1,192,256]{2,1,0:T(8,128)(2,1)} %get-tuple-element.25.a0) | copy-start | bytes 294916
  4.8 21.7 %copy-start.5 = (bf16[192,1024]{1,0:T(8,128)(2,1)S(1)}, bf16[192,1024]{1,0:T(8,128)(2,1)}, u32[]{:S(2)}) copy-start(bf16[192,1024]{1,0:T(8,128)(2,1)} %q0.1) | copy-start | bytes 1179652
  4.9 21.0 %all-to-all-start = ((bf16[16,24,1024]{2,1,0:T(8,128)(2,1)}), bf16[16,24,1024]{2,1,0:T(8,128)(2,1)S(1)}, u32[]{:S(2)}, u32[]{:S(2)}) async-start(bf16[16,24,1024]{2,1,0:T(8,128)(2,1)} %get-tuple-element.24), calls=%async_computation | async-start | bytes 1572864 | tf_op jit(solution)/shard_map/all_to_all | solution.py:213
  11.5 5.3 %collective-permute-start = (bf16[1,192,256]{2,1,0:T(8,128)(2,1)S(1)}, bf16[1,192,256]{2,1,0:T(8,128)(2,1)S(1)}, u32[]{:S(2)}, u32[]{:S(2)}) collective-permute-start(bf16[1,192,256]{2,1,0:T(8,128)(2,1)S(1)} %copy-done.3), channel_id=1, source_target_pairs={{0,32},{32,0},{64,96},{96,64},{128,160},{160,128},{192,224},{224,1... | collective-permute-start | bytes 294920 | tf_op jit(solution)/shard_map/ppermute | solution.py:209
  16.8 9.0 %collective-permute-start.1 = (bf16[2,192,256]{2,1,0:T(8,128)(2,1)S(1)}, bf16[2,192,256]{2,1,0:T(8,128)(2,1)S(1)}, u32[]{:S(2)}, u32[]{:S(2)}) collective-permute-start(bf16[2,192,256]{2,1,0:T(8,128)(2,1)S(1)} %pad_maximum_fusion), channel_id=1, source_target_pairs={{0,224},{32,64},{64,32},{96,128},{128,96},{160,192},{192,160},{224... | collective-permute-start | bytes 589832 | tf_op jit(solution)/shard_map/ppermute | solution.py:209
  25.8 1.3 %copy-start.1 = (bf16[16,24,1024]{2,1,0:T(8,128)(2,1)}, bf16[16,24,1024]{2,1,0:T(8,128)(2,1)S(1)}, u32[]{:S(2)}) copy-start(bf16[16,24,1024]{2,1,0:T(8,128)(2,1)S(1)} %all-to-all-done) | copy-start | bytes 2359300
  25.8 18.9 %collective-permute-start.8 = (bf16[2,192,1024]{2,1,0:T(8,128)(2,1)S(1)}, bf16[2,192,1024]{2,1,0:T(8,128)(2,1)S(1)}, u32[]{:S(2)}, u32[]{:S(2)}) collective-permute-start(bf16[2,192,1024]{2,1,0:T(8,128)(2,1)S(1)} %bitcast.29), channel_id=1, source_target_pairs={{0,8},{8,0},{1,9},{9,1},{2,10},{10,2},{3,11},{11,3},{4,12},{12,4},... | collective-permute-start | bytes 2359304 | tf_op jit(solution)/shard_map/ppermute | solution.py:201
  25.8 7.4 %collective-permute-start.2 = (bf16[2,192,256]{2,1,0:T(8,128)(2,1)S(1)}, bf16[2,192,256]{2,1,0:T(8,128)(2,1)}, u32[]{:S(2)}, u32[]{:S(2)}) collective-permute-start(bf16[2,192,256]{2,1,0:T(8,128)(2,1)S(1)} %collective-permute-done.1.a2), channel_id=1, source_target_pairs={{0,32},{32,0},{64,96},{96,64},{128,160},{160,128},{192,224},{224,1... | collective-permute-start | bytes 589832 | tf_op jit(solution)/shard_map/ppermute | solution.py:209
  26.5 17.3 %collective-permute-start.6 = (bf16[192,1024]{1,0:T(8,128)(2,1)S(1)}, bf16[192,1024]{1,0:T(8,128)(2,1)S(1)}, u32[]{:S(2)}, u32[]{:S(2)}) collective-permute-start(bf16[192,1024]{1,0:T(8,128)(2,1)S(1)} %copy-done.5), channel_id=1, source_target_pairs={{0,8},{8,0},{1,9},{9,1},{2,10},{10,2},{3,11},{11,3},{4,12},{12,4},... | collective-permute-start | bytes 1179656 | tf_op jit(solution)/shard_map/ppermute | solution.py:201
  26.8 17.1 %collective-permute-start.7 = (bf16[192,1024]{1,0:T(8,128)(2,1)S(1)}, bf16[192,1024]{1,0:T(8,128)(2,1)S(1)}, u32[]{:S(2)}, u32[]{:S(2)}) collective-permute-start(bf16[192,1024]{1,0:T(8,128)(2,1)S(1)} %collective-permute-done.5.q1), channel_id=1, source_target_pairs={{0,8},{8,0},{1,9},{9,1},{2,10},{10,2},{3,11},{11,3},{4,12},{12,4},... | collective-permute-start | bytes 1179656 | tf_op jit(solution)/shard_map/ppermute | solution.py:201
  33.2 10.1 %collective-permute-start.4 = (bf16[2,192,256]{2,1,0:T(8,128)(2,1)}, bf16[2,192,256]{2,1,0:T(8,128)(2,1)S(1)}, u32[]{:S(2)}, u32[]{:S(2)}) collective-permute-start(bf16[2,192,256]{2,1,0:T(8,128)(2,1)} %collective-permute-done.2.a3), channel_id=1, source_target_pairs={{0,224},{32,64},{64,32},{96,128},{128,96},{160,192},{192,160},{224... | collective-permute-start | bytes 589832 | tf_op jit(solution)/shard_map/ppermute | solution.py:209
  37.9 5.4 %collective-permute-start.3 = (f32[2,2,1,768]{3,2,1,0:T(1,128)}, f32[2,2,1,768]{3,2,1,0:T(1,128)S(1)}, u32[]{:S(2)}, u32[]{:S(2)}) collective-permute-start(f32[2,2,1,768]{3,2,1,0:T(1,128)} %shard_map.104.st0), channel_id=1, source_target_pairs={{0,16},{16,0},{1,17},{17,1},{2,18},{18,2},{3,19},{19,3},{4,20},{20... | collective-permute-start | bytes 36872 | tf_op jit(solution)/shard_map/ppermute | solution.py:205
  43.3 1.4 %collective-permute-start.9 = (f32[2,2,1,768]{3,2,1,0:T(1,128)}, f32[2,2,1,768]{3,2,1,0:T(1,128)S(1)}, u32[]{:S(2)}, u32[]{:S(2)}) collective-permute-start(f32[2,2,1,768]{3,2,1,0:T(1,128)} %shard_map.104.st0), channel_id=1, source_target_pairs={{0,8},{8,0},{1,9},{9,1},{2,10},{10,2},{3,11},{11,3},{4,12},{12,4},... | collective-permute-start | bytes 36872 | tf_op jit(solution)/shard_map/ppermute | solution.py:201
  43.3 1.4 %collective-permute-start.10 = (f32[2,2,1,768]{3,2,1,0:T(1,128)S(1)}, f32[2,2,1,768]{3,2,1,0:T(1,128)S(1)}, u32[]{:S(2)}, u32[]{:S(2)}) collective-permute-start(f32[2,2,1,768]{3,2,1,0:T(1,128)S(1)} %collective-permute-done.3.st1), channel_id=1, source_target_pairs={{0,8},{8,0},{1,9},{9,1},{2,10},{10,2},{3,11},{11,3},{4,12},{12,4},... | collective-permute-start | bytes 36872 | tf_op jit(solution)/shard_map/ppermute | solution.py:201
  44.7 1.1 %copy-start.2 = (bf16[16,24,1024]{2,1,0:T(8,128)(2,1)S(1)}, bf16[16,24,1024]{2,1,0:T(8,128)(2,1)}, u32[]{:S(2)}) copy-start(bf16[16,24,1024]{2,1,0:T(8,128)(2,1)} %copy-done.1) | copy-start | bytes 2359300
  45.8 0.7 copy-start.4
  66.7 2.4 %collective-permute-start.12 = (bf16[2,192,1024]{2,1,0:T(8,128)(2,1)S(1)}, bf16[2,192,1024]{2,1,0:T(8,128)(2,1)S(1)}, u32[]{:S(2)}, u32[]{:S(2)}) collective-permute-start(bf16[2,192,1024]{2,1,0:T(8,128)(2,1)S(1)} %get-tuple-element.39), channel_id=1, source_target_pairs={{0,8},{8,0},{1,9},{9,1},{2,10},{10,2},{3,11},{11,3},{4,12},{12,4},... | collective-permute-start | bytes 2359304 | tf_op jit(solution)/shard_map/ppermute | solution.py:201
  67.0 8.3 %collective-permute-start.11 = (bf16[2,192,256]{2,1,0:T(8,128)(2,1)S(1)}, bf16[2,192,256]{2,1,0:T(8,128)(2,1)S(1)}, u32[]{:S(2)}, u32[]{:S(2)}) collective-permute-start(bf16[2,192,256]{2,1,0:T(8,128)(2,1)S(1)} %get-tuple-element.37), channel_id=1, source_target_pairs={{0,224},{32,64},{64,32},{96,128},{128,96},{160,192},{192,160},{224... | collective-permute-start | bytes 589832 | tf_op jit(solution)/shard_map/ppermute | solution.py:209
  75.4 7.8 %collective-permute-start.13 = (bf16[2,192,256]{2,1,0:T(8,128)(2,1)S(1)}, bf16[2,192,256]{2,1,0:T(8,128)(2,1)S(1)}, u32[]{:S(2)}, u32[]{:S(2)}) collective-permute-start(bf16[2,192,256]{2,1,0:T(8,128)(2,1)S(1)} %add_convert_fusion.3), channel_id=1, source_target_pairs={{0,32},{32,0},{64,96},{96,64},{128,160},{160,128},{192,224},{224,1... | collective-permute-start | bytes 589832 | tf_op jit(solution)/shard_map/ppermute | solution.py:209
  75.7 20.2 %all-to-all-start.1 = ((bf16[16,24,1024]{2,1,0:T(8,128)(2,1)}), bf16[16,24,1024]{2,1,0:T(8,128)(2,1)S(1)}, u32[]{:S(2)}, u32[]{:S(2)}) async-start(bf16[16,24,1024]{2,1,0:T(8,128)(2,1)} %bitcast.14), calls=%async_computation.1 | async-start | bytes 1572864 | tf_op jit(solution)/shard_map/all_to_all | solution.py:213
  83.2 7.2 %collective-permute-start.14 = (bf16[2,192,256]{2,1,0:T(8,128)(2,1)S(1)}, bf16[2,192,256]{2,1,0:T(8,128)(2,1)S(1)}, u32[]{:S(2)}, u32[]{:S(2)}) collective-permute-start(bf16[2,192,256]{2,1,0:T(8,128)(2,1)S(1)} %add_convert_fusion.2), channel_id=1, source_target_pairs={{0,224},{32,64},{64,32},{96,128},{128,96},{160,192},{192,160},{224... | collective-permute-start | bytes 589832 | tf_op jit(solution)/shard_map/ppermute | solution.py:209
  96.3 4.7 %collective-permute-start.15 = (bf16[1,192,256]{2,1,0:T(8,128)(2,1)S(1)}, bf16[1,192,256]{2,1,0:T(8,128)(2,1)S(1)}, u32[]{:S(2)}, u32[]{:S(2)}) collective-permute-start(bf16[1,192,256]{2,1,0:T(8,128)(2,1)S(1)} %add_convert_fusion.5), channel_id=1, source_target_pairs={{0,32},{32,0},{64,96},{96,64},{128,160},{160,128},{192,224},{224,1... | collective-permute-start | bytes 294920 | tf_op jit(solution)/shard_map/ppermute | solution.py:209

commit v4 on v3

--- a/solution.py
+++ b/solution.py
@@ -91,21 +91,29 @@
             dva[k0:k1] += dv
             dqt[s] += dq
 
-        for b in range(NS // 4):
-            start = 4 * b
-            full = info[9 + start + 3] < span
-
-            @pl.when(full)
+        for c in range(NS // 8):
+            whole = info[9 + 8 * c + 7] < span
+
+            @pl.when(whole)
             def _():
-                work(start, 4, False)
-
-            @pl.when((count >= start + 3) & jnp.logical_not(full))
+                work(8 * c, 8, False)
+
+            @pl.when(jnp.logical_not(whole))
             def _():
-                work(start, 4, True)
-
-            @pl.when((count >= start + 1) & (count < start + 3))
-            def _():
-                work(start, 2, True)
+                for start in (8 * c, 8 * c + 4):
+                    full = info[9 + start + 3] < span
+
+                    @pl.when(full)
+                    def _():
+                        work(start, 4, False)
+
+                    @pl.when((count >= start + 3) & jnp.logical_not(full))
+                    def _():
+                        work(start, 4, True)
+
+                    @pl.when((count >= start + 1) & (count < start + 3))
+                    def _():
+                        work(start, 2, True)
 
         return carry
 
@@ -149,7 +157,7 @@
         in_specs=[pl.BlockSpec(memory_space=pltpu.SMEM)] + [vm] * 15,
         out_specs=[vm] * len(out_shape),
         scratch_shapes=scratch,
-        compiler_params=pltpu.CompilerParams(vmem_limit_bytes=24 * 2**20),
+        compiler_params=pltpu.CompilerParams(vmem_limit_bytes=32 * 2**20),
         cost_estimate=pl.CostEstimate(flops=16 * 10**9, bytes_accessed=10**7, transcendentals=5 * 10**6),
     )(info, *keys, *qs, d_own, d_mate, *stats)
 
@@ -253,12 +261,12 @@
         in_specs=[pl.BlockSpec(memory_space=pltpu.SMEM), vm, vm, vm],
         out_specs=vm,
         scratch_shapes=[pltpu.VMEM((W, HD), f32)],
+        compiler_params=pltpu.CompilerParams(vmem_limit_bytes=8 * 2**20),
     )(x_hi[None].astype(jnp.int32), grad_rows, attn_output, lse)
-    stats, a3 = lax.optimization_barrier((stats, a3))
+    stats_x = across(stats)
+    stats_x, a3 = lax.optimization_barrier((stats_x, a3))
     a4 = along(a3, ODD)
     grad_mate = mate(grad_rows)
-    stats_x = across(stats)
-    stats_x, a4 = lax.optimization_barrier((stats_x, a4))
     stats = (stats, stats_x, mate(stats), mate(stats_x))
     g0, g1, g2, g3, g4, dq_own, dq_mate = attend(
         info, (a0, a1, a2, a3, a4), (query_rows, q_x, q_m, q_mx), grad_rows, grad_mate, stats)

time: 103 us -> 98.7 us (0.958); the launches traced: 102 us -> 99.9 us
  starting transfers between devices: 36.5 us -> 48.9 us
  Pallas kernels: 24.3 us -> 16.7 us
  waiting for transfers between devices: 31.2 us -> 27 us
  local copies, waits for them, and re-layouts: 6.33 us -> 3.89 us
    ppermute x8, starting transfers between devices: 17.1 us -> 29 us  [along(): return lax.ppermute(x, 'z', route)]
    pallas_call x1, Pallas kernels: 20.1 us -> 14.4 us  [attend(): pl.pallas_call(kernel, out_shape=out_shape, in_specs=[pl.BlockSpec(memory...]
    ppermute x6, waiting for transfers between devices: 2.97 us -> 0.84 us  [mate(): return lax.ppermute(x, 'core', SWAP)]
    pallas_call x1, Pallas kernels: 2.22 us -> 0.34 us  [per_device(): pl.pallas_call(row_stats, out_shape=jax.ShapeDtypeStruct((2, 2, 1, W), f3...]
    ppermute x8, waiting for transfers between devices: 19 us -> 17.1 us  [along(): return lax.ppermute(x, 'z', route)]
    unnamed x15 -> x11, local copies, waits for them, and re-layouts: 2.83 us -> 0.99 us
  transfers between devices with their start and end apart: 18 -> 18, of which waited for: 9 -> 10; matrix products, arithmetic and copies ran while one was open for 6% -> 5% of each run, Pallas kernels for 4% -> 2%
where the time goes in v4:
time: 98.7 us; the launch traced here: 99.9 us
  starting transfers between devices  48.9 us (50%)
  waiting for transfers between devices  27 us (27%)
  Pallas kernels  16.7 us (17%)
  local copies, waits for them, and re-layouts  3.89 us (4%)
  other arithmetic  2.69 us (3%)
    ppermute x8, starting transfers between devices, along(): return lax.ppermute(x, 'z', route)  29 us
    ppermute x8, waiting for transfers between devices, along(): return lax.ppermute(x, 'z', route)  17.1 us
    all_to_all x2, starting transfers between devices, exchange(): return lax.all_to_all(x, axes, split_axis=0, concat_axis=0, tiled=True)  14.7 us
    pallas_call x1, Pallas kernels, attend(): pl.pallas_call(kernel, out_shape=out_shape, in_specs=[pl.BlockSpec(memory...  14.4 us
    all_to_all x2, waiting for transfers between devices, exchange(): return lax.all_to_all(x, axes, split_axis=0, concat_axis=0, tiled=True)  5.52 us
    ppermute x2, starting transfers between devices, across(): return lax.ppermute(x, 'x', SWAP)  4 us
    ppermute x2, waiting for transfers between devices, across(): return lax.ppermute(x, 'x', SWAP)  3.47 us
    pallas_call x1, Pallas kernels, per_device(): pl.pallas_call(prepare, out_shape=(jax.ShapeDtypeStruct((16, 24, 1024), b...  1.98 us
  transfers between devices with their start and end apart: 18, of which 10 were waited for; matrix products, arithmetic and copies ran while one was open for 5% of the time, Pallas kernels for 2%

profile of v4, /device:TPU:2, one launch (start us, length us, event | category | flops | bytes accessed | tf_op | source)
XLA Modules:
  0.0 99.9 jit_solution(2211356338154592707)
XLA Ops:
  0.6 0.0 copy-start
  0.6 0.0 copy-start.4
  0.7 2.2 %collective-permute-start.5 = (bf16[192,1024]{1,0:T(8,128)(2,1)}, bf16[192,1024]{1,0:T(8,128)(2,1)S(1)}, u32[]{:S(2)}, u32[]{:S(2)}) collective-permute-start(bf16[192,1024]{1,0:T(8,128)(2,1)} %q0.1), channel_id=1, source_target_pairs={{0,16},{16,0},{1,17},{17,1},{2,18},{18,2},{3,19},{19,3},{4,20},{20... | collective-permute-start | bytes 1179656 | tf_op jit(solution)/shard_map/ppermute | solution.py:213
  2.9 2.0 %shard_map.103 = (bf16[16,24,1024]{2,1,0:T(8,128)(2,1)}, bf16[1,192,256]{2,1,0:T(8,128)(2,1)}) custom-call(bf16[24,8192]{1,0:T(8,128)(2,1)} %grad.1, bf16[192,128]{1,0:T(8,128)(2,1)} %keys.1, bf16[192,128]{1,0:T(8,128)(2,1)} %values.1), custom_call_target="tpu_custom_call" | custom-call | tf_op jit(solution)/shard_map/pallas_call | solution.py:243
  4.9 6.6 %all-to-all-start = ((bf16[16,24,1024]{2,1,0:T(8,128)(2,1)}), bf16[16,24,1024]{2,1,0:T(8,128)(2,1)S(1)}, u32[]{:S(2)}, u32[]{:S(2)}) async-start(bf16[16,24,1024]{2,1,0:T(8,128)(2,1)} %get-tuple-element.22), calls=%async_computation | async-start | bytes 1572864 | tf_op jit(solution)/shard_map/all_to_all | solution.py:221
  11.5 0.0 copy-done.2
  11.5 2.0 %collective-permute-start = (bf16[1,192,256]{2,1,0:T(8,128)(2,1)S(1)}, bf16[1,192,256]{2,1,0:T(8,128)(2,1)S(1)}, u32[]{:S(2)}, u32[]{:S(2)}) collective-permute-start(bf16[1,192,256]{2,1,0:T(8,128)(2,1)S(1)} %copy-done.2), channel_id=1, source_target_pairs={{0,32},{32,0},{64,96},{96,64},{128,160},{160,128},{192,224},{224,1... | collective-permute-start | bytes 294920 | tf_op jit(solution)/shard_map/ppermute | solution.py:217
  13.5 0.1 stack.40
  13.6 0.7 broadcast_add_fusion
  14.3 0.1 copy.19
  14.4 0.1 reshape.414
  14.5 0.0 copy-done
  14.5 0.7 gather_fusion.1
  15.2 0.7 gather_fusion
  15.8 0.0 copy-done.4
  15.8 0.1 reshape.415
  15.9 0.1 reshape.416.lse
  16.0 0.2 convert_reduce_fusion
  16.2 0.0 collective-permute-done.a1
  16.2 5.9 %collective-permute-start.1 = (bf16[2,192,256]{2,1,0:T(8,128)(2,1)S(1)}, bf16[2,192,256]{2,1,0:T(8,128)(2,1)S(1)}, u32[]{:S(2)}, u32[]{:S(2)}) collective-permute-start(bf16[2,192,256]{2,1,0:T(8,128)(2,1)S(1)} %pad_maximum_fusion), channel_id=1, source_target_pairs={{0,224},{32,64},{64,32},{96,128},{128,96},{160,192},{192,160},{224... | collective-permute-start | bytes 589832 | tf_op jit(solution)/shard_map/ppermute | solution.py:217
  22.2 0.1 select_reduce_fusion
  22.3 0.2 convert_reduce_fusion.1
  22.5 0.1 concatenate.26.info
  22.5 3.3 %collective-permute-done.1.a2 = bf16[2,192,256]{2,1,0:T(8,128)(2,1)S(1)} collective-permute-done((bf16[2,192,256]{2,1,0:T(8,128)(2,1)S(1)}, bf16[2,192,256]{2,1,0:T(8,128)(2,1)S(1)}, u32[]{:S(2)}, u32[]{:S(2)}) %collective-permute-start.1) | collective-permute-done | bytes 196640 | tf_op jit(solution)/shard_map/ppermute | solution.py:217
  25.8 0.0 all-to-all-done
  25.8 0.0 collective-permute-start.8
  25.8 0.0 copy-done.3
  25.8 0.5 collective-permute-start.6
  26.3 0.7 collective-permute-start.3
  27.1 0.0 collective-permute-done.5.q1
  27.1 0.0 collective-permute-start.7
  27.1 0.0 copy-done.1
  27.1 0.3 shard_map.104.st0
  27.4 1.8 %collective-permute-start.2 = (f32[2,2,1,768]{3,2,1,0:T(1,128)S(1)}, f32[2,2,1,768]{3,2,1,0:T(1,128)S(1)}, u32[]{:S(2)}, u32[]{:S(2)}) collective-permute-start(f32[2,2,1,768]{3,2,1,0:T(1,128)S(1)} %shard_map.104.st0), channel_id=1, source_target_pairs={{0,16},{16,0},{1,17},{17,1},{2,18},{18,2},{3,19},{19,3},{4,20},{20... | collective-permute-start | bytes 36872 | tf_op jit(solution)/shard_map/ppermute | solution.py:213
  29.2 3.5 %collective-permute-done.2.st1 = f32[2,2,1,768]{3,2,1,0:T(1,128)S(1)} collective-permute-done((f32[2,2,1,768]{3,2,1,0:T(1,128)S(1)}, f32[2,2,1,768]{3,2,1,0:T(1,128)S(1)}, u32[]{:S(2)}, u32[]{:S(2)}) %collective-permute-start.2) | collective-permute-done | bytes 12320 | tf_op jit(solution)/shard_map/ppermute | solution.py:213
  32.7 0.6 collective-permute-done.3.a3
  33.2 4.6 %collective-permute-start.4 = (bf16[2,192,256]{2,1,0:T(8,128)(2,1)S(1)}, bf16[2,192,256]{2,1,0:T(8,128)(2,1)S(1)}, u32[]{:S(2)}, u32[]{:S(2)}) collective-permute-start(bf16[2,192,256]{2,1,0:T(8,128)(2,1)S(1)} %collective-permute-done.3.a3), channel_id=1, source_target_pairs={{0,224},{32,64},{64,32},{96,128},{128,96},{160,192},{192,160},{224... | collective-permute-start | bytes 589832 | tf_op jit(solution)/shard_map/ppermute | solution.py:217
  37.8 0.0 collective-permute-start.9
  37.8 0.0 collective-permute-done.6.q2
  37.8 0.5 collective-permute-start.10
  38.3 0.7 collective-permute-done.9.st2
  39.0 0.0 collective-permute-done.7.q3
  39.0 0.2 collective-permute-done.10.st3
  39.2 2.9 %collective-permute-done.4.a4 = bf16[2,192,256]{2,1,0:T(8,128)(2,1)S(1)} collective-permute-done((bf16[2,192,256]{2,1,0:T(8,128)(2,1)S(1)}, bf16[2,192,256]{2,1,0:T(8,128)(2,1)S(1)}, u32[]{:S(2)}, u32[]{:S(2)}) %collective-permute-start.4) | collective-permute-done | bytes 196640 | tf_op jit(solution)/shard_map/ppermute | solution.py:217
  42.0 0.0 collective-permute-done.8.d_mate
  42.0 14.4 %shard_map.105 = (f32[1,192,256]{2,1,0:T(8,128)S(1)}, f32[1,192,256]{2,1,0:T(8,128)S(1)}, f32[2,192,256]{2,1,0:T(8,128)S(1)}, f32[2,192,256]{2,1,0:T(8,128)S(1)}...) custom-call(s32[49]{0:T(128)S(1)} %concatenate.26.info, ...), custom_call_target="tpu_custom_call" | custom-call | flops 16000000000 | bytes 10000000 | tf_op jit(solution)/shard_map/pallas_call | solution.py:154
  56.4 0.1 collective-permute-start.12
  56.5 10.8 %collective-permute-start.11 = (bf16[2,192,256]{2,1,0:T(8,128)(2,1)S(1)}, bf16[2,192,256]{2,1,0:T(8,128)(2,1)S(1)}, u32[]{:S(2)}, u32[]{:S(2)}) collective-permute-start(bf16[2,192,256]{2,1,0:T(8,128)(2,1)S(1)} %get-tuple-element.33), channel_id=1, source_target_pairs={{0,224},{32,64},{64,32},{96,128},{128,96},{160,192},{192,160},{224... | collective-permute-start | bytes 589832 | tf_op jit(solution)/shard_map/ppermute | solution.py:217
  67.4 0.0 collective-permute-done.12
  67.4 1.2 %add_convert_fusion = bf16[2,192,1024]{2,1,0:T(8,128)(2,1)} fusion(f32[2,192,1024]{2,1,0:T(8,128)S(1)} %get-tuple-element.34, bf16[2,192,1024]{2,1,0:T(8,128)(2,1)S(1)} %collective-permute-done.12), kind=kLoop, calls=%fused_computation.2 | loop fusion | flops 1179648 | bytes 3145728 | tf_op jit(solution)/shard_map/convert_element_type | solution.py:274
  68.5 4.3 %collective-permute-done.11 = bf16[2,192,256]{2,1,0:T(8,128)(2,1)S(1)} collective-permute-done((bf16[2,192,256]{2,1,0:T(8,128)(2,1)S(1)}, bf16[2,192,256]{2,1,0:T(8,128)(2,1)S(1)}, u32[]{:S(2)}, u32[]{:S(2)}) %collective-permute-start.11) | collective-permute-done | bytes 196640 | tf_op jit(solution)/shard_map/ppermute | solution.py:217
  72.9 0.1 collective-permute-start.13
  73.0 8.1 %all-to-all-start.1 = ((bf16[16,24,1024]{2,1,0:T(8,128)(2,1)}), bf16[16,24,1024]{2,1,0:T(8,128)(2,1)S(1)}, u32[]{:S(2)}, u32[]{:S(2)}) async-start(bf16[16,24,1024]{2,1,0:T(8,128)(2,1)} %bitcast.14), calls=%async_computation.1 | async-start | bytes 1572864 | tf_op jit(solution)/shard_map/all_to_all | solution.py:221
  81.1 0.0 collective-permute-done.13
  81.1 0.1 add_convert_fusion.2
  81.2 3.1 %collective-permute-start.14 = (bf16[2,192,256]{2,1,0:T(8,128)(2,1)S(1)}, bf16[2,192,256]{2,1,0:T(8,128)(2,1)S(1)}, u32[]{:S(2)}, u32[]{:S(2)}) collective-permute-start(bf16[2,192,256]{2,1,0:T(8,128)(2,1)S(1)} %add_convert_fusion.2), channel_id=1, source_target_pairs={{0,224},{32,64},{64,32},{96,128},{128,96},{160,192},{192,160},{224... | collective-permute-start | bytes 589832 | tf_op jit(solution)/shard_map/ppermute | solution.py:217
  84.2 4.3 %collective-permute-done.14 = bf16[2,192,256]{2,1,0:T(8,128)(2,1)S(1)} collective-permute-done((bf16[2,192,256]{2,1,0:T(8,128)(2,1)S(1)}, bf16[2,192,256]{2,1,0:T(8,128)(2,1)S(1)}, u32[]{:S(2)}, u32[]{:S(2)}) %collective-permute-start.14) | collective-permute-done | bytes 196640 | tf_op jit(solution)/shard_map/ppermute | solution.py:217
  88.6 5.5 %all-to-all-done.1 = bf16[16,24,1024]{2,1,0:T(8,128)(2,1)S(1)} async-done(((bf16[16,24,1024]{2,1,0:T(8,128)(2,1)}), bf16[16,24,1024]{2,1,0:T(8,128)(2,1)S(1)}, u32[]{:S(2)}, u32[]{:S(2)}) %all-to-all-start.1) | async-done | bytes 786464 | tf_op jit(solution)/shard_map/all_to_all | solution.py:221
  94.1 0.4 copy.21
  94.5 1.8 %collective-permute-start.15 = (bf16[1,192,256]{2,1,0:T(8,128)(2,1)S(1)}, bf16[1,192,256]{2,1,0:T(8,128)(2,1)S(1)}, u32[]{:S(2)}, u32[]{:S(2)}) collective-permute-start(bf16[1,192,256]{2,1,0:T(8,128)(2,1)S(1)} %add_convert_fusion.5), channel_id=1, source_target_pairs={{0,32},{32,0},{64,96},{96,64},{128,160},{160,128},{192,224},{224,1... | collective-permute-start | bytes 294920 | tf_op jit(solution)/shard_map/ppermute | solution.py:217
  96.3 0.1 add_convert_fusion.1
  96.5 1.0 copy.23
  97.4 1.8 %collective-permute-done.15 = bf16[1,192,256]{2,1,0:T(8,128)(2,1)S(1)} collective-permute-done((bf16[1,192,256]{2,1,0:T(8,128)(2,1)S(1)}, bf16[1,192,256]{2,1,0:T(8,128)(2,1)S(1)}, u32[]{:S(2)}, u32[]{:S(2)}) %collective-permute-start.15) | collective-permute-done | bytes 98336 | tf_op jit(solution)/shard_map/ppermute | solution.py:217
  99.3 0.6 fusion.3
  (14 shorter events, 0.2 us)
Async XLA Ops:
  0.6 13.9 %copy-start = (s32[64]{0:T(128)S(1)}, s32[64]{0:T(128)}, u32[]{:S(2)}) copy-start(s32[64]{0:T(128)} %param.14) | copy-start | bytes 772
  0.6 15.2 %copy-start.4 = (f32[8,192]{1,0:T(8,128)S(1)}, f32[8,192]{1,0:T(8,128)}, u32[]{:S(2)}) copy-start(f32[8,192]{1,0:T(8,128)} %param.12) | copy-start | bytes 18436
  0.7 26.4 %collective-permute-start.5 = (bf16[192,1024]{1,0:T(8,128)(2,1)}, bf16[192,1024]{1,0:T(8,128)(2,1)S(1)}, u32[]{:S(2)}, u32[]{:S(2)}) collective-permute-start(bf16[192,1024]{1,0:T(8,128)(2,1)} %q0.1), channel_id=1, source_target_pairs={{0,16},{16,0},{1,17},{17,1},{2,18},{18,2},{3,19},{19,3},{4,20},{20... | collective-permute-start | bytes 1179656 | tf_op jit(solution)/shard_map/ppermute | solution.py:213
  4.8 6.6 %copy-start.2 = (bf16[1,192,256]{2,1,0:T(8,128)(2,1)S(1)}, bf16[1,192,256]{2,1,0:T(8,128)(2,1)}, u32[]{:S(2)}) copy-start(bf16[1,192,256]{2,1,0:T(8,128)(2,1)} %get-tuple-element.23.a0) | copy-start | bytes 294916
  4.8 21.0 %copy-start.3 = (bf16[192,1024]{1,0:T(8,128)(2,1)S(1)}, bf16[192,1024]{1,0:T(8,128)(2,1)}, u32[]{:S(2)}) copy-start(bf16[192,1024]{1,0:T(8,128)(2,1)} %q0.1) | copy-start | bytes 1179652
  4.9 22.2 %copy-start.1 = (bf16[192,1024]{1,0:T(8,128)(2,1)S(1)}, bf16[192,1024]{1,0:T(8,128)(2,1)}, u32[]{:S(2)}) copy-start(bf16[192,1024]{1,0:T(8,128)(2,1)} %attn.1) | copy-start | bytes 1179652
  4.9 21.0 %all-to-all-start = ((bf16[16,24,1024]{2,1,0:T(8,128)(2,1)}), bf16[16,24,1024]{2,1,0:T(8,128)(2,1)S(1)}, u32[]{:S(2)}, u32[]{:S(2)}) async-start(bf16[16,24,1024]{2,1,0:T(8,128)(2,1)} %get-tuple-element.22), calls=%async_computation | async-start | bytes 1572864 | tf_op jit(solution)/shard_map/all_to_all | solution.py:221
  11.5 4.7 %collective-permute-start = (bf16[1,192,256]{2,1,0:T(8,128)(2,1)S(1)}, bf16[1,192,256]{2,1,0:T(8,128)(2,1)S(1)}, u32[]{:S(2)}, u32[]{:S(2)}) collective-permute-start(bf16[1,192,256]{2,1,0:T(8,128)(2,1)S(1)} %copy-done.2), channel_id=1, source_target_pairs={{0,32},{32,0},{64,96},{96,64},{128,160},{160,128},{192,224},{224,1... | collective-permute-start | bytes 294920 | tf_op jit(solution)/shard_map/ppermute | solution.py:217
  16.2 9.6 %collective-permute-start.1 = (bf16[2,192,256]{2,1,0:T(8,128)(2,1)S(1)}, bf16[2,192,256]{2,1,0:T(8,128)(2,1)S(1)}, u32[]{:S(2)}, u32[]{:S(2)}) collective-permute-start(bf16[2,192,256]{2,1,0:T(8,128)(2,1)S(1)} %pad_maximum_fusion), channel_id=1, source_target_pairs={{0,224},{32,64},{64,32},{96,128},{128,96},{160,192},{192,160},{224... | collective-permute-start | bytes 589832 | tf_op jit(solution)/shard_map/ppermute | solution.py:217
  25.8 16.2 %collective-permute-start.8 = (bf16[2,192,1024]{2,1,0:T(8,128)(2,1)S(1)}, bf16[2,192,1024]{2,1,0:T(8,128)(2,1)S(1)}, u32[]{:S(2)}, u32[]{:S(2)}) collective-permute-start(bf16[2,192,1024]{2,1,0:T(8,128)(2,1)S(1)} %bitcast.29), channel_id=1, source_target_pairs={{0,8},{8,0},{1,9},{9,1},{2,10},{10,2},{3,11},{11,3},{4,12},{12,4},... | collective-permute-start | bytes 2359304 | tf_op jit(solution)/shard_map/ppermute | solution.py:209
  25.8 12.0 %collective-permute-start.6 = (bf16[192,1024]{1,0:T(8,128)(2,1)S(1)}, bf16[192,1024]{1,0:T(8,128)(2,1)S(1)}, u32[]{:S(2)}, u32[]{:S(2)}) collective-permute-start(bf16[192,1024]{1,0:T(8,128)(2,1)S(1)} %copy-done.3), channel_id=1, source_target_pairs={{0,8},{8,0},{1,9},{9,1},{2,10},{10,2},{3,11},{11,3},{4,12},{12,4},... | collective-permute-start | bytes 1179656 | tf_op jit(solution)/shard_map/ppermute | solution.py:209
  26.3 6.9 %collective-permute-start.3 = (bf16[2,192,256]{2,1,0:T(8,128)(2,1)S(1)}, bf16[2,192,256]{2,1,0:T(8,128)(2,1)S(1)}, u32[]{:S(2)}, u32[]{:S(2)}) collective-permute-start(bf16[2,192,256]{2,1,0:T(8,128)(2,1)S(1)} %collective-permute-done.1.a2), channel_id=1, source_target_pairs={{0,32},{32,0},{64,96},{96,64},{128,160},{160,128},{192,224},{224,1... | collective-permute-start | bytes 589832 | tf_op jit(solution)/shard_map/ppermute | solution.py:217
  27.1 11.9 %collective-permute-start.7 = (bf16[192,1024]{1,0:T(8,128)(2,1)S(1)}, bf16[192,1024]{1,0:T(8,128)(2,1)S(1)}, u32[]{:S(2)}, u32[]{:S(2)}) collective-permute-start(bf16[192,1024]{1,0:T(8,128)(2,1)S(1)} %collective-permute-done.5.q1), channel_id=1, source_target_pairs={{0,8},{8,0},{1,9},{9,1},{2,10},{10,2},{3,11},{11,3},{4,12},{12,4},... | collective-permute-start | bytes 1179656 | tf_op jit(solution)/shard_map/ppermute | solution.py:209
  27.4 5.3 %collective-permute-start.2 = (f32[2,2,1,768]{3,2,1,0:T(1,128)S(1)}, f32[2,2,1,768]{3,2,1,0:T(1,128)S(1)}, u32[]{:S(2)}, u32[]{:S(2)}) collective-permute-start(f32[2,2,1,768]{3,2,1,0:T(1,128)S(1)} %shard_map.104.st0), channel_id=1, source_target_pairs={{0,16},{16,0},{1,17},{17,1},{2,18},{18,2},{3,19},{19,3},{4,20},{20... | collective-permute-start | bytes 36872 | tf_op jit(solution)/shard_map/ppermute | solution.py:213
  33.2 8.8 %collective-permute-start.4 = (bf16[2,192,256]{2,1,0:T(8,128)(2,1)S(1)}, bf16[2,192,256]{2,1,0:T(8,128)(2,1)S(1)}, u32[]{:S(2)}, u32[]{:S(2)}) collective-permute-start(bf16[2,192,256]{2,1,0:T(8,128)(2,1)S(1)} %collective-permute-done.3.a3), channel_id=1, source_target_pairs={{0,224},{32,64},{64,32},{96,128},{128,96},{160,192},{192,160},{224... | collective-permute-start | bytes 589832 | tf_op jit(solution)/shard_map/ppermute | solution.py:217
  37.8 1.2 %collective-permute-start.9 = (f32[2,2,1,768]{3,2,1,0:T(1,128)S(1)}, f32[2,2,1,768]{3,2,1,0:T(1,128)S(1)}, u32[]{:S(2)}, u32[]{:S(2)}) collective-permute-start(f32[2,2,1,768]{3,2,1,0:T(1,128)S(1)} %shard_map.104.st0), channel_id=1, source_target_pairs={{0,8},{8,0},{1,9},{9,1},{2,10},{10,2},{3,11},{11,3},{4,12},{12,4},... | collective-permute-start | bytes 36872 | tf_op jit(solution)/shard_map/ppermute | solution.py:209
  37.8 1.3 %collective-permute-start.10 = (f32[2,2,1,768]{3,2,1,0:T(1,128)S(1)}, f32[2,2,1,768]{3,2,1,0:T(1,128)S(1)}, u32[]{:S(2)}, u32[]{:S(2)}) collective-permute-start(f32[2,2,1,768]{3,2,1,0:T(1,128)S(1)} %collective-permute-done.2.st1), channel_id=1, source_target_pairs={{0,8},{8,0},{1,9},{9,1},{2,10},{10,2},{3,11},{11,3},{4,12},{12,4},... | collective-permute-start | bytes 36872 | tf_op jit(solution)/shard_map/ppermute | solution.py:209
  56.4 11.0 %collective-permute-start.12 = (bf16[2,192,1024]{2,1,0:T(8,128)(2,1)S(1)}, bf16[2,192,1024]{2,1,0:T(8,128)(2,1)S(1)}, u32[]{:S(2)}, u32[]{:S(2)}) collective-permute-start(bf16[2,192,1024]{2,1,0:T(8,128)(2,1)S(1)} %get-tuple-element.35), channel_id=1, source_target_pairs={{0,8},{8,0},{1,9},{9,1},{2,10},{10,2},{3,11},{11,3},{4,12},{12,4},... | collective-permute-start | bytes 2359304 | tf_op jit(solution)/shard_map/ppermute | solution.py:209
  56.5 16.3 %collective-permute-start.11 = (bf16[2,192,256]{2,1,0:T(8,128)(2,1)S(1)}, bf16[2,192,256]{2,1,0:T(8,128)(2,1)S(1)}, u32[]{:S(2)}, u32[]{:S(2)}) collective-permute-start(bf16[2,192,256]{2,1,0:T(8,128)(2,1)S(1)} %get-tuple-element.33), channel_id=1, source_target_pairs={{0,224},{32,64},{64,32},{96,128},{128,96},{160,192},{192,160},{224... | collective-permute-start | bytes 589832 | tf_op jit(solution)/shard_map/ppermute | solution.py:217
  72.9 8.2 %collective-permute-start.13 = (bf16[2,192,256]{2,1,0:T(8,128)(2,1)S(1)}, bf16[2,192,256]{2,1,0:T(8,128)(2,1)S(1)}, u32[]{:S(2)}, u32[]{:S(2)}) collective-permute-start(bf16[2,192,256]{2,1,0:T(8,128)(2,1)S(1)} %add_convert_fusion.3), channel_id=1, source_target_pairs={{0,32},{32,0},{64,96},{96,64},{128,160},{160,128},{192,224},{224,1... | collective-permute-start | bytes 589832 | tf_op jit(solution)/shard_map/ppermute | solution.py:217
  73.0 21.1 %all-to-all-start.1 = ((bf16[16,24,1024]{2,1,0:T(8,128)(2,1)}), bf16[16,24,1024]{2,1,0:T(8,128)(2,1)S(1)}, u32[]{:S(2)}, u32[]{:S(2)}) async-start(bf16[16,24,1024]{2,1,0:T(8,128)(2,1)} %bitcast.14), calls=%async_computation.1 | async-start | bytes 1572864 | tf_op jit(solution)/shard_map/all_to_all | solution.py:221
  81.2 7.4 %collective-permute-start.14 = (bf16[2,192,256]{2,1,0:T(8,128)(2,1)S(1)}, bf16[2,192,256]{2,1,0:T(8,128)(2,1)S(1)}, u32[]{:S(2)}, u32[]{:S(2)}) collective-permute-start(bf16[2,192,256]{2,1,0:T(8,128)(2,1)S(1)} %add_convert_fusion.2), channel_id=1, source_target_pairs={{0,224},{32,64},{64,32},{96,128},{128,96},{160,192},{192,160},{224... | collective-permute-start | bytes 589832 | tf_op jit(solution)/shard_map/ppermute | solution.py:217
  94.5 4.7 %collective-permute-start.15 = (bf16[1,192,256]{2,1,0:T(8,128)(2,1)S(1)}, bf16[1,192,256]{2,1,0:T(8,128)(2,1)S(1)}, u32[]{:S(2)}, u32[]{:S(2)}) collective-permute-start(bf16[1,192,256]{2,1,0:T(8,128)(2,1)S(1)} %add_convert_fusion.5), channel_id=1, source_target_pairs={{0,32},{32,0},{64,96},{96,64},{128,160},{160,128},{192,224},{224,1... | collective-permute-start | bytes 294920 | tf_op jit(solution)/shard_map/ppermute | solution.py:217
